TPU v7x, 512 devices: a whole 4x8x8 slice. The times are simulated.
512 devices in a mesh: pos: 64 (over z, y_hi, core), off: 8 (over x, y_lo).
Axes of the slice: x: 4, y: 8 (y_hi: 4, y_lo: 2; y = y_hi * 2 + y_lo), z: 8, core: 2. Of those that a mesh axis runs over, the one named last changes fastest.
Arguments:
- band_in: bfloat16 [32, 1024, 1024], P(None, 'pos', 'off'), may hold values from -6 to 6
- conv_weight: bfloat16 [2, 9, 32, 32], replicated, may hold values from -0.375 to 0.375
- mix_weight: bfloat16 [2, 32, 32], replicated, may hold values from -1 to 1
- norm_gain: float32 [2, 32], replicated, may hold values from 0.1 to 1.9
- norm_bias: float32 [2, 32], replicated, may hold values from -3 to 3
- cotangent: bfloat16 [32, 1024, 1024], P(None, 'pos', 'off'), may hold values from -6 to 6
Outputs:
- grad_band: bfloat16 [32, 1024, 1024], P(None, 'pos', 'off')
- grad_conv: float32 [2, 9, 32, 32], replicated
- grad_mix: float32 [2, 32, 32], replicated
- grad_gain: float32 [2, 32], replicated
- grad_bias: float32 [2, 32], replicated
All inputs are finite; a program needn't handle non-finite values.
Results may differ from a plain program's by a relative error of at most 0.0095.
Values may be sent and summed in bfloat16 or wider, within the bound.
No kernel may reach another device: no remote copies, remote signals or barrier semaphores. Data moves between devices by JAX's collectives and lax.ppermute only.
A program may use at most 64 MiB of HBM per device.

v0:
```python
import math

import jax
import jax.numpy as jnp
from jax import lax
from jax.sharding import PartitionSpec as P

FIRST_DILATION = 2
SECOND_DILATION = 4


def with_halo(shard, sides, width):
    for axis, dim in sides:
        devices, length = (lax.axis_size(axis), shard.shape[dim])
        up = [(i, (i + 1) % devices) for i in range(devices - 1)]
        down = [(j, i) for i, j in up]
        last = lax.slice_in_dim(shard, length - width, length, axis=dim)
        first = lax.slice_in_dim(shard, 0, width, axis=dim)
        before = lax.ppermute(last, axis, up)
        after = lax.ppermute(first, axis, down)
        shard = jnp.concatenate([before, shard, after], axis=dim)
    return shard


def from_partner(shard, axis, distance):
    return lax.ppermute(shard, axis, [(i, i ^ 1 << distance) for i in range(lax.axis_size(axis))])


def shifted(block, axis, distance):
    devices = range(lax.axis_size(axis))
    route = [(i - distance, i) for i in devices if i - distance in devices]
    return lax.ppermute(block, axis, route)


def tap_list(dilation):
    offsets = []
    for along_row in (-dilation, 0, dilation):
        for along_col in (-dilation, 0, dilation):
            offsets.append(((along_row + along_col) // 2, along_col - along_row))
    return offsets


def window(extended, dilation, row_count, column_count, row_shift, col_shift):
    row_start = dilation + row_shift
    column_start = 2 * dilation + col_shift
    return lax.slice(
        extended,
        (0, row_start, column_start),
        (extended.shape[0], row_start + row_count, column_start + column_count),
    )


def smooth(values):
    return values * jax.nn.sigmoid(1.702 * values)


def smooth_slope(values):
    logistic = jax.nn.sigmoid(1.702 * values)
    return logistic + 1.702 * values * logistic * (1.0 - logistic)


def extend(source, dilation):
    tall_ext = with_halo(source, (("pos", 1),), dilation)
    return with_halo(tall_ext, (("off", 2),), 2 * dilation)


def reflect(source):
    reversed_tile = source
    for binary_digit_index in range(lax.axis_size("off").bit_length() - 1):
        reversed_tile = from_partner(reversed_tile, "off", binary_digit_index)
    edge_col = shifted(reversed_tile[:, :, :1], "off", 1)
    flipped = reversed_tile[:, :, ::-1]
    return jnp.concatenate([edge_col, flipped[:, :, :-1]], axis=2)


def local(band_in, conv_weight, mix_weight, norm_gain, norm_bias, cotangent):
    row_count = band_in.shape[1]
    column_count = band_in.shape[2]
    grad_scale = 1.0 / math.sqrt(
        row_count * lax.axis_size("pos") * column_count * lax.axis_size("off")
    )
    dilation_list = (FIRST_DILATION, SECOND_DILATION)
    current = band_in
    stored = []
    for section_index in range(2):
        dilation = dilation_list[section_index]
        activated = smooth(current.astype(jnp.float32)).astype(jnp.bfloat16)
        extended = extend(activated, dilation)
        pre_conv = jnp.zeros(current.shape, jnp.float32)
        for tap_index, shifts in enumerate(tap_list(dilation)):
            pre_conv = pre_conv + jnp.einsum(
                "oi,iqc->oqc",
                conv_weight[section_index, tap_index],
                window(extended, dilation, row_count, column_count, shifts[0], shifts[1]),
                preferred_element_type=jnp.float32,
            )
        gain_col = norm_gain[section_index][:, None, None]
        bias_col = norm_bias[section_index][:, None, None]
        hidden = smooth(gain_col * pre_conv + bias_col).astype(jnp.bfloat16)
        mixed = jnp.einsum(
            "oi,iqc->oqc", mix_weight[section_index], hidden, preferred_element_type=jnp.float32
        )
        summed = (current.astype(jnp.float32) + mixed).astype(jnp.bfloat16)
        stored.append((current, extended, pre_conv, hidden))
        current = ((summed.astype(jnp.float32) + reflect(summed).astype(jnp.float32)) * 0.5).astype(
            jnp.bfloat16
        )
    gradient = cotangent
    grad_parts = [None, None]
    for section_index in (1, 0):
        dilation = dilation_list[section_index]
        source, extended, pre_conv, hidden = stored[section_index]
        gain_col = norm_gain[section_index][:, None, None]
        bias_col = norm_bias[section_index][:, None, None]
        grad_sum = (
            (gradient.astype(jnp.float32) + reflect(gradient).astype(jnp.float32)) * 0.5
        ).astype(jnp.bfloat16)
        mix_term = jnp.einsum("oqc,iqc->oi", grad_sum, hidden, preferred_element_type=jnp.float32)
        grad_hidden = jnp.einsum(
            "oi,oqc->iqc", mix_weight[section_index], grad_sum, preferred_element_type=jnp.float32
        )
        grad_pre = grad_hidden * smooth_slope(gain_col * pre_conv + bias_col)
        gain_term = jnp.sum(grad_pre * pre_conv, axis=(1, 2))
        bias_term = jnp.sum(grad_pre, axis=(1, 2))
        grad_conv_in = (grad_pre * gain_col).astype(jnp.bfloat16)
        grad_ext = extend(grad_conv_in, dilation)
        grad_act = jnp.zeros(source.shape, jnp.float32)
        tap_contributions = []
        for tap_index, shifts in enumerate(tap_list(dilation)):
            tap_contributions.append(
                jnp.einsum(
                    "oqc,iqc->oi",
                    grad_conv_in,
                    window(extended, dilation, row_count, column_count, shifts[0], shifts[1]),
                    preferred_element_type=jnp.float32,
                )
            )
            grad_act = grad_act + jnp.einsum(
                "oi,oqc->iqc",
                conv_weight[section_index, tap_index],
                window(grad_ext, dilation, row_count, column_count, -shifts[0], -shifts[1]),
                preferred_element_type=jnp.float32,
            )
        gradient = (
            grad_sum.astype(jnp.float32) + grad_act * smooth_slope(source.astype(jnp.float32))
        ).astype(jnp.bfloat16)
        tap_stack = jnp.stack(tap_contributions)
        grad_parts[section_index] = (tap_stack, mix_term, gain_term, bias_term)
    conv_total = jnp.stack([grad_parts[0][0], grad_parts[1][0]])
    mix_total = jnp.stack([grad_parts[0][1], grad_parts[1][1]])
    gain_total = jnp.stack([grad_parts[0][2], grad_parts[1][2]])
    bias_total = jnp.stack([grad_parts[0][3], grad_parts[1][3]])
    conv_total, mix_total, gain_total, bias_total = lax.psum(
        (conv_total, mix_total, gain_total, bias_total), ("pos", "off")
    )
    return (
        gradient,
        conv_total * grad_scale,
        mix_total * grad_scale,
        gain_total * grad_scale,
        bias_total * grad_scale,
    )


def solution(mesh):
    placed = (P(None, "pos", "off"), P(), P(), P(), P(), P(None, "pos", "off"))
    return jax.shard_map(
        local,
        mesh=mesh,
        in_specs=placed,
        out_specs=(P(None, "pos", "off"), P(), P(), P(), P()),
        check_vma=False,
    )
```

profile of v0, /device:TPU:1, one launch (start us, length us, event | category | flops | bytes accessed | tf_op | source)
XLA Modules:
  0.0 540.6 jit_solution(743625463789698319)
XLA Ops:
  8.3 5.7 %collective-permute-start.4 = (bf16[32,2,128]{2,0,1:T(8,128)(2,1)S(1)}, bf16[32,2,128]{2,0,1:T(8,128)(2,1)S(1)}, u32[]{:S(2)}, u32[]{:S(2)}) collective-permute-start(bf16[32,2,128]{2,0,1:T(8,128)(2,1)S(1)} %get-tuple-element.41), channel_id=1, source_target_pairs={{0,8},{8,16},{16,24},{24,32},{32,40},{40,48},{48,56},{56,64},{64,7... | collective-permute-start | bytes 49160 | tf_op jit(solution)/shard_map/ppermute | solution.py:19
  14.0 4.4 collective-permute-start.5
  22.1 4.0 collective-permute-start.7
  26.3 2.8 collective-permute-done.6
  32.6 4.1 collective-permute-start.8
  36.8 4.7 collective-permute-start.1
  41.5 3.2 collective-permute-start.9
  47.2 4.3 collective-permute-start.10
  51.9 3.2 collective-permute-start.3
  61.3 7.5 %collective-permute-start.12 = (bf16[32,4,128]{2,0,1:T(8,128)(2,1)S(1)}, bf16[32,4,128]{2,0,1:T(8,128)(2,1)S(1)}, u32[]{:S(2)}, u32[]{:S(2)}) collective-permute-start(bf16[32,4,128]{2,0,1:T(8,128)(2,1)S(1)} %get-tuple-element.39), channel_id=1, source_target_pairs={{0,8},{8,16},{16,24},{24,32},{32,40},{40,48},{48,56},{56,64},{64,7... | collective-permute-start | bytes 98312 | tf_op jit(solution)/shard_map/ppermute | solution.py:19
  70.9 4.0 collective-permute-done.13
  76.4 4.7 collective-permute-start.15
  88.4 4.5 collective-permute-start.17
  94.2 4.8 collective-permute-start.18
  102.1 6.9 %collective-permute-done.19 = bf16[32,24,8]{2,0,1:T(8,128)(2,1)S(1)} collective-permute-done((bf16[32,24,8]{2,0,1:T(8,128)(2,1)S(1)}, bf16[32,24,8]{2,0,1:T(8,128)(2,1)S(1)}, u32[]{:S(2)}, u32[]{:S(2)}) %collective-permute-start.19) | collective-permute-done | bytes 12320 | tf_op jit(solution)/shard_map/ppermute | solution.py:20
  111.2 3.6 collective-permute-start.20
  115.0 3.6 collective-permute-done.20
  121.5 3.6 collective-permute-done.21
  125.1 4.5 collective-permute-start.22
  132.3 3.3 collective-permute-start.23
  138.5 114.2 %all-reduce = (f32[2,32,32]{2,1,0:T(8,128)S(1)}, f32[2,32]{1,0:T(2,128)S(1)}, f32[2,32]{1,0:T(2,128)S(1)}) all-reduce(f32[2,32,32]{2,1,0:T(8,128)S(1)} %pad_maximum_fusion.21, f32[2,32]{1,0:T(2,128)S(1)} %pad_maximum_fusion.22, f32[2,32]{1,0:T(2,128)S(1)} %pad_maximum_fusion.23), channel_id=1, replica_groups=mesh['pos'=64,'off'=8] {'pos','off'}, use_global_device_ids=true, to_apply=%region_1.0 | all-reduce | flops 2176 | bytes 17408 | tf_op jit(solution)/shard_map/psum | solution.py:153
  257.0 3.9 collective-permute-start.25
  268.9 6.6 %collective-permute-done.27 = bf16[32,20,4]{2,0,1:T(8,128)(2,1)S(1)} collective-permute-done((bf16[32,20,4]{2,0,1:T(8,128)(2,1)S(1)}, bf16[32,20,4]{2,0,1:T(8,128)(2,1)S(1)}, u32[]{:S(2)}, u32[]{:S(2)}) %collective-permute-start.27) | collective-permute-done | bytes 5152 | tf_op jit(solution)/shard_map/ppermute | solution.py:20
  278.3 253.7 %all-reduce.3.cloned.1.call-done = f32[2,9,32,32]{3,2,1,0:T(8,128)} async-done(((f32[2,9,32,32]{3,2,1,0:T(8,128)}), f32[2,9,32,32]{3,2,1,0:T(8,128)}) %all-reduce.3.cloned.1.call-update) | async-done | bytes 73744 | tf_op jit(solution)/shard_map/psum | solution.py:153
  (144 shorter events, 59.9 us)
Async XLA Ops:
  7.2 524.9 %all-reduce.3.cloned.1.call-start = ((), (), s32[]{:S(2)}) async-start(), calls=%async_computation | async-start | bytes 589824 | tf_op jit(solution)/shard_map/psum | solution.py:153
  8.3 12.4 %collective-permute-start.4 = (bf16[32,2,128]{2,0,1:T(8,128)(2,1)S(1)}, bf16[32,2,128]{2,0,1:T(8,128)(2,1)S(1)}, u32[]{:S(2)}, u32[]{:S(2)}) collective-permute-start(bf16[32,2,128]{2,0,1:T(8,128)(2,1)S(1)} %get-tuple-element.41), channel_id=1, source_target_pairs={{0,8},{8,16},{16,24},{24,32},{32,40},{40,48},{48,56},{56,64},{64,7... | collective-permute-start | bytes 49160 | tf_op jit(solution)/shard_map/ppermute | solution.py:19
  14.0 6.7 %collective-permute-start.5 = (bf16[32,2,128]{2,0,1:T(8,128)(2,1)S(1)}, bf16[32,2,128]{2,0,1:T(8,128)(2,1)S(1)}, u32[]{:S(2)}, u32[]{:S(2)}) collective-permute-start(bf16[32,2,128]{2,0,1:T(8,128)(2,1)S(1)} %get-tuple-element.42), channel_id=1, source_target_pairs={{8,0},{16,8},{24,16},{32,24},{40,32},{48,40},{56,48},{64,56},{72,6... | collective-permute-start | bytes 49160 | tf_op jit(solution)/shard_map/ppermute | solution.py:20
  18.5 18.2 %collective-permute-start = (bf16[32,16,128]{2,0,1:T(8,128)(2,1)S(1)}, bf16[32,16,128]{2,0,1:T(8,128)(2,1)S(1)}, u32[]{:S(2)}, u32[]{:S(2)}) collective-permute-start(bf16[32,16,128]{2,0,1:T(8,128)(2,1)S(1)} %copy.11), channel_id=1, source_target_pairs={{0,1},{1,0},{2,3},{3,2},{4,5},{5,4},{6,7},{7,6},{8,9},{9,8},{10,11... | collective-permute-start | bytes 393224 | tf_op jit(solution)/shard_map/ppermute | solution.py:26
  20.8 8.3 %collective-permute-start.6 = (bf16[32,20,4]{2,0,1:T(8,128)(2,1)S(1)}, bf16[32,20,4]{2,0,1:T(8,128)(2,1)S(1)}, u32[]{:S(2)}, u32[]{:S(2)}) collective-permute-start(bf16[32,20,4]{2,0,1:T(8,128)(2,1)S(1)} %get-tuple-element.33), channel_id=1, source_target_pairs={{1,0},{2,1},{3,2},{4,3},{5,4},{6,5},{7,6},{9,8},{10,9},{11,10},{12... | collective-permute-start | bytes 15368 | tf_op jit(solution)/shard_map/ppermute | solution.py:20
  22.1 7.9 %collective-permute-start.7 = (bf16[32,20,4]{2,0,1:T(8,128)(2,1)S(1)}, bf16[32,20,4]{2,0,1:T(8,128)(2,1)S(1)}, u32[]{:S(2)}, u32[]{:S(2)}) collective-permute-start(bf16[32,20,4]{2,0,1:T(8,128)(2,1)S(1)} %get-tuple-element.34), channel_id=1, source_target_pairs={{0,1},{1,2},{2,3},{3,4},{4,5},{5,6},{6,7},{8,9},{9,10},{10,11},{11... | collective-permute-start | bytes 15368 | tf_op jit(solution)/shard_map/ppermute | solution.py:19
  32.6 8.8 %collective-permute-start.8 = (bf16[32,16,128]{2,0,1:T(8,128)(2,1)S(1)}, bf16[32,16,128]{2,0,1:T(8,128)(2,1)S(1)}, u32[]{:S(2)}, u32[]{:S(2)}) collective-permute-start(bf16[32,16,128]{2,0,1:T(8,128)(2,1)S(1)} %fusion.39), channel_id=1, source_target_pairs={{0,1},{1,0},{2,3},{3,2},{4,5},{5,4},{6,7},{7,6},{8,9},{9,8},{10,11... | collective-permute-start | bytes 393224 | tf_op jit(solution)/shard_map/ppermute | solution.py:26
  36.8 7.9 %collective-permute-start.1 = (bf16[32,16,128]{2,0,1:T(8,128)(2,1)S(1)}, bf16[32,16,128]{2,0,1:T(8,128)(2,1)S(1)}, u32[]{:S(2)}, u32[]{:S(2)}) collective-permute-start(bf16[32,16,128]{2,0,1:T(8,128)(2,1)S(1)} %collective-permute-done), channel_id=1, source_target_pairs={{0,2},{1,3},{2,0},{3,1},{4,6},{5,7},{6,4},{7,5},{8,10},{9,11},{10,... | collective-permute-start | bytes 393224 | tf_op jit(solution)/shard_map/ppermute | solution.py:26
  44.7 7.2 %collective-permute-start.2 = (bf16[32,16,128]{2,0,1:T(8,128)(2,1)S(1)}, bf16[32,16,128]{2,0,1:T(8,128)(2,1)S(1)}, u32[]{:S(2)}, u32[]{:S(2)}) collective-permute-start(bf16[32,16,128]{2,0,1:T(8,128)(2,1)S(1)} %collective-permute-done.1), channel_id=1, source_target_pairs={{0,4},{1,5},{2,6},{3,7},{4,0},{5,1},{6,2},{7,3},{8,12},{9,13},{10,... | collective-permute-start | bytes 393224 | tf_op jit(solution)/shard_map/ppermute | solution.py:26
  47.2 8.8 %collective-permute-start.10 = (bf16[32,16,128]{2,0,1:T(8,128)(2,1)S(1)}, bf16[32,16,128]{2,0,1:T(8,128)(2,1)S(1)}, u32[]{:S(2)}, u32[]{:S(2)}) collective-permute-start(bf16[32,16,128]{2,0,1:T(8,128)(2,1)S(1)} %collective-permute-done.9), channel_id=1, source_target_pairs={{0,4},{1,5},{2,6},{3,7},{4,0},{5,1},{6,2},{7,3},{8,12},{9,13},{10,... | collective-permute-start | bytes 393224 | tf_op jit(solution)/shard_map/ppermute | solution.py:26
  51.9 6.8 %collective-permute-start.3 = (bf16[32,16,1]{2,0,1:T(8,128)(2,1)S(1)}, bf16[32,16,1]{2,0,1:T(8,128)(2,1)S(1)}, u32[]{:S(2)}, u32[]{:S(2)}) collective-permute-start(bf16[32,16,1]{2,0,1:T(8,128)(2,1)S(1)} %bitcast.343), channel_id=1, source_target_pairs={{0,1},{1,2},{2,3},{3,4},{4,5},{5,6},{6,7},{8,9},{9,10},{10,11},{11... | collective-permute-start | bytes 3080 | tf_op jit(solution)/shard_map/ppermute | solution.py:32
  61.3 9.6 %collective-permute-start.12 = (bf16[32,4,128]{2,0,1:T(8,128)(2,1)S(1)}, bf16[32,4,128]{2,0,1:T(8,128)(2,1)S(1)}, u32[]{:S(2)}, u32[]{:S(2)}) collective-permute-start(bf16[32,4,128]{2,0,1:T(8,128)(2,1)S(1)} %get-tuple-element.39), channel_id=1, source_target_pairs={{0,8},{8,16},{16,24},{24,32},{32,40},{40,48},{48,56},{56,64},{64,7... | collective-permute-start | bytes 98312 | tf_op jit(solution)/shard_map/ppermute | solution.py:19
  68.8 6.1 %collective-permute-start.13 = (bf16[32,4,128]{2,0,1:T(8,128)(2,1)S(1)}, bf16[32,4,128]{2,0,1:T(8,128)(2,1)S(1)}, u32[]{:S(2)}, u32[]{:S(2)}) collective-permute-start(bf16[32,4,128]{2,0,1:T(8,128)(2,1)S(1)} %get-tuple-element.40), channel_id=1, source_target_pairs={{8,0},{16,8},{24,16},{32,24},{40,32},{48,40},{56,48},{64,56},{72,6... | collective-permute-start | bytes 98312 | tf_op jit(solution)/shard_map/ppermute | solution.py:20
  75.1 7.2 %collective-permute-start.14 = (bf16[32,24,8]{2,0,1:T(8,128)(2,1)S(1)}, bf16[32,24,8]{2,0,1:T(8,128)(2,1)S(1)}, u32[]{:S(2)}, u32[]{:S(2)}) collective-permute-start(bf16[32,24,8]{2,0,1:T(8,128)(2,1)S(1)} %get-tuple-element.25), channel_id=1, source_target_pairs={{1,0},{2,1},{3,2},{4,3},{5,4},{6,5},{7,6},{9,8},{10,9},{11,10},{12... | collective-permute-start | bytes 36872 | tf_op jit(solution)/shard_map/ppermute | solution.py:20
  76.4 7.3 %collective-permute-start.15 = (bf16[32,24,8]{2,0,1:T(8,128)(2,1)S(1)}, bf16[32,24,8]{2,0,1:T(8,128)(2,1)S(1)}, u32[]{:S(2)}, u32[]{:S(2)}) collective-permute-start(bf16[32,24,8]{2,0,1:T(8,128)(2,1)S(1)} %get-tuple-element.26), channel_id=1, source_target_pairs={{0,1},{1,2},{2,3},{3,4},{4,5},{5,6},{6,7},{8,9},{9,10},{10,11},{11... | collective-permute-start | bytes 36872 | tf_op jit(solution)/shard_map/ppermute | solution.py:19
  86.5 7.5 %collective-permute-start.16 = (bf16[32,4,128]{2,0,1:T(8,128)(2,1)S(1)}, bf16[32,4,128]{2,0,1:T(8,128)(2,1)S(1)}, u32[]{:S(2)}, u32[]{:S(2)}) collective-permute-start(bf16[32,4,128]{2,0,1:T(8,128)(2,1)S(1)} %get-tuple-element.37), channel_id=1, source_target_pairs={{8,0},{16,8},{24,16},{32,24},{40,32},{48,40},{56,48},{64,56},{72,6... | collective-permute-start | bytes 98312 | tf_op jit(solution)/shard_map/ppermute | solution.py:20
  94.2 7.9 %collective-permute-start.18 = (bf16[32,24,8]{2,0,1:T(8,128)(2,1)S(1)}, bf16[32,24,8]{2,0,1:T(8,128)(2,1)S(1)}, u32[]{:S(2)}, u32[]{:S(2)}) collective-permute-start(bf16[32,24,8]{2,0,1:T(8,128)(2,1)S(1)} %get-tuple-element.21), channel_id=1, source_target_pairs={{0,1},{1,2},{2,3},{3,4},{4,5},{5,6},{6,7},{8,9},{9,10},{10,11},{11... | collective-permute-start | bytes 36872 | tf_op jit(solution)/shard_map/ppermute | solution.py:19
  99.0 9.9 %collective-permute-start.19 = (bf16[32,24,8]{2,0,1:T(8,128)(2,1)S(1)}, bf16[32,24,8]{2,0,1:T(8,128)(2,1)S(1)}, u32[]{:S(2)}, u32[]{:S(2)}) collective-permute-start(bf16[32,24,8]{2,0,1:T(8,128)(2,1)S(1)} %get-tuple-element.22), channel_id=1, source_target_pairs={{1,0},{2,1},{3,2},{4,3},{5,4},{6,5},{7,6},{9,8},{10,9},{11,10},{12... | collective-permute-start | bytes 36872 | tf_op jit(solution)/shard_map/ppermute | solution.py:20
  111.2 7.4 %collective-permute-start.20 = (bf16[32,16,128]{2,0,1:T(8,128)(2,1)S(1)}, bf16[32,16,128]{2,0,1:T(8,128)(2,1)S(1)}, u32[]{:S(2)}, u32[]{:S(2)}) collective-permute-start(bf16[32,16,128]{2,0,1:T(8,128)(2,1)S(1)} %fusion.37), channel_id=1, source_target_pairs={{0,1},{1,0},{2,3},{3,2},{4,5},{5,4},{6,7},{7,6},{8,9},{9,8},{10,11... | collective-permute-start | bytes 393224 | tf_op jit(solution)/shard_map/ppermute | solution.py:26
  118.6 6.5 %collective-permute-start.21 = (bf16[32,16,128]{2,0,1:T(8,128)(2,1)S(1)}, bf16[32,16,128]{2,0,1:T(8,128)(2,1)S(1)}, u32[]{:S(2)}, u32[]{:S(2)}) collective-permute-start(bf16[32,16,128]{2,0,1:T(8,128)(2,1)S(1)} %collective-permute-done.20), channel_id=1, source_target_pairs={{0,2},{1,3},{2,0},{3,1},{4,6},{5,7},{6,4},{7,5},{8,10},{9,11},{10,... | collective-permute-start | bytes 393224 | tf_op jit(solution)/shard_map/ppermute | solution.py:26
  125.1 7.2 %collective-permute-start.22 = (bf16[32,16,128]{2,0,1:T(8,128)(2,1)S(1)}, bf16[32,16,128]{2,0,1:T(8,128)(2,1)S(1)}, u32[]{:S(2)}, u32[]{:S(2)}) collective-permute-start(bf16[32,16,128]{2,0,1:T(8,128)(2,1)S(1)} %collective-permute-done.21), channel_id=1, source_target_pairs={{0,4},{1,5},{2,6},{3,7},{4,0},{5,1},{6,2},{7,3},{8,12},{9,13},{10,... | collective-permute-start | bytes 393224 | tf_op jit(solution)/shard_map/ppermute | solution.py:26
  254.4 9.1 %collective-permute-start.24 = (bf16[32,2,128]{2,0,1:T(8,128)(2,1)S(1)}, bf16[32,2,128]{2,0,1:T(8,128)(2,1)S(1)}, u32[]{:S(2)}, u32[]{:S(2)}) collective-permute-start(bf16[32,2,128]{2,0,1:T(8,128)(2,1)S(1)} %get-tuple-element.35), channel_id=1, source_target_pairs={{8,0},{16,8},{24,16},{32,24},{40,32},{48,40},{56,48},{64,56},{72,6... | collective-permute-start | bytes 49160 | tf_op jit(solution)/shard_map/ppermute | solution.py:20
  257.0 6.6 %collective-permute-start.25 = (bf16[32,2,128]{2,0,1:T(8,128)(2,1)S(1)}, bf16[32,2,128]{2,0,1:T(8,128)(2,1)S(1)}, u32[]{:S(2)}, u32[]{:S(2)}) collective-permute-start(bf16[32,2,128]{2,0,1:T(8,128)(2,1)S(1)} %get-tuple-element.36), channel_id=1, source_target_pairs={{0,8},{8,16},{16,24},{24,32},{32,40},{40,48},{48,56},{56,64},{64,7... | collective-permute-start | bytes 49160 | tf_op jit(solution)/shard_map/ppermute | solution.py:19
  265.9 9.6 %collective-permute-start.27 = (bf16[32,20,4]{2,0,1:T(8,128)(2,1)S(1)}, bf16[32,20,4]{2,0,1:T(8,128)(2,1)S(1)}, u32[]{:S(2)}, u32[]{:S(2)}) collective-permute-start(bf16[32,20,4]{2,0,1:T(8,128)(2,1)S(1)} %get-tuple-element.30), channel_id=1, source_target_pairs={{1,0},{2,1},{3,2},{4,3},{5,4},{6,5},{7,6},{9,8},{10,9},{11,10},{12... | collective-permute-start | bytes 15368 | tf_op jit(solution)/shard_map/ppermute | solution.py:20
  (11 other events, 56.4 us)
Sparse Core Ops, SparseCore 0:
  263.7 268.3 all-reduce.2
where the time goes:
time: 542 us; the launch traced here: 541 us
  waiting for transfers between devices  295 us (54%)
  blocking collectives  114 us (21%)
  starting transfers between devices  94 us (17%)
  between operations  14.9 us (3%)
  matrix products  13.5 us (2%)
  other arithmetic  6.8 us (1%)
    psum x1, waiting for transfers between devices, local(): lax.psum((conv_total, mix_total, gain_total, bias_total), ('pos', 'off'))  254 us
    psum x1, blocking collectives, local(): lax.psum((conv_total, mix_total, gain_total, bias_total), ('pos', 'off'))  114 us
    ppermute x8, starting transfers between devices, with_halo(): before = lax.ppermute(last, axis, up)  37.3 us
    ppermute x9, starting transfers between devices, from_partner(): lax.ppermute(shard, axis, [(i, i ^ 1 << distance) for i in range(lax.axis...  31.5 us
    ppermute x8, waiting for transfers between devices, with_halo(): after = lax.ppermute(first, axis, down)  21.4 us
    ppermute x8, starting transfers between devices, with_halo(): after = lax.ppermute(first, axis, down)  16 us
  transfers between devices with their start and end apart: 29, of which 18 were waited for; matrix products, arithmetic and copies ran while one was open for 2% of the time, Pallas kernels for 0%

commit v1 on v0

--- a/solution.py
+++ b/solution.py
@@ -22,14 +22,15 @@
     return shard
 
 
-def from_partner(shard, axis, distance):
-    return lax.ppermute(shard, axis, [(i, i ^ 1 << distance) for i in range(lax.axis_size(axis))])
-
-
-def shifted(block, axis, distance):
-    devices = range(lax.axis_size(axis))
-    route = [(i - distance, i) for i in devices if i - distance in devices]
-    return lax.ppermute(block, axis, route)
+def summed_over_mesh(flat):
+    rows, columns = (lax.axis_size("pos"), lax.axis_size("off"))
+    pad = -flat.shape[0] % (rows * 128)
+    parts = jnp.pad(flat, (0, pad)).reshape(rows, -1)
+    part = jnp.sum(lax.all_to_all(parts, "pos", 0, 0, tiled=True), axis=0)
+    copies = jnp.broadcast_to(part[None], (columns,) + part.shape)
+    part = jnp.sum(lax.all_to_all(copies, "off", 0, 0, tiled=True), axis=0)
+    copies = jnp.broadcast_to(part[None], (rows,) + part.shape)
+    return lax.all_to_all(copies, "pos", 0, 0, tiled=True).reshape(-1)[: flat.shape[0]]
 
 
 def tap_list(dilation):
@@ -65,12 +66,10 @@
 
 
 def reflect(source):
-    reversed_tile = source
-    for binary_digit_index in range(lax.axis_size("off").bit_length() - 1):
-        reversed_tile = from_partner(reversed_tile, "off", binary_digit_index)
-    edge_col = shifted(reversed_tile[:, :, :1], "off", 1)
-    flipped = reversed_tile[:, :, ::-1]
-    return jnp.concatenate([edge_col, flipped[:, :, :-1]], axis=2)
+    devices = lax.axis_size("off")
+    opposite = lax.ppermute(source, "off", [(i, devices - 1 - i) for i in range(devices)])
+    edge_col = lax.ppermute(source[:, :, :1], "off", [(devices - i, i) for i in range(1, devices)])
+    return jnp.concatenate([edge_col, opposite[:, :, :0:-1]], axis=2)
 
 
 def local(band_in, conv_weight, mix_weight, norm_gain, norm_bias, cotangent):
@@ -150,8 +149,14 @@
     mix_total = jnp.stack([grad_parts[0][1], grad_parts[1][1]])
     gain_total = jnp.stack([grad_parts[0][2], grad_parts[1][2]])
     bias_total = jnp.stack([grad_parts[0][3], grad_parts[1][3]])
-    conv_total, mix_total, gain_total, bias_total = lax.psum(
-        (conv_total, mix_total, gain_total, bias_total), ("pos", "off")
+    totals = (conv_total, mix_total, gain_total, bias_total)
+    flat = summed_over_mesh(jnp.concatenate([total.reshape(-1) for total in totals]))
+    starts = [0]
+    for total in totals:
+        starts.append(starts[-1] + total.size)
+    conv_total, mix_total, gain_total, bias_total = (
+        flat[start : start + total.size].reshape(total.shape)
+        for start, total in zip(starts, totals)
     )
     return (
         gradient,

time: 542 us -> 194 us (0.36)
  waiting for transfers between devices: 295 us -> 51.1 us
  blocking collectives: 114 us -> 0 us
  starting transfers between devices: 94 us -> 116 us
  between operations: 14.9 us -> 1.57 us
    psum x1 -> x0, waiting for transfers between devices: 254 us -> none  [local(): lax.psum((conv_total, mix_total, gain_total, bias_total), ('pos', 'off'))]
    psum x1 -> x0, blocking collectives: 114 us -> none  [local(): lax.psum((conv_total, mix_total, gain_total, bias_total), ('pos', 'off'))]
    all_to_all x0 -> x3, starting transfers between devices: none -> 43.1 us  [the longest x1 22.4 us: summed_over_mesh(): part = jnp.sum(lax.all_to_all(parts, 'pos', 0, 0, tiled=True), axis=0)]
    ppermute x12 -> x6, starting transfers between devices: 40.7 us -> 10.3 us  [the longest x3 8.25 us: reflect(): lax.ppermute(source, 'off', [(i, devices - 1 - i) for i in range(devices)])]
    all_to_all x0 -> x3, waiting for transfers between devices: none -> 16.3 us  [the longest x1 11.6 us: summed_over_mesh(): lax.all_to_all(copies, 'pos', 0, 0, tiled=True).reshape(-1)[:flat.shape[0]]]
    ppermute x8, starting transfers between devices: 37.3 us -> 47.7 us  [with_halo(): before = lax.ppermute(last, axis, up)]
    ppermute x12 -> x6, waiting for transfers between devices: 14.3 us -> 9.21 us  [the longest x3 9.21 us: reflect(): lax.ppermute(source, 'off', [(i, devices - 1 - i) for i in range(devices)])]
  transfers between devices with their start and end apart: 29 -> 25, of which waited for: 18 -> 13; matrix products, arithmetic and copies ran while one was open for 2% -> 6% of each run, Pallas kernels for 0% -> 0%
where the time goes in v1:
time: 194 us; the launch traced here: 193 us
  starting transfers between devices  116 us (60%)
  waiting for transfers between devices  51.1 us (26%)
  matrix products  13.5 us (7%)
  local copies, waits for them, and re-layouts  6.03 us (3%)
  other arithmetic  4.4 us (2%)
    ppermute x8, starting transfers between devices, with_halo(): before = lax.ppermute(last, axis, up)  47.7 us
    all_to_all x1, starting transfers between devices, summed_over_mesh(): part = jnp.sum(lax.all_to_all(parts, 'pos', 0, 0, tiled=True), axis=0)  22.4 us
    ppermute x8, waiting for transfers between devices, with_halo(): after = lax.ppermute(first, axis, down)  19.6 us
    ppermute x8, starting transfers between devices, with_halo(): after = lax.ppermute(first, axis, down)  15.4 us
    all_to_all x1, starting transfers between devices, summed_over_mesh(): lax.all_to_all(copies, 'pos', 0, 0, tiled=True).reshape(-1)[:flat.shape[0]]  15.3 us
    all_to_all x1, waiting for transfers between devices, summed_over_mesh(): lax.all_to_all(copies, 'pos', 0, 0, tiled=True).reshape(-1)[:flat.shape[0]]  11.6 us
    ppermute x3, waiting for transfers between devices, reflect(): lax.ppermute(source, 'off', [(i, devices - 1 - i) for i in range(devices)])  9.21 us
    ppermute x3, starting transfers between devices, reflect(): lax.ppermute(source, 'off', [(i, devices - 1 - i) for i in range(devices)])  8.25 us
  transfers between devices with their start and end apart: 25, of which 13 were waited for; matrix products, arithmetic and copies ran while one was open for 6% of the time, Pallas kernels for 0%

profile of v1, /device:TPU:1, one launch (start us, length us, event | category | flops | bytes accessed | tf_op | source)
XLA Modules:
  0.0 193.0 jit_solution(5027643954208872299)
XLA Ops:
  1.7 5.7 %collective-permute-start.2 = (bf16[32,2,128]{2,0,1:T(8,128)(2,1)S(1)}, bf16[32,2,128]{2,0,1:T(8,128)(2,1)S(1)}, u32[]{:S(2)}, u32[]{:S(2)}) collective-permute-start(bf16[32,2,128]{2,0,1:T(8,128)(2,1)S(1)} %get-tuple-element.60), channel_id=1, source_target_pairs={{0,8},{8,16},{16,24},{24,32},{32,40},{40,48},{48,56},{56,64},{64,7... | collective-permute-start | bytes 49160 | tf_op jit(solution)/shard_map/ppermute | solution.py:19
  7.4 4.4 %collective-permute-start.3 = (bf16[32,2,128]{2,0,1:T(8,128)(2,1)S(1)}, bf16[32,2,128]{2,0,1:T(8,128)(2,1)S(1)}, u32[]{:S(2)}, u32[]{:S(2)}) collective-permute-start(bf16[32,2,128]{2,0,1:T(8,128)(2,1)S(1)} %get-tuple-element.61), channel_id=1, source_target_pairs={{8,0},{16,8},{24,16},{32,24},{40,32},{48,40},{56,48},{64,56},{72,6... | collective-permute-start | bytes 49160 | tf_op jit(solution)/shard_map/ppermute | solution.py:20
  11.9 2.9 %collective-permute-start.1 = (bf16[32,16,128]{2,0,1:T(8,128)(2,1)S(1)}, bf16[32,16,128]{2,0,1:T(8,128)(2,1)S(1)}, u32[]{:S(2)}, u32[]{:S(2)}) collective-permute-start(bf16[32,16,128]{2,0,1:T(8,128)(2,1)S(1)} %copy.111), channel_id=1, source_target_pairs={{0,7},{1,6},{2,5},{3,4},{4,3},{5,2},{6,1},{7,0},{8,15},{9,14},{10,... | collective-permute-start | bytes 393224 | tf_op jit(solution)/shard_map/ppermute | solution.py:70
  17.2 6.7 %collective-permute-start.5 = (bf16[32,20,4]{2,0,1:T(8,128)(2,1)S(1)}, bf16[32,20,4]{2,0,1:T(8,128)(2,1)S(1)}, u32[]{:S(2)}, u32[]{:S(2)}) collective-permute-start(bf16[32,20,4]{2,0,1:T(8,128)(2,1)S(1)} %get-tuple-element.53), channel_id=1, source_target_pairs={{0,1},{1,2},{2,3},{3,4},{4,5},{5,6},{6,7},{8,9},{9,10},{10,11},{11... | collective-permute-start | bytes 15368 | tf_op jit(solution)/shard_map/ppermute | solution.py:19
  24.0 2.5 %collective-permute-done.4 = bf16[32,20,4]{2,0,1:T(8,128)(2,1)S(1)} collective-permute-done((bf16[32,20,4]{2,0,1:T(8,128)(2,1)S(1)}, bf16[32,20,4]{2,0,1:T(8,128)(2,1)S(1)}, u32[]{:S(2)}, u32[]{:S(2)}) %collective-permute-start.4) | collective-permute-done | bytes 5152 | tf_op jit(solution)/shard_map/ppermute | solution.py:20
  30.1 3.5 %collective-permute-start.7 = (bf16[32,16,128]{2,0,1:T(8,128)(2,1)S(1)}, bf16[32,16,128]{2,0,1:T(8,128)(2,1)S(1)}, u32[]{:S(2)}, u32[]{:S(2)}) collective-permute-start(bf16[32,16,128]{2,0,1:T(8,128)(2,1)S(1)} %fusion.39), channel_id=1, source_target_pairs={{0,7},{1,6},{2,5},{3,4},{4,3},{5,2},{6,1},{7,0},{8,15},{9,14},{10,... | collective-permute-start | bytes 393224 | tf_op jit(solution)/shard_map/ppermute | solution.py:70
  34.6 3.7 %collective-permute-done.7 = bf16[32,16,128]{2,0,1:T(8,128)(2,1)S(1)} collective-permute-done((bf16[32,16,128]{2,0,1:T(8,128)(2,1)S(1)}, bf16[32,16,128]{2,0,1:T(8,128)(2,1)S(1)}, u32[]{:S(2)}, u32[]{:S(2)}) %collective-permute-start.7) | collective-permute-done | bytes 131104 | tf_op jit(solution)/shard_map/ppermute | solution.py:70
  38.8 5.5 %collective-permute-start.8 = (bf16[32,4,128]{2,0,1:T(8,128)(2,1)S(1)}, bf16[32,4,128]{2,0,1:T(8,128)(2,1)S(1)}, u32[]{:S(2)}, u32[]{:S(2)}) collective-permute-start(bf16[32,4,128]{2,0,1:T(8,128)(2,1)S(1)} %get-tuple-element.58), channel_id=1, source_target_pairs={{0,8},{8,16},{16,24},{24,32},{32,40},{40,48},{48,56},{56,64},{64,7... | collective-permute-start | bytes 98312 | tf_op jit(solution)/shard_map/ppermute | solution.py:19
  44.3 1.9 collective-permute-start.9
  46.4 4.0 %collective-permute-done.9 = bf16[32,4,128]{2,0,1:T(8,128)(2,1)S(1)} collective-permute-done((bf16[32,4,128]{2,0,1:T(8,128)(2,1)S(1)}, bf16[32,4,128]{2,0,1:T(8,128)(2,1)S(1)}, u32[]{:S(2)}, u32[]{:S(2)}) %collective-permute-start.9) | collective-permute-done | bytes 32800 | tf_op jit(solution)/shard_map/ppermute | solution.py:20
  51.9 8.2 %collective-permute-start.11 = (bf16[32,24,8]{2,0,1:T(8,128)(2,1)S(1)}, bf16[32,24,8]{2,0,1:T(8,128)(2,1)S(1)}, u32[]{:S(2)}, u32[]{:S(2)}) collective-permute-start(bf16[32,24,8]{2,0,1:T(8,128)(2,1)S(1)} %get-tuple-element.45), channel_id=1, source_target_pairs={{0,1},{1,2},{2,3},{3,4},{4,5},{5,6},{6,7},{8,9},{9,10},{10,11},{11... | collective-permute-start | bytes 36872 | tf_op jit(solution)/shard_map/ppermute | solution.py:19
  67.4 4.5 %collective-permute-start.13 = (bf16[32,4,128]{2,0,1:T(8,128)(2,1)S(1)}, bf16[32,4,128]{2,0,1:T(8,128)(2,1)S(1)}, u32[]{:S(2)}, u32[]{:S(2)}) collective-permute-start(bf16[32,4,128]{2,0,1:T(8,128)(2,1)S(1)} %get-tuple-element.57), channel_id=1, source_target_pairs={{0,8},{8,16},{16,24},{24,32},{32,40},{40,48},{48,56},{56,64},{64,7... | collective-permute-start | bytes 98312 | tf_op jit(solution)/shard_map/ppermute | solution.py:19
  73.8 4.5 %collective-permute-start.14 = (bf16[32,24,8]{2,0,1:T(8,128)(2,1)S(1)}, bf16[32,24,8]{2,0,1:T(8,128)(2,1)S(1)}, u32[]{:S(2)}, u32[]{:S(2)}) collective-permute-start(bf16[32,24,8]{2,0,1:T(8,128)(2,1)S(1)} %get-tuple-element.40), channel_id=1, source_target_pairs={{0,1},{1,2},{2,3},{3,4},{4,5},{5,6},{6,7},{8,9},{9,10},{10,11},{11... | collective-permute-start | bytes 36872 | tf_op jit(solution)/shard_map/ppermute | solution.py:19
  81.3 7.3 %collective-permute-done.15 = bf16[32,24,8]{2,0,1:T(8,128)(2,1)S(1)} collective-permute-done((bf16[32,24,8]{2,0,1:T(8,128)(2,1)S(1)}, bf16[32,24,8]{2,0,1:T(8,128)(2,1)S(1)}, u32[]{:S(2)}, u32[]{:S(2)}) %collective-permute-start.15) | collective-permute-done | bytes 12320 | tf_op jit(solution)/shard_map/ppermute | solution.py:20
  93.6 5.5 %collective-permute-done.17 = bf16[32,16,128]{2,0,1:T(8,128)(2,1)S(1)} collective-permute-done((bf16[32,16,128]{2,0,1:T(8,128)(2,1)S(1)}, bf16[32,16,128]{2,0,1:T(8,128)(2,1)S(1)}, u32[]{:S(2)}, u32[]{:S(2)}) %collective-permute-start.17) | collective-permute-done | bytes 131104 | tf_op jit(solution)/shard_map/ppermute | solution.py:70
  102.2 6.2 %collective-permute-start.19 = (bf16[32,2,128]{2,0,1:T(8,128)(2,1)S(1)}, bf16[32,2,128]{2,0,1:T(8,128)(2,1)S(1)}, u32[]{:S(2)}, u32[]{:S(2)}) collective-permute-start(bf16[32,2,128]{2,0,1:T(8,128)(2,1)S(1)} %get-tuple-element.55), channel_id=1, source_target_pairs={{0,8},{8,16},{16,24},{24,32},{32,40},{40,48},{48,56},{56,64},{64,7... | collective-permute-start | bytes 49160 | tf_op jit(solution)/shard_map/ppermute | solution.py:19
  111.5 22.4 %all-to-all-start = ((f32[64,1,384]{2,1,0:T(1,128)}), f32[64,1,384]{2,1,0:T(1,128)S(1)}, u32[]{:S(2)}, u32[]{:S(2)}) async-start(f32[64,1,384]{2,1,0:T(1,128)} %bitcast.116), calls=%async_computation | async-start | bytes 196608 | tf_op jit(solution)/shard_map/all_to_all | solution.py:29
  134.0 6.4 %collective-permute-start.20 = (bf16[32,20,4]{2,0,1:T(8,128)(2,1)S(1)}, bf16[32,20,4]{2,0,1:T(8,128)(2,1)S(1)}, u32[]{:S(2)}, u32[]{:S(2)}) collective-permute-start(bf16[32,20,4]{2,0,1:T(8,128)(2,1)S(1)} %get-tuple-element.48), channel_id=1, source_target_pairs={{0,1},{1,2},{2,3},{3,4},{4,5},{5,6},{6,7},{8,9},{9,10},{10,11},{11... | collective-permute-start | bytes 15368 | tf_op jit(solution)/shard_map/ppermute | solution.py:19
  142.0 2.2 %collective-permute-done.20 = bf16[32,20,4]{2,0,1:T(8,128)(2,1)S(1)} collective-permute-done((bf16[32,20,4]{2,0,1:T(8,128)(2,1)S(1)}, bf16[32,20,4]{2,0,1:T(8,128)(2,1)S(1)}, u32[]{:S(2)}, u32[]{:S(2)}) %collective-permute-start.20) | collective-permute-done | bytes 5152 | tf_op jit(solution)/shard_map/ppermute | solution.py:19
  144.2 4.7 %collective-permute-done.21 = bf16[32,20,4]{2,0,1:T(8,128)(2,1)S(1)} collective-permute-done((bf16[32,20,4]{2,0,1:T(8,128)(2,1)S(1)}, bf16[32,20,4]{2,0,1:T(8,128)(2,1)S(1)}, u32[]{:S(2)}, u32[]{:S(2)}) %collective-permute-start.21) | collective-permute-done | bytes 5152 | tf_op jit(solution)/shard_map/ppermute | solution.py:20
  151.1 5.3 %all-to-all-start.1 = ((f32[8,1,384]{2,1,0:T(1,128)}), f32[8,1,384]{2,1,0:T(1,128)S(1)}, u32[]{:S(2)}, u32[]{:S(2)}) async-start(f32[8,1,384]{2,1,0:T(1,128)} %broadcast_in_dim.4), calls=%async_computation.1 | async-start | bytes 24576 | tf_op jit(solution)/shard_map/all_to_all | solution.py:31
  156.7 4.8 %all-to-all-done.1 = f32[8,1,384]{2,1,0:T(1,128)S(1)} async-done(((f32[8,1,384]{2,1,0:T(1,128)}), f32[8,1,384]{2,1,0:T(1,128)S(1)}, u32[]{:S(2)}, u32[]{:S(2)}) %all-to-all-start.1) | async-done | bytes 12320 | tf_op jit(solution)/shard_map/all_to_all | solution.py:31
  162.3 15.3 %all-to-all-start.2 = ((f32[64,1,384]{2,1,0:T(1,128)}), f32[64,1,384]{2,1,0:T(1,128)S(1)}, u32[]{:S(2)}, u32[]{:S(2)}) async-start(f32[64,1,384]{2,1,0:T(1,128)} %broadcast_in_dim.5), calls=%async_computation.2 | async-start | bytes 196608 | tf_op jit(solution)/shard_map/all_to_all | solution.py:33
  178.7 11.6 %all-to-all-done.2 = f32[64,1,384]{2,1,0:T(1,128)S(1)} async-done(((f32[64,1,384]{2,1,0:T(1,128)}), f32[64,1,384]{2,1,0:T(1,128)S(1)}, u32[]{:S(2)}, u32[]{:S(2)}) %all-to-all-start.2) | async-done | bytes 98336 | tf_op jit(solution)/shard_map/all_to_all | solution.py:33
  (147 shorter events, 41.7 us)
Async XLA Ops:
  1.7 14.0 %collective-permute-start.2 = (bf16[32,2,128]{2,0,1:T(8,128)(2,1)S(1)}, bf16[32,2,128]{2,0,1:T(8,128)(2,1)S(1)}, u32[]{:S(2)}, u32[]{:S(2)}) collective-permute-start(bf16[32,2,128]{2,0,1:T(8,128)(2,1)S(1)} %get-tuple-element.60), channel_id=1, source_target_pairs={{0,8},{8,16},{16,24},{24,32},{32,40},{40,48},{48,56},{56,64},{64,7... | collective-permute-start | bytes 49160 | tf_op jit(solution)/shard_map/ppermute | solution.py:19
  7.4 8.3 %collective-permute-start.3 = (bf16[32,2,128]{2,0,1:T(8,128)(2,1)S(1)}, bf16[32,2,128]{2,0,1:T(8,128)(2,1)S(1)}, u32[]{:S(2)}, u32[]{:S(2)}) collective-permute-start(bf16[32,2,128]{2,0,1:T(8,128)(2,1)S(1)} %get-tuple-element.61), channel_id=1, source_target_pairs={{8,0},{16,8},{24,16},{32,24},{40,32},{48,40},{56,48},{64,56},{72,6... | collective-permute-start | bytes 49160 | tf_op jit(solution)/shard_map/ppermute | solution.py:20
  11.9 22.3 %collective-permute-start.1 = (bf16[32,16,128]{2,0,1:T(8,128)(2,1)S(1)}, bf16[32,16,128]{2,0,1:T(8,128)(2,1)S(1)}, u32[]{:S(2)}, u32[]{:S(2)}) collective-permute-start(bf16[32,16,128]{2,0,1:T(8,128)(2,1)S(1)} %copy.111), channel_id=1, source_target_pairs={{0,7},{1,6},{2,5},{3,4},{4,3},{5,2},{6,1},{7,0},{8,15},{9,14},{10,... | collective-permute-start | bytes 393224 | tf_op jit(solution)/shard_map/ppermute | solution.py:70
  14.8 19.6 %collective-permute-start = (bf16[32,16,1]{2,0,1:T(8,128)(2,1)S(1)}, bf16[32,16,1]{2,0,1:T(8,128)(2,1)S(1)}, u32[]{:S(2)}, u32[]{:S(2)}) collective-permute-start(bf16[32,16,1]{2,0,1:T(8,128)(2,1)S(1)} %bitcast.347), channel_id=1, source_target_pairs={{7,1},{6,2},{5,3},{4,4},{3,5},{2,6},{1,7},{15,9},{14,10},{13,11},{... | collective-permute-start | bytes 3080 | tf_op jit(solution)/shard_map/ppermute | solution.py:71
  15.9 10.7 %collective-permute-start.4 = (bf16[32,20,4]{2,0,1:T(8,128)(2,1)S(1)}, bf16[32,20,4]{2,0,1:T(8,128)(2,1)S(1)}, u32[]{:S(2)}, u32[]{:S(2)}) collective-permute-start(bf16[32,20,4]{2,0,1:T(8,128)(2,1)S(1)} %get-tuple-element.52), channel_id=1, source_target_pairs={{1,0},{2,1},{3,2},{4,3},{5,4},{6,5},{7,6},{9,8},{10,9},{11,10},{12... | collective-permute-start | bytes 15368 | tf_op jit(solution)/shard_map/ppermute | solution.py:20
  17.2 10.3 %collective-permute-start.5 = (bf16[32,20,4]{2,0,1:T(8,128)(2,1)S(1)}, bf16[32,20,4]{2,0,1:T(8,128)(2,1)S(1)}, u32[]{:S(2)}, u32[]{:S(2)}) collective-permute-start(bf16[32,20,4]{2,0,1:T(8,128)(2,1)S(1)} %get-tuple-element.53), channel_id=1, source_target_pairs={{0,1},{1,2},{2,3},{3,4},{4,5},{5,6},{6,7},{8,9},{9,10},{10,11},{11... | collective-permute-start | bytes 15368 | tf_op jit(solution)/shard_map/ppermute | solution.py:19
  30.1 8.3 %collective-permute-start.7 = (bf16[32,16,128]{2,0,1:T(8,128)(2,1)S(1)}, bf16[32,16,128]{2,0,1:T(8,128)(2,1)S(1)}, u32[]{:S(2)}, u32[]{:S(2)}) collective-permute-start(bf16[32,16,128]{2,0,1:T(8,128)(2,1)S(1)} %fusion.39), channel_id=1, source_target_pairs={{0,7},{1,6},{2,5},{3,4},{4,3},{5,2},{6,1},{7,0},{8,15},{9,14},{10,... | collective-permute-start | bytes 393224 | tf_op jit(solution)/shard_map/ppermute | solution.py:70
  38.8 7.6 %collective-permute-start.8 = (bf16[32,4,128]{2,0,1:T(8,128)(2,1)S(1)}, bf16[32,4,128]{2,0,1:T(8,128)(2,1)S(1)}, u32[]{:S(2)}, u32[]{:S(2)}) collective-permute-start(bf16[32,4,128]{2,0,1:T(8,128)(2,1)S(1)} %get-tuple-element.58), channel_id=1, source_target_pairs={{0,8},{8,16},{16,24},{24,32},{32,40},{40,48},{48,56},{56,64},{64,7... | collective-permute-start | bytes 98312 | tf_op jit(solution)/shard_map/ppermute | solution.py:19
  44.3 6.1 %collective-permute-start.9 = (bf16[32,4,128]{2,0,1:T(8,128)(2,1)S(1)}, bf16[32,4,128]{2,0,1:T(8,128)(2,1)S(1)}, u32[]{:S(2)}, u32[]{:S(2)}) collective-permute-start(bf16[32,4,128]{2,0,1:T(8,128)(2,1)S(1)} %get-tuple-element.59), channel_id=1, source_target_pairs={{8,0},{16,8},{24,16},{32,24},{40,32},{48,40},{56,48},{64,56},{72,6... | collective-permute-start | bytes 98312 | tf_op jit(solution)/shard_map/ppermute | solution.py:20
  50.6 10.7 %collective-permute-start.10 = (bf16[32,24,8]{2,0,1:T(8,128)(2,1)S(1)}, bf16[32,24,8]{2,0,1:T(8,128)(2,1)S(1)}, u32[]{:S(2)}, u32[]{:S(2)}) collective-permute-start(bf16[32,24,8]{2,0,1:T(8,128)(2,1)S(1)} %get-tuple-element.44), channel_id=1, source_target_pairs={{1,0},{2,1},{3,2},{4,3},{5,4},{6,5},{7,6},{9,8},{10,9},{11,10},{12... | collective-permute-start | bytes 36872 | tf_op jit(solution)/shard_map/ppermute | solution.py:20
  51.9 10.8 %collective-permute-start.11 = (bf16[32,24,8]{2,0,1:T(8,128)(2,1)S(1)}, bf16[32,24,8]{2,0,1:T(8,128)(2,1)S(1)}, u32[]{:S(2)}, u32[]{:S(2)}) collective-permute-start(bf16[32,24,8]{2,0,1:T(8,128)(2,1)S(1)} %get-tuple-element.45), channel_id=1, source_target_pairs={{0,1},{1,2},{2,3},{3,4},{4,5},{5,6},{6,7},{8,9},{9,10},{10,11},{11... | collective-permute-start | bytes 36872 | tf_op jit(solution)/shard_map/ppermute | solution.py:19
  65.5 8.2 %collective-permute-start.12 = (bf16[32,4,128]{2,0,1:T(8,128)(2,1)S(1)}, bf16[32,4,128]{2,0,1:T(8,128)(2,1)S(1)}, u32[]{:S(2)}, u32[]{:S(2)}) collective-permute-start(bf16[32,4,128]{2,0,1:T(8,128)(2,1)S(1)} %get-tuple-element.56), channel_id=1, source_target_pairs={{8,0},{16,8},{24,16},{32,24},{40,32},{48,40},{56,48},{64,56},{72,6... | collective-permute-start | bytes 98312 | tf_op jit(solution)/shard_map/ppermute | solution.py:20
  67.4 6.3 %collective-permute-start.13 = (bf16[32,4,128]{2,0,1:T(8,128)(2,1)S(1)}, bf16[32,4,128]{2,0,1:T(8,128)(2,1)S(1)}, u32[]{:S(2)}, u32[]{:S(2)}) collective-permute-start(bf16[32,4,128]{2,0,1:T(8,128)(2,1)S(1)} %get-tuple-element.57), channel_id=1, source_target_pairs={{0,8},{8,16},{16,24},{24,32},{32,40},{40,48},{48,56},{56,64},{64,7... | collective-permute-start | bytes 98312 | tf_op jit(solution)/shard_map/ppermute | solution.py:19
  73.8 7.5 %collective-permute-start.14 = (bf16[32,24,8]{2,0,1:T(8,128)(2,1)S(1)}, bf16[32,24,8]{2,0,1:T(8,128)(2,1)S(1)}, u32[]{:S(2)}, u32[]{:S(2)}) collective-permute-start(bf16[32,24,8]{2,0,1:T(8,128)(2,1)S(1)} %get-tuple-element.40), channel_id=1, source_target_pairs={{0,1},{1,2},{2,3},{3,4},{4,5},{5,6},{6,7},{8,9},{9,10},{10,11},{11... | collective-permute-start | bytes 36872 | tf_op jit(solution)/shard_map/ppermute | solution.py:19
  78.3 10.3 %collective-permute-start.15 = (bf16[32,24,8]{2,0,1:T(8,128)(2,1)S(1)}, bf16[32,24,8]{2,0,1:T(8,128)(2,1)S(1)}, u32[]{:S(2)}, u32[]{:S(2)}) collective-permute-start(bf16[32,24,8]{2,0,1:T(8,128)(2,1)S(1)} %get-tuple-element.41), channel_id=1, source_target_pairs={{1,0},{2,1},{3,2},{4,3},{5,4},{6,5},{7,6},{9,8},{10,9},{11,10},{12... | collective-permute-start | bytes 36872 | tf_op jit(solution)/shard_map/ppermute | solution.py:20
  90.8 8.2 %collective-permute-start.17 = (bf16[32,16,128]{2,0,1:T(8,128)(2,1)S(1)}, bf16[32,16,128]{2,0,1:T(8,128)(2,1)S(1)}, u32[]{:S(2)}, u32[]{:S(2)}) collective-permute-start(bf16[32,16,128]{2,0,1:T(8,128)(2,1)S(1)} %fusion.37), channel_id=1, source_target_pairs={{0,7},{1,6},{2,5},{3,4},{4,3},{5,2},{6,1},{7,0},{8,15},{9,14},{10,... | collective-permute-start | bytes 393224 | tf_op jit(solution)/shard_map/ppermute | solution.py:70
  92.8 6.5 %collective-permute-start.16 = (bf16[32,16,1]{2,0,1:T(8,128)(2,1)S(1)}, bf16[32,16,1]{2,0,1:T(8,128)(2,1)S(1)}, u32[]{:S(2)}, u32[]{:S(2)}) collective-permute-start(bf16[32,16,1]{2,0,1:T(8,128)(2,1)S(1)} %bitcast.344), channel_id=1, source_target_pairs={{7,1},{6,2},{5,3},{4,4},{3,5},{2,6},{1,7},{15,9},{14,10},{13,11},{... | collective-permute-start | bytes 3080 | tf_op jit(solution)/shard_map/ppermute | solution.py:71
  100.2 33.6 %collective-permute-start.18 = (bf16[32,2,128]{2,0,1:T(8,128)(2,1)S(1)}, bf16[32,2,128]{2,0,1:T(8,128)(2,1)S(1)}, u32[]{:S(2)}, u32[]{:S(2)}) collective-permute-start(bf16[32,2,128]{2,0,1:T(8,128)(2,1)S(1)} %get-tuple-element.54), channel_id=1, source_target_pairs={{8,0},{16,8},{24,16},{32,24},{40,32},{48,40},{56,48},{64,56},{72,6... | collective-permute-start | bytes 49160 | tf_op jit(solution)/shard_map/ppermute | solution.py:20
  102.2 31.7 %collective-permute-start.19 = (bf16[32,2,128]{2,0,1:T(8,128)(2,1)S(1)}, bf16[32,2,128]{2,0,1:T(8,128)(2,1)S(1)}, u32[]{:S(2)}, u32[]{:S(2)}) collective-permute-start(bf16[32,2,128]{2,0,1:T(8,128)(2,1)S(1)} %get-tuple-element.55), channel_id=1, source_target_pairs={{0,8},{8,16},{16,24},{24,32},{32,40},{40,48},{48,56},{56,64},{64,7... | collective-permute-start | bytes 49160 | tf_op jit(solution)/shard_map/ppermute | solution.py:19
  111.5 39.0 %all-to-all-start = ((f32[64,1,384]{2,1,0:T(1,128)}), f32[64,1,384]{2,1,0:T(1,128)S(1)}, u32[]{:S(2)}, u32[]{:S(2)}) async-start(f32[64,1,384]{2,1,0:T(1,128)} %bitcast.116), calls=%async_computation | async-start | bytes 196608 | tf_op jit(solution)/shard_map/all_to_all | solution.py:29
  134.0 10.2 %collective-permute-start.20 = (bf16[32,20,4]{2,0,1:T(8,128)(2,1)S(1)}, bf16[32,20,4]{2,0,1:T(8,128)(2,1)S(1)}, u32[]{:S(2)}, u32[]{:S(2)}) collective-permute-start(bf16[32,20,4]{2,0,1:T(8,128)(2,1)S(1)} %get-tuple-element.48), channel_id=1, source_target_pairs={{0,1},{1,2},{2,3},{3,4},{4,5},{5,6},{6,7},{8,9},{9,10},{10,11},{11... | collective-permute-start | bytes 15368 | tf_op jit(solution)/shard_map/ppermute | solution.py:19
  140.5 8.4 %collective-permute-start.21 = (bf16[32,20,4]{2,0,1:T(8,128)(2,1)S(1)}, bf16[32,20,4]{2,0,1:T(8,128)(2,1)S(1)}, u32[]{:S(2)}, u32[]{:S(2)}) collective-permute-start(bf16[32,20,4]{2,0,1:T(8,128)(2,1)S(1)} %get-tuple-element.49), channel_id=1, source_target_pairs={{1,0},{2,1},{3,2},{4,3},{5,4},{6,5},{7,6},{9,8},{10,9},{11,10},{12... | collective-permute-start | bytes 15368 | tf_op jit(solution)/shard_map/ppermute | solution.py:20
  151.1 10.4 %all-to-all-start.1 = ((f32[8,1,384]{2,1,0:T(1,128)}), f32[8,1,384]{2,1,0:T(1,128)S(1)}, u32[]{:S(2)}, u32[]{:S(2)}) async-start(f32[8,1,384]{2,1,0:T(1,128)} %broadcast_in_dim.4), calls=%async_computation.1 | async-start | bytes 24576 | tf_op jit(solution)/shard_map/all_to_all | solution.py:31
  162.3 28.0 %all-to-all-start.2 = ((f32[64,1,384]{2,1,0:T(1,128)}), f32[64,1,384]{2,1,0:T(1,128)S(1)}, u32[]{:S(2)}, u32[]{:S(2)}) async-start(f32[64,1,384]{2,1,0:T(1,128)} %broadcast_in_dim.5), calls=%async_computation.2 | async-start | bytes 196608 | tf_op jit(solution)/shard_map/all_to_all | solution.py:33
  (7 other events, 33.7 us)

commit v2 on v0

v2 whole, which is shorter than its diff:
```python
import math

import jax
import jax.numpy as jnp
from jax import lax
from jax.experimental import pallas as pl
from jax.experimental.pallas import tpu as pltpu
from jax.sharding import PartitionSpec as P

FIRST_DILATION = 2
SECOND_DILATION = 4
CH = 32
TAPS = 9
WIDE_ROWS = 2 * (FIRST_DILATION + SECOND_DILATION)
NARROW_ROWS = FIRST_DILATION + SECOND_DILATION
WIDE_COLS = 32
NARROW_COLS = 16
LANES = 256
GRAD_COLS = 384

SLOPE = 1.702


def tap_list(dilation):
    offsets = []
    for along_row in (-dilation, 0, dilation):
        for along_col in (-dilation, 0, dilation):
            offsets.append(((along_row + along_col) // 2, along_col - along_row))
    return offsets


def logistic(values):
    return 0.5 + 0.5 * jnp.tanh((0.5 * SLOPE) * values)


def smooth(values):
    return values * logistic(values)


def slope_of(values, gate):
    return gate + SLOPE * values * gate * (1.0 - gate)


def twin(halves):
    return jnp.concatenate(halves, axis=0)


def body(
    place,
    wide,
    narrow,
    conv,
    conv_back,
    conv_back_own,
    mix,
    mix_back,
    gain,
    bias,
    out,
    grads,
    act0,
    act1,
    back1,
    back0,
    mid,
    pre0,
    hid0,
    gsum0,
    hid1,
    gsum1,
    sums,
):
    rows = out.shape[0]
    tile = out.shape[2]
    total_rows, total_cols = (place[2], place[3])
    first_row, first_col = (place[0], place[1])
    lane = lax.broadcasted_iota(jnp.int32, (1, LANES), 1)
    column = first_col + jnp.where(lane < LANES - 64, lane, lane - LANES)
    own_ok = jnp.where((column >= 0) & (column < total_cols), 1.0, 0.0)
    mir_ok = jnp.where((column > 0) & (column <= total_cols), 1.0, 0.0)

    def row_ok(local_row):
        row = first_row + local_row
        return jnp.where((row >= 0) & (row < total_rows), 1.0, 0.0)

    def spread(target, index, values, dilation):
        for step in range(-2, 3):
            moved = values
            if step:
                moved = pltpu.roll(values, (-step * dilation) % LANES, 1)
            target[step + 2, index] = moved.astype(jnp.bfloat16)

    def stacked(source, index, dilation, sign, part=slice(None), lanes=slice(None)):
        pieces = []
        for row_shift, col_shift in tap_list(dilation):
            pieces.append(
                source[sign * col_shift // dilation + 2, index + sign * row_shift, part, lanes]
            )
        return jnp.concatenate(pieces, axis=0)

    def dot(left, right):
        return jnp.dot(left, right, preferred_element_type=jnp.float32)

    def own_dot(left, right):
        return lax.dot_general(
            left, right, (((1,), (1,)), ((), ())), preferred_element_type=jnp.float32
        )

    gains = [gain[s] for s in range(2)]
    biases = [bias[s] for s in range(2)]
    gains2 = [twin([g, g]) for g in gains]
    biases2 = [twin([b, b]) for b in biases]
    sums[...] = jnp.zeros_like(sums)

    def first_act(q, carry):
        values = wide[q].astype(jnp.float32)
        values = twin([values[:CH], pltpu.roll(values[CH:], 1, 1)])
        spread(act0, q, smooth(values), FIRST_DILATION)
        return carry

    lax.fori_loop(0, rows + 2 * WIDE_ROWS, first_act, 0)

    def first_block(n, carry):
        q = n + FIRST_DILATION
        pre = dot(conv[0], stacked(act0, q, FIRST_DILATION, 1))
        shifted = gains2[0] * pre + biases2[0]
        hidden = smooth(shifted).astype(jnp.bfloat16)
        mixed = dot(mix[0], hidden)
        values = wide[q].astype(jnp.float32)
        values = twin([values[:CH], pltpu.roll(values[CH:], 1, 1)])
        summed = (values + mixed).astype(jnp.bfloat16).astype(jnp.float32)
        both = (summed[:CH] * own_ok + summed[CH:] * mir_ok) * (0.5 * row_ok(q - WIDE_ROWS))
        both = both.astype(jnp.bfloat16)
        mid[n] = both
        act = smooth(both.astype(jnp.float32))
        spread(act1, n, twin([act * own_ok, act * mir_ok]), SECOND_DILATION)
        inner = q - (WIDE_ROWS - FIRST_DILATION)

        @pl.when((inner >= 0) & (inner < rows + 2 * FIRST_DILATION))
        def _():
            pre0[inner] = pre[:CH]
            hid0[inner] = hidden[:CH]

        return carry

    lax.fori_loop(0, rows + 2 * (WIDE_ROWS - FIRST_DILATION), first_block, 0)

    def second_block(n, carry):
        q = n + SECOND_DILATION
        pre = dot(conv[1], stacked(act1, q, SECOND_DILATION, 1))
        shifted = gains2[1] * pre + biases2[1]
        gate = logistic(shifted)
        cot = narrow[n].astype(jnp.float32)
        total = ((cot[:CH] + pltpu.roll(cot[CH:], 1, 1)) * 0.5).astype(jnp.bfloat16)
        grad = dot(mix_back[1], total)
        grad_pre = twin([grad * own_ok, grad * mir_ok]) * slope_of(shifted, gate)
        grad_conv = grad_pre * gains2[1]
        spread(back1, n, grad_conv, SECOND_DILATION)
        gsum1[n] = total
        inner = n - NARROW_ROWS

        @pl.when((inner >= 0) & (inner < rows))
        def _():
            hid1[inner] = (shifted * gate)[:CH, :tile].astype(jnp.bfloat16)
            own = grad_pre[:CH, :tile]
            sums[2] += own * pre[:CH, :tile]
            sums[3] += own

        return carry

    lax.fori_loop(0, rows + 2 * NARROW_ROWS, second_block, 0)

    def between(n, carry):
        back = dot(conv_back[1], stacked(back1, n + SECOND_DILATION, SECOND_DILATION, -1))
        values = mid[n + NARROW_ROWS + FIRST_DILATION].astype(jnp.float32)
        slope = slope_of(values, logistic(values))
        total = gsum1[n + SECOND_DILATION].astype(jnp.float32)
        grad_in = twin([total, total]) + twin([slope, slope]) * back
        grad_in = grad_in.astype(jnp.bfloat16).astype(jnp.float32)
        both = (grad_in[:CH] * own_ok + grad_in[CH:] * mir_ok) * 0.5
        both = (both * (own_ok * row_ok(n - FIRST_DILATION))).astype(jnp.bfloat16)
        grad = dot(mix_back[0], both)
        pre = pre0[n]
        shifted = gains[0] * pre + biases[0]
        grad_pre = grad * slope_of(shifted, logistic(shifted))
        spread(back0, n, grad_pre * gains[0], FIRST_DILATION)
        gsum0[n] = both

        @pl.when((n >= FIRST_DILATION) & (n < rows + FIRST_DILATION))
        def _():
            own = grad_pre[:, :tile]
            sums[0] += own * pre[:, :tile]
            sums[1] += own

        return carry

    lax.fori_loop(0, rows + 2 * FIRST_DILATION, between, 0)

    near = slice(0, tile)
    own = slice(0, CH)

    def finish(m, carry):
        conv0, conv1, mix0, mix1 = carry

        def pair(load):
            return jnp.concatenate([load(2 * m), load(2 * m + 1)], axis=1)

        back = dot(
            conv_back_own[...],
            pair(lambda n: stacked(back0, n + FIRST_DILATION, FIRST_DILATION, -1, own, near)),
        )
        values = pair(lambda n: wide[n + WIDE_ROWS, own, near]).astype(jnp.float32)
        total0 = pair(lambda n: gsum0[n + FIRST_DILATION, :, near])
        result = total0.astype(jnp.float32) + slope_of(values, logistic(values)) * back
        result = result.astype(jnp.bfloat16)
        out[2 * m] = result[:, :tile]
        out[2 * m + 1] = result[:, tile:]
        grad0 = pair(lambda n: back0[2, n + FIRST_DILATION, :, near])
        grad1 = pair(lambda n: back1[2, n + NARROW_ROWS, own, near])
        stack0 = pair(lambda n: stacked(act0, n + WIDE_ROWS, FIRST_DILATION, 1, own, near))
        stack1 = pair(
            lambda n: stacked(
                act1, n + WIDE_ROWS - FIRST_DILATION, SECOND_DILATION, 1, own, near
            )
        )
        conv0 = conv0 + own_dot(grad0, stack0)
        conv1 = conv1 + own_dot(grad1, stack1)
        mix0 = mix0 + own_dot(total0, pair(lambda n: hid0[n + FIRST_DILATION, :, near]))
        total1 = pair(lambda n: gsum1[n + NARROW_ROWS, :, near])
        mix1 = mix1 + own_dot(total1, pair(lambda n: hid1[n]))
        return conv0, conv1, mix0, mix1

    wide_zero = jnp.zeros((CH, TAPS * CH), jnp.float32)
    small_zero = jnp.zeros((CH, CH), jnp.float32)
    conv0, conv1, mix0, mix1 = lax.fori_loop(
        0, rows // 2, finish, (wide_zero, wide_zero, small_zero, small_zero)
    )
    grads[...] = jnp.zeros_like(grads)
    edge = TAPS * CH
    for s, (conv_s, mix_s) in enumerate(((conv0, mix0), (conv1, mix1))):
        part = slice(s * CH, (s + 1) * CH)
        grads[part, 0:edge] = conv_s
        grads[part, edge : edge + CH] = mix_s
        grads[part, edge + CH : edge + CH + 1] = jnp.sum(sums[2 * s], axis=1, keepdims=True)
        grads[part, edge + CH + 1 : edge + CH + 2] = jnp.sum(
            sums[2 * s + 1], axis=1, keepdims=True
        )


def swap_mesh_tap(weights):
    return weights.reshape((3, 3) + weights.shape[1:]).swapaxes(0, 1).reshape(weights.shape)


def two_sided(weights):
    other = swap_mesh_tap(weights)
    zero = jnp.zeros_like(weights)
    top = jnp.concatenate([weights, zero], axis=2)
    low = jnp.concatenate([zero, other], axis=2)
    both = jnp.concatenate([top, low], axis=1)
    return both.transpose(1, 0, 2).reshape(2 * CH, TAPS * 2 * CH)


def on_tile(wide, narrow, place, conv_weight, mix_weight, norm_gain, norm_bias, rows, tile):
    back = conv_weight.swapaxes(2, 3)
    mix_back = mix_weight.swapaxes(1, 2)
    zero = jnp.zeros_like(mix_weight)
    mix_two = jnp.concatenate(
        [
            jnp.concatenate([mix_weight, zero], axis=2),
            jnp.concatenate([zero, mix_weight], axis=2),
        ],
        axis=1,
    )
    operands = (
        place,
        wide,
        narrow,
        jnp.stack([two_sided(conv_weight[s]) for s in range(2)]),
        jnp.stack([two_sided(back[s]) for s in range(2)]),
        back[0].transpose(1, 0, 2).reshape(CH, TAPS * CH),
        mix_two,
        mix_back,
        norm_gain[:, :, None],
        norm_bias[:, :, None],
    )
    bf16, f32 = (jnp.bfloat16, jnp.float32)
    wide_rows = rows + 2 * WIDE_ROWS
    mid_rows = wide_rows - 2 * FIRST_DILATION
    narrow_rows = rows + 2 * NARROW_ROWS
    inner_rows = rows + 2 * FIRST_DILATION
    vmem = pl.BlockSpec(memory_space=pltpu.VMEM)
    return pl.pallas_call(
        body,
        out_shape=(
            jax.ShapeDtypeStruct((rows, CH, tile), bf16),
            jax.ShapeDtypeStruct((2 * CH, GRAD_COLS), f32),
        ),
        in_specs=[pl.BlockSpec(memory_space=pltpu.SMEM)] + [vmem] * (len(operands) - 1),
        out_specs=(vmem, vmem),
        scratch_shapes=[
            pltpu.VMEM((5, wide_rows, 2 * CH, LANES), bf16),
            pltpu.VMEM((5, mid_rows, 2 * CH, LANES), bf16),
            pltpu.VMEM((5, narrow_rows, 2 * CH, LANES), bf16),
            pltpu.VMEM((5, inner_rows, CH, LANES), bf16),
            pltpu.VMEM((mid_rows, CH, LANES), bf16),
            pltpu.VMEM((inner_rows, CH, LANES), f32),
            pltpu.VMEM((inner_rows, CH, LANES), bf16),
            pltpu.VMEM((inner_rows, CH, LANES), bf16),
            pltpu.VMEM((rows, CH, tile), bf16),
            pltpu.VMEM((narrow_rows, CH, LANES), bf16),
            pltpu.VMEM((4, CH, tile), f32),
        ],
        compiler_params=pltpu.CompilerParams(vmem_limit_bytes=48 * 1024 * 1024),
        name="blocks_backward",
    )(*operands)


def gather_sides(axis, down, up):
    devices = lax.axis_size(axis)
    before = lax.ppermute(down, axis, [(i, i + 1) for i in range(devices - 1)])
    after = lax.ppermute(up, axis, [(i + 1, i) for i in range(devices - 1)])
    return before, after


def packed(wide, narrow, last):
    rows, narrow_rows = (wide.shape[0], narrow.shape[0])
    cut = slice(-WIDE_COLS, None) if last else slice(0, WIDE_COLS)
    wide = wide[:, :, cut]
    per = 128 // WIDE_COLS
    wide = jnp.concatenate(jnp.split(wide, per, axis=0), axis=2)
    cut = slice(-NARROW_COLS, None) if last else slice(0, NARROW_COLS)
    narrow = narrow[:, :, cut]
    per = 128 // NARROW_COLS
    fill = -narrow_rows % per
    narrow = jnp.concatenate([narrow, narrow[:fill]], axis=0)
    narrow = jnp.concatenate(jnp.split(narrow, per, axis=0), axis=2)
    return jnp.concatenate([wide, narrow], axis=0)


def unpacked(message, wide_rows, narrow_rows):
    per = 128 // WIDE_COLS
    count = wide_rows // per
    wide = jnp.concatenate(jnp.split(message[:count], per, axis=2), axis=0)
    per = 128 // NARROW_COLS
    narrow = jnp.concatenate(jnp.split(message[count:], per, axis=2), axis=0)
    return wide, narrow[:narrow_rows]


def with_surroundings(band, cotangent):
    devices = lax.axis_size("off")
    mine = jnp.concatenate([band, cotangent], axis=1)
    other = lax.ppermute(mine[:, :, ::-1], "off", [(i, devices - 1 - i) for i in range(devices)])
    wide = jnp.concatenate([band, other[:, :CH]], axis=1)
    narrow = jnp.concatenate([cotangent, other[:, CH:]], axis=1)
    before, after = gather_sides(
        "pos",
        jnp.concatenate([wide[-WIDE_ROWS:], narrow[-NARROW_ROWS:]], axis=0),
        jnp.concatenate([wide[:WIDE_ROWS], narrow[:NARROW_ROWS]], axis=0),
    )
    wide = jnp.concatenate([before[:WIDE_ROWS], wide, after[:WIDE_ROWS]], axis=0)
    narrow = jnp.concatenate([before[WIDE_ROWS:], narrow, after[WIDE_ROWS:]], axis=0)
    before, after = gather_sides(
        "off", packed(wide, narrow, True), packed(wide, narrow, False)
    )
    before = unpacked(before, wide.shape[0], narrow.shape[0])
    after = unpacked(after, wide.shape[0], narrow.shape[0])
    full = []
    for tile, low, high in zip((wide, narrow), before, after):
        gap = LANES - tile.shape[2] - low.shape[2] - high.shape[2]
        zero = jnp.zeros(tile.shape[:2] + (gap,), tile.dtype)
        full.append(jnp.concatenate([tile, high, zero, low], axis=2))
    return full


def summed_over_mesh(parts):
    rows, columns = (lax.axis_size("pos"), lax.axis_size("off"))
    whole = parts.shape
    parts = parts.reshape(rows, -1)
    part = jnp.sum(lax.all_to_all(parts, "pos", 0, 0, tiled=True), axis=0)
    copies = jnp.broadcast_to(part[None], (columns,) + part.shape)
    part = jnp.sum(lax.all_to_all(copies, "off", 0, 0, tiled=True), axis=0)
    copies = jnp.broadcast_to(part[None], (rows,) + part.shape)
    return lax.all_to_all(copies, "pos", 0, 0, tiled=True).reshape(whole)


def local(band_in, conv_weight, mix_weight, norm_gain, norm_bias, cotangent):
    rows, tile = band_in.shape[1:]
    total_rows = rows * lax.axis_size("pos")
    total_cols = tile * lax.axis_size("off")
    grad_scale = 1.0 / math.sqrt(total_rows * total_cols)
    place = jnp.stack(
        [
            lax.axis_index("pos") * rows,
            lax.axis_index("off") * tile,
            jnp.int32(total_rows),
            jnp.int32(total_cols),
        ]
    )
    wide, narrow = with_surroundings(band_in.swapaxes(0, 1), cotangent.swapaxes(0, 1))
    gradient, grads = on_tile(
        wide, narrow, place, conv_weight, mix_weight, norm_gain, norm_bias, rows, tile
    )
    edge = TAPS * CH
    totals = summed_over_mesh(grads).reshape(2, CH, GRAD_COLS) * grad_scale
    conv_total = totals[:, :, :edge].reshape(2, CH, TAPS, CH).swapaxes(1, 2)
    return (
        gradient.swapaxes(0, 1),
        conv_total,
        totals[:, :, edge : edge + CH],
        totals[:, :, edge + CH],
        totals[:, :, edge + CH + 1],
    )


def solution(mesh):
    placed = (P(None, "pos", "off"), P(), P(), P(), P(), P(None, "pos", "off"))
    return jax.shard_map(
        local,
        mesh=mesh,
        in_specs=placed,
        out_specs=(P(None, "pos", "off"), P(), P(), P(), P()),
        check_vma=False,
    )
```

time: 542 us -> 150 us (0.28)
  waiting for transfers between devices: 295 us -> 21.8 us
  blocking collectives: 114 us -> 42 us
  starting transfers between devices: 94 us -> 29 us
  Pallas kernels: 0 us -> 43.6 us
  between operations: 14.9 us -> 1.11 us
  matrix products: 13.5 us -> 0 us
  local copies, waits for them, and re-layouts: 2.53 us -> 9.26 us
    psum x1 -> x0, waiting for transfers between devices: 254 us -> none  [local(): lax.psum((conv_total, mix_total, gain_total, bias_total), ('pos', 'off'))]
    psum x1 -> x0, blocking collectives: 114 us -> none  [local(): lax.psum((conv_total, mix_total, gain_total, bias_total), ('pos', 'off'))]
    ppermute x28 -> x5, starting transfers between devices: 94 us -> 23.2 us  [the longest x2 10.4 us: gather_sides(): after = lax.ppermute(up, axis, [(i + 1, i) for i in range(devices - 1)])]
    pallas_call x0 -> x1, Pallas kernels: none -> 43.6 us  [on_tile(): pl.pallas_call(body, out_shape=(jax.ShapeDtypeStruct((rows, CH, tile), bf...]
    all_to_all x0 -> x2, blocking collectives: none -> 42 us  [the longest x1 32.5 us: summed_over_mesh(): part = jnp.sum(lax.all_to_all(parts, 'pos', 0, 0, tiled=True), axis=0)]
    ppermute x28 -> x5, waiting for transfers between devices: 40.9 us -> 9.79 us  [the longest x2 6.16 us: gather_sides(): after = lax.ppermute(up, axis, [(i + 1, i) for i in range(devices - 1)])]
    dot_general x59 -> x0, matrix products: 13.5 us -> none  [the longest x18 4.69 us: local(): jnp.einsum('oi,oqc->iqc', conv_weight[section_index, tap_index], window(g...]
    all_to_all x0 -> x1, waiting for transfers between devices: none -> 12 us  [summed_over_mesh(): return lax.all_to_all(copies, 'pos', 0, 0, tiled=True).reshape(whole)]
  transfers between devices with their start and end apart: 29 -> 6, of which waited for: 18 -> 5; matrix products, arithmetic and copies ran while one was open for 2% -> 2% of each run, Pallas kernels for 0% -> 0%
where the time goes in v2:
time: 150 us
  Pallas kernels  43.6 us (29%)
  blocking collectives  42 us (28%)
  starting transfers between devices  29 us (19%)
  waiting for transfers between devices  21.8 us (15%)
  local copies, waits for them, and re-layouts  9.26 us (6%)
  other arithmetic  2.88 us (2%)
    pallas_call x1, Pallas kernels, on_tile(): pl.pallas_call(body, out_shape=(jax.ShapeDtypeStruct((rows, CH, tile), bf...  43.6 us
    all_to_all x1, blocking collectives, summed_over_mesh(): part = jnp.sum(lax.all_to_all(parts, 'pos', 0, 0, tiled=True), axis=0)  32.5 us
    all_to_all x1, waiting for transfers between devices, summed_over_mesh(): return lax.all_to_all(copies, 'pos', 0, 0, tiled=True).reshape(whole)  12 us
    ppermute x2, starting transfers between devices, gather_sides(): after = lax.ppermute(up, axis, [(i + 1, i) for i in range(devices - 1)])  10.4 us
    all_to_all x1, blocking collectives, summed_over_mesh(): part = jnp.sum(lax.all_to_all(copies, 'off', 0, 0, tiled=True), axis=0)  9.42 us
    ppermute x2, starting transfers between devices, gather_sides(): before = lax.ppermute(down, axis, [(i, i + 1) for i in range(devices - 1)])  6.51 us
    ppermute x1, starting transfers between devices, with_surroundings(): lax.ppermute(mine[:, :, ::-1], 'off', [(i, devices - 1 - i) for i in rang...  6.22 us
    ppermute x2, waiting for transfers between devices, gather_sides(): after = lax.ppermute(up, axis, [(i + 1, i) for i in range(devices - 1)])  6.16 us
  transfers between devices with their start and end apart: 6, of which 5 were waited for; matrix products, arithmetic and copies ran while one was open for 2% of the time, Pallas kernels for 0%

profile of v2, /device:TPU:1, one launch (start us, length us, event | category | flops | bytes accessed | tf_op | source)
XLA Modules:
  0.0 149.7 jit_solution(2673202154675271882)
XLA Ops:
  0.6 1.1 copy_bitcast_fusion
  1.9 6.2 %collective-permute-start = (bf16[16,64,128]{2,1,0:T(8,128)(2,1)S(1)}, bf16[16,64,128]{2,1,0:T(8,128)(2,1)S(1)}, u32[]{:S(2)}, u32[]{:S(2)}) collective-permute-start(bf16[16,64,128]{2,1,0:T(8,128)(2,1)S(1)} %rev.3), channel_id=1, source_target_pairs={{0,7},{1,6},{2,5},{3,4},{4,3},{5,2},{6,1},{7,0},{8,15},{9,14},{10,... | collective-permute-start | bytes 786440 | tf_op jit(solution)/shard_map/ppermute | solution.py:352
  8.6 3.3 %collective-permute-done = bf16[16,64,128]{2,1,0:T(8,128)(2,1)S(1)} collective-permute-done((bf16[16,64,128]{2,1,0:T(8,128)(2,1)S(1)}, bf16[16,64,128]{2,1,0:T(8,128)(2,1)S(1)}, u32[]{:S(2)}, u32[]{:S(2)}) %collective-permute-start) | collective-permute-done | bytes 262176 | tf_op jit(solution)/shard_map/ppermute | solution.py:352
  12.0 9.2 %collective-permute-start.2 = (bf16[18,64,128]{2,1,0:T(8,128)(2,1)S(1)}, bf16[18,64,128]{2,1,0:T(8,128)(2,1)S(1)}, u32[]{:S(2)}, u32[]{:S(2)}) collective-permute-start(bf16[18,64,128]{2,1,0:T(8,128)(2,1)S(1)} %fusion.19), channel_id=1, source_target_pairs={{8,0},{16,8},{24,16},{32,24},{40,32},{48,40},{56,48},{64,56},{72,6... | collective-permute-start | bytes 884744 | tf_op jit(solution)/shard_map/ppermute | solution.py:321
  21.2 1.9 %collective-permute-start.1 = (bf16[18,64,128]{2,1,0:T(8,128)(2,1)S(1)}, bf16[18,64,128]{2,1,0:T(8,128)(2,1)S(1)}, u32[]{:S(2)}, u32[]{:S(2)}) collective-permute-start(bf16[18,64,128]{2,1,0:T(8,128)(2,1)S(1)} %pad_maximum_fusion.2), channel_id=1, source_target_pairs={{0,8},{8,16},{16,24},{24,32},{32,40},{40,48},{48,56},{56,64},{64,7... | collective-permute-start | bytes 884744 | tf_op jit(solution)/shard_map/ppermute | solution.py:320
  24.5 2.7 %collective-permute-done.2 = bf16[18,64,128]{2,1,0:T(8,128)(2,1)S(1)} collective-permute-done((bf16[18,64,128]{2,1,0:T(8,128)(2,1)S(1)}, bf16[18,64,128]{2,1,0:T(8,128)(2,1)S(1)}, u32[]{:S(2)}, u32[]{:S(2)}) %collective-permute-start.2) | collective-permute-done | bytes 294944 | tf_op jit(solution)/shard_map/ppermute | solution.py:321
  27.4 0.3 collective-permute-done.1
  28.0 0.2 concatenate.133
  28.8 0.4 fusion.33
  29.2 1.3 collective-permute-start.3
  30.8 4.6 %collective-permute-start.4 = (bf16[14,64,128]{2,1,0:T(8,128)(2,1)S(1)}, bf16[14,64,128]{2,1,0:T(8,128)(2,1)S(1)}, u32[]{:S(2)}, u32[]{:S(2)}) collective-permute-start(bf16[14,64,128]{2,1,0:T(8,128)(2,1)S(1)} %get-tuple-element.42), channel_id=1, source_target_pairs={{0,1},{1,2},{2,3},{3,4},{4,5},{5,6},{6,7},{8,9},{9,10},{10,11},{11... | collective-permute-start | bytes 688136 | tf_op jit(solution)/shard_map/ppermute | solution.py:320
  35.4 3.4 %collective-permute-done.3 = bf16[14,64,128]{2,1,0:T(8,128)(2,1)S(1)} collective-permute-done((bf16[14,64,128]{2,1,0:T(8,128)(2,1)S(1)}, bf16[14,64,128]{2,1,0:T(8,128)(2,1)S(1)}, u32[]{:S(2)}, u32[]{:S(2)}) %collective-permute-start.3) | collective-permute-done | bytes 229408 | tf_op jit(solution)/shard_map/ppermute | solution.py:321
  40.1 0.3 pad_maximum_fusion.narrow
  40.9 1.2 maximum_maximum_fusion.wide
  42.1 43.6 %blocks_backward.1 = (bf16[16,32,128]{2,1,0:T(8,128)(2,1)S(1)}, f32[64,384]{1,0:T(8,128)S(1)}) custom-call(s32[4]{0:T(128)S(1)} %pad_add_fusion.place, bf16[40,64,256]{2,1,0:T(8,128)(2,1)S(1)} %maximum_maximum_fusion.wide, bf16[28,64,256]{2,1,0:T(8,128)(2,1)S(1)} %pad_maximum_fusion.narrow, bf16[2,64,576]{2,1,0:T(8,128)(2,1)S(1)} %pad_maximum_fusion.3.conv, ...), custom_call_target="tpu_custom_call" | custom-call | tf_op jit(solution)/shard_map/blocks_backward/pallas_call | solution.py:292
  85.8 32.5 %all_to_all.21 = f32[64,1,384]{2,1,0:T(1,128)S(1)} all-to-all(f32[64,1,384]{2,1,0:T(1,128)S(1)} %copy.139), channel_id=1, replica_groups=mesh['pos'=64,'off'=8] {'pos'}, dimensions={0} | all-to-all | bytes 196608 | tf_op jit(solution)/shard_map/all_to_all | solution.py:379
  118.4 9.4 %all_to_all.22 = f32[8,1,384]{2,1,0:T(1,128)S(1)} all-to-all(f32[8,1,384]{2,1,0:T(1,128)S(1)} %broadcast_in_dim.29), channel_id=1, replica_groups=mesh['pos'=64,'off'=8] {'off'}, dimensions={0} | all-to-all | bytes 24576 | tf_op jit(solution)/shard_map/all_to_all | solution.py:381
  127.9 0.7 broadcast_in_dim.30
  128.6 5.9 %all-to-all-start.2 = ((f32[64,1,384]{2,1,0:T(1,128)}), f32[64,1,384]{2,1,0:T(1,128)S(1)}, u32[]{:S(2)}, u32[]{:S(2)}) async-start(f32[64,1,384]{2,1,0:T(1,128)} %broadcast_in_dim.30), calls=%async_computation.2 | async-start | bytes 196608 | tf_op jit(solution)/shard_map/all_to_all | solution.py:383
  134.5 0.7 copy.143
  135.2 12.0 %all-to-all-done.2 = f32[64,1,384]{2,1,0:T(1,128)S(1)} async-done(((f32[64,1,384]{2,1,0:T(1,128)}), f32[64,1,384]{2,1,0:T(1,128)S(1)}, u32[]{:S(2)}, u32[]{:S(2)}) %all-to-all-start.2) | async-done | bytes 98336 | tf_op jit(solution)/shard_map/all_to_all | solution.py:383
  147.2 0.7 slice.172
  147.9 0.7 slice_reduce_fusion
  148.8 0.9 copy.144
  (76 shorter events, 5.2 us)
Async XLA Ops:
  0.6 7.5 %copy-start = (bf16[2,9,32,32]{3,2,1,0:T(8,128)(2,1)S(1)}, bf16[2,9,32,32]{3,2,1,0:T(8,128)(2,1)}, u32[]{:S(2)}) copy-start(bf16[2,9,32,32]{3,2,1,0:T(8,128)(2,1)} %param.7) | copy-start | bytes 110596
  1.9 10.0 %collective-permute-start = (bf16[16,64,128]{2,1,0:T(8,128)(2,1)S(1)}, bf16[16,64,128]{2,1,0:T(8,128)(2,1)S(1)}, u32[]{:S(2)}, u32[]{:S(2)}) collective-permute-start(bf16[16,64,128]{2,1,0:T(8,128)(2,1)S(1)} %rev.3), channel_id=1, source_target_pairs={{0,7},{1,6},{2,5},{3,4},{4,3},{5,2},{6,1},{7,0},{8,15},{9,14},{10,... | collective-permute-start | bytes 786440 | tf_op jit(solution)/shard_map/ppermute | solution.py:352
  12.0 12.4 %copy-start.2 = (f32[2,32]{1,0:T(2,128)S(1)}, f32[2,32]{1,0:T(2,128)}, u32[]{:S(2)}) copy-start(f32[2,32]{1,0:T(2,128)} %param.9) | copy-start | bytes 772
  12.0 15.2 %collective-permute-start.2 = (bf16[18,64,128]{2,1,0:T(8,128)(2,1)S(1)}, bf16[18,64,128]{2,1,0:T(8,128)(2,1)S(1)}, u32[]{:S(2)}, u32[]{:S(2)}) collective-permute-start(bf16[18,64,128]{2,1,0:T(8,128)(2,1)S(1)} %fusion.19), channel_id=1, source_target_pairs={{8,0},{16,8},{24,16},{32,24},{40,32},{48,40},{56,48},{64,56},{72,6... | collective-permute-start | bytes 884744 | tf_op jit(solution)/shard_map/ppermute | solution.py:321
  21.2 6.5 %collective-permute-start.1 = (bf16[18,64,128]{2,1,0:T(8,128)(2,1)S(1)}, bf16[18,64,128]{2,1,0:T(8,128)(2,1)S(1)}, u32[]{:S(2)}, u32[]{:S(2)}) collective-permute-start(bf16[18,64,128]{2,1,0:T(8,128)(2,1)S(1)} %pad_maximum_fusion.2), channel_id=1, source_target_pairs={{0,8},{8,16},{16,24},{24,32},{32,40},{40,48},{48,56},{56,64},{64,7... | collective-permute-start | bytes 884744 | tf_op jit(solution)/shard_map/ppermute | solution.py:320
  28.7 1.8 %copy-start.3 = (f32[2,32]{1,0:T(2,128)S(1)}, f32[2,32]{1,0:T(2,128)}, u32[]{:S(2)}) copy-start(f32[2,32]{1,0:T(2,128)} %param.10) | copy-start | bytes 772
  28.7 1.9 %copy-start.1 = (bf16[2,32,32]{2,1,0:T(8,128)(2,1)S(1)}, bf16[2,32,32]{2,1,0:T(8,128)(2,1)}, u32[]{:S(2)}) copy-start(bf16[2,32,32]{2,1,0:T(8,128)(2,1)} %param.8) | copy-start | bytes 12292
  29.2 9.6 %collective-permute-start.3 = (bf16[14,64,128]{2,1,0:T(8,128)(2,1)S(1)}, bf16[14,64,128]{2,1,0:T(8,128)(2,1)S(1)}, u32[]{:S(2)}, u32[]{:S(2)}) collective-permute-start(bf16[14,64,128]{2,1,0:T(8,128)(2,1)S(1)} %get-tuple-element.41), channel_id=1, source_target_pairs={{1,0},{2,1},{3,2},{4,3},{5,4},{6,5},{7,6},{9,8},{10,9},{11,10},{12... | collective-permute-start | bytes 688136 | tf_op jit(solution)/shard_map/ppermute | solution.py:321
  30.8 8.7 %collective-permute-start.4 = (bf16[14,64,128]{2,1,0:T(8,128)(2,1)S(1)}, bf16[14,64,128]{2,1,0:T(8,128)(2,1)S(1)}, u32[]{:S(2)}, u32[]{:S(2)}) collective-permute-start(bf16[14,64,128]{2,1,0:T(8,128)(2,1)S(1)} %get-tuple-element.42), channel_id=1, source_target_pairs={{0,1},{1,2},{2,3},{3,4},{4,5},{5,6},{6,7},{8,9},{9,10},{10,11},{11... | collective-permute-start | bytes 688136 | tf_op jit(solution)/shard_map/ppermute | solution.py:320
  128.6 18.6 %all-to-all-start.2 = ((f32[64,1,384]{2,1,0:T(1,128)}), f32[64,1,384]{2,1,0:T(1,128)S(1)}, u32[]{:S(2)}, u32[]{:S(2)}) async-start(f32[64,1,384]{2,1,0:T(1,128)} %broadcast_in_dim.30), calls=%async_computation.2 | async-start | bytes 196608 | tf_op jit(solution)/shard_map/all_to_all | solution.py:383

commit v3 on v2

v3 whole, which is shorter than its diff:
```python
import math

import jax
import jax.numpy as jnp
from jax import lax
from jax.experimental import pallas as pl
from jax.experimental.pallas import tpu as pltpu
from jax.sharding import PartitionSpec as P

FIRST_DILATION = 2
SECOND_DILATION = 4
CH = 32
TAPS = 9
WIDE_ROWS = 2 * (FIRST_DILATION + SECOND_DILATION)
NARROW_ROWS = FIRST_DILATION + SECOND_DILATION
WIDE_COLS = 32
NARROW_COLS = 16
LANES = 256
GRAD_COLS = 384

SLOPE = 1.702


def tap_list(dilation):
    offsets = []
    for along_row in (-dilation, 0, dilation):
        for along_col in (-dilation, 0, dilation):
            offsets.append(((along_row + along_col) // 2, along_col - along_row))
    return offsets


def gated(values):
    half = 0.5 * values
    return half + half * jnp.tanh(SLOPE * half)


def twice_slope(halved, bent):
    return (1.0 + bent) * (1.0 + halved * (1.0 - bent))


def body(
    place,
    wide,
    narrow,
    conv,
    conv_back,
    conv_back_own,
    mix,
    mix_back,
    gain,
    bias,
    out,
    grads,
    act0,
    act1,
    back1,
    back0,
    mid,
    pre0,
    hid0,
    slope0,
    gsum0,
    hid1,
    gsum1,
    pre1,
    slope1,
    masks,
):
    rows = out.shape[0]
    tile = out.shape[2]
    bf16, f32 = (jnp.bfloat16, jnp.float32)
    first_row, first_col, total_rows, total_cols = [place[k] for k in range(4)]
    lane = lax.broadcasted_iota(jnp.int32, (CH, LANES), 1)
    column = first_col + jnp.where(lane < LANES - 64, lane, lane - LANES)
    masks[0] = jnp.where((column >= 0) & (column < total_cols), 1.0, 0.0).astype(bf16)
    masks[1] = jnp.where((column > 0) & (column <= total_cols), 1.0, 0.0).astype(bf16)

    def half_in_rows(local_row):
        row = first_row + local_row
        factor = jnp.where((row >= 0) & (row < total_rows), 0.5, 0.0)
        return jnp.broadcast_to(factor, (CH, LANES)).astype(bf16)

    def spread(target, index, values, dilation):
        stores = []
        for step in range(-2, 3):
            moved = values
            if step:
                moved = pltpu.roll(values, (-step * dilation) % LANES, 1)
            stores.append((target, (step + 2, index), moved))
        return stores

    def over_rows(count, at_once, stores_of):
        def step(m, carry):
            stores = [stores_of(at_once * m + k) for k in range(at_once)]
            for target, index, values in sum(stores, []):
                target[index] = values
            return carry

        lax.fori_loop(0, count // at_once, step, 0)

    def stacked(source, index, dilation, sign, part=slice(None), lanes=slice(None)):
        pieces = []
        for row_shift, col_shift in tap_list(dilation):
            pieces.append(
                source[sign * col_shift // dilation + 2, index + sign * row_shift, part, lanes]
            )
        return jnp.concatenate(pieces, axis=0)

    def dot(left, right):
        return jnp.dot(left, right, preferred_element_type=f32)

    def own_dot(left, right):
        return lax.dot_general(left, right, (((1,), (1,)), ((), ())), preferred_element_type=f32)

    def across(values, count=LANES):
        return jnp.concatenate([values] * (count // 128), axis=1)

    def both_halves(values):
        return jnp.concatenate([values, values], axis=0)

    def first_act(q):
        return spread(act0, q, gated(wide[q].astype(f32)).astype(bf16), FIRST_DILATION)

    over_rows(rows + 2 * WIDE_ROWS, 4, first_act)

    def first_block(n):
        q = n + FIRST_DILATION
        pre = dot(conv[0], stacked(act0, q, FIRST_DILATION, 1))
        hidden = gated(across(gain[0]) * pre + across(bias[0])).astype(bf16)
        summed = (wide[q].astype(f32) + dot(mix[0], hidden)).astype(bf16)
        other = pltpu.roll(summed[CH:], 1, 1)
        both = (summed[:CH] * masks[0] + other * masks[1]) * half_in_rows(q - WIDE_ROWS)
        act = gated(both.astype(f32)).astype(bf16)
        acts = jnp.concatenate([act * masks[0], act * masks[1]], axis=0)
        return spread(act1, n, acts, SECOND_DILATION) + [
            (mid, n, both),
            (pre0, n, pre[:CH]),
            (hid0, n, hidden[:CH, :tile]),
        ]

    over_rows(rows + 2 * (WIDE_ROWS - FIRST_DILATION), 4, first_block)

    def second_block(n):
        pre = dot(conv[1], stacked(act1, n + SECOND_DILATION, SECOND_DILATION, 1))
        halved = (0.5 * SLOPE) * (across(gain[1]) * pre + across(bias[1]))
        bent = jnp.tanh(halved)
        cot = narrow[n]
        total = (cot[:CH] + pltpu.roll(cot[CH:], 1, 1)) * jnp.asarray(0.5, bf16)
        sides = jnp.concatenate([total * masks[0], total * masks[1]], axis=0)
        grad_pre = dot(mix_back[1], sides) * twice_slope(halved, bent)
        hidden = (halved[:CH, :tile] * (1.0 / SLOPE)) * (1.0 + bent[:CH, :tile])
        grad_conv = (grad_pre * across(gain[1])).astype(bf16)
        return spread(back1, n, grad_conv, SECOND_DILATION) + [
            (gsum1, n, total),
            (pre1, n, pre[:CH, :tile]),
            (slope1, n, grad_pre[:CH, :tile]),
            (hid1, n, hidden.astype(bf16)),
        ]

    over_rows(rows + 2 * NARROW_ROWS, 4, second_block)

    def between(n):
        back = dot(conv_back[...], stacked(back1, n + SECOND_DILATION, SECOND_DILATION, -1))
        halved = (0.5 * SLOPE) * mid[n + NARROW_ROWS + FIRST_DILATION].astype(f32)
        slope = twice_slope(halved, jnp.tanh(halved))
        total = gsum1[n + SECOND_DILATION].astype(f32)
        grad_in = (both_halves(total) + both_halves(slope) * back).astype(bf16)
        both = grad_in[:CH] * masks[0] + grad_in[CH:] * masks[1]
        both = (both * masks[0]) * half_in_rows(n - FIRST_DILATION)
        pre = pre0[n + WIDE_ROWS - 2 * FIRST_DILATION]
        halved = (0.5 * SLOPE) * (across(gain[0, :CH]) * pre + across(bias[0, :CH]))
        grad_pre = dot(mix_back[0, :CH, :CH], both) * twice_slope(halved, jnp.tanh(halved))
        grad_conv = (grad_pre * across(gain[0, :CH])).astype(bf16)
        return spread(back0, n, grad_conv, FIRST_DILATION) + [
            (gsum0, n, both),
            (slope0, n, grad_pre[:, :tile]),
        ]

    over_rows(rows + 2 * FIRST_DILATION, 4, between)

    near = slice(0, tile)
    own = slice(0, CH)

    def finish(m, carry):
        conv0, conv1, mix0, mix1, gain0, bias0, gain1, bias1 = carry

        def pair(load):
            return jnp.concatenate([load(2 * m), load(2 * m + 1)], axis=1)

        back = dot(
            conv_back_own[...],
            pair(lambda n: stacked(back0, n + FIRST_DILATION, FIRST_DILATION, -1, own, near)),
        )
        values = pair(lambda n: wide[n + WIDE_ROWS, own, near]).astype(f32)
        halved = (0.5 * SLOPE) * values
        total0 = pair(lambda n: gsum0[n + FIRST_DILATION, :, near])
        result = total0.astype(f32) + twice_slope(halved, jnp.tanh(halved)) * back
        result = result.astype(bf16)
        out[2 * m] = result[:, :tile]
        out[2 * m + 1] = result[:, tile:]
        grad0 = pair(lambda n: back0[2, n + FIRST_DILATION, :, near])
        grad1 = pair(lambda n: back1[2, n + NARROW_ROWS, own, near])
        stack0 = pair(lambda n: stacked(act0, n + WIDE_ROWS, FIRST_DILATION, 1, own, near))
        stack1 = pair(
            lambda n: stacked(
                act1, n + WIDE_ROWS - FIRST_DILATION, SECOND_DILATION, 1, own, near
            )
        )
        conv0 = conv0 + own_dot(grad0, stack0)
        conv1 = conv1 + own_dot(grad1, stack1)
        mix0 = mix0 + own_dot(total0, pair(lambda n: hid0[n + WIDE_ROWS - FIRST_DILATION]))
        total1 = pair(lambda n: gsum1[n + NARROW_ROWS, :, near])
        mix1 = mix1 + own_dot(total1, pair(lambda n: hid1[n + NARROW_ROWS]))
        for n in (2 * m, 2 * m + 1):
            grad = slope0[n + FIRST_DILATION]
            bias0 = bias0 + grad
            gain0 = gain0 + grad * pre0[n + WIDE_ROWS - FIRST_DILATION, :, near]
            grad = slope1[n + NARROW_ROWS]
            bias1 = bias1 + grad
            gain1 = gain1 + grad * pre1[n + NARROW_ROWS]
        return conv0, conv1, mix0, mix1, gain0, bias0, gain1, bias1

    taps_zero = jnp.zeros((CH, TAPS * CH), f32)
    small_zero = jnp.zeros((CH, CH), f32)
    tile_zero = jnp.zeros((CH, tile), f32)
    start = (taps_zero,) * 2 + (small_zero,) * 2 + (tile_zero,) * 4
    conv0, conv1, mix0, mix1, gain0, bias0, gain1, bias1 = lax.fori_loop(
        0, rows // 2, finish, start, unroll=2
    )
    edge = TAPS * CH
    for s, parts in enumerate(((conv0, mix0, gain0, bias0), (conv1, mix1, gain1, bias1))):
        place_s = slice(s * CH, (s + 1) * CH)
        grads[place_s, 0:edge] = parts[0]
        sums = [jnp.sum(part, axis=1, keepdims=True) for part in parts[2:]]
        rest = jnp.zeros((CH, GRAD_COLS - edge - CH - 2), f32)
        grads[place_s, edge:] = jnp.concatenate([parts[1]] + sums + [rest], axis=1)


def swap_mesh_tap(weights):
    return weights.reshape((3, 3) + weights.shape[1:]).swapaxes(0, 1).reshape(weights.shape)


def two_sided(weights):
    other = swap_mesh_tap(weights)
    zero = jnp.zeros_like(weights)
    top = jnp.concatenate([weights, zero], axis=2)
    low = jnp.concatenate([zero, other], axis=2)
    both = jnp.concatenate([top, low], axis=1)
    return both.transpose(1, 0, 2).reshape(2 * CH, TAPS * 2 * CH)


def two_diagonal(weights):
    zero = jnp.zeros_like(weights)
    top = jnp.concatenate([weights, zero], axis=2)
    return jnp.concatenate([top, jnp.concatenate([zero, weights], axis=2)], axis=1)


def on_tile(wide, narrow, place, conv_weight, mix_weight, norm_gain, norm_bias, rows, tile):
    bf16, f32 = (jnp.bfloat16, jnp.float32)
    back = 0.5 * conv_weight.swapaxes(2, 3)

    def per_channel(values):
        return jnp.broadcast_to(jnp.tile(values, (1, 2))[:, :, None], (2, 2 * CH, 128))

    operands = (
        place,
        wide,
        narrow,
        jnp.stack([two_sided(conv_weight[s]) for s in range(2)]),
        two_sided(back[1]),
        back[0].transpose(1, 0, 2).reshape(CH, TAPS * CH),
        two_diagonal(mix_weight),
        two_diagonal(0.5 * mix_weight.swapaxes(1, 2)),
        per_channel(norm_gain),
        per_channel(norm_bias),
    )
    wide_rows = rows + 2 * WIDE_ROWS
    mid_rows = wide_rows - 2 * FIRST_DILATION
    narrow_rows = rows + 2 * NARROW_ROWS
    inner_rows = rows + 2 * FIRST_DILATION
    vmem = pl.BlockSpec(memory_space=pltpu.VMEM)
    return pl.pallas_call(
        body,
        out_shape=(
            jax.ShapeDtypeStruct((rows, CH, tile), bf16),
            jax.ShapeDtypeStruct((2 * CH, GRAD_COLS), f32),
        ),
        in_specs=[pl.BlockSpec(memory_space=pltpu.SMEM)] + [vmem] * (len(operands) - 1),
        out_specs=(vmem, vmem),
        scratch_shapes=[
            pltpu.VMEM((5, wide_rows, 2 * CH, LANES), bf16),
            pltpu.VMEM((5, mid_rows, 2 * CH, LANES), bf16),
            pltpu.VMEM((5, narrow_rows, 2 * CH, LANES), bf16),
            pltpu.VMEM((5, inner_rows, CH, LANES), bf16),
            pltpu.VMEM((mid_rows, CH, LANES), bf16),
            pltpu.VMEM((mid_rows, CH, LANES), f32),
            pltpu.VMEM((mid_rows, CH, tile), bf16),
            pltpu.VMEM((inner_rows, CH, tile), f32),
            pltpu.VMEM((inner_rows, CH, LANES), bf16),
            pltpu.VMEM((narrow_rows, CH, tile), bf16),
            pltpu.VMEM((narrow_rows, CH, LANES), bf16),
            pltpu.VMEM((narrow_rows, CH, tile), f32),
            pltpu.VMEM((narrow_rows, CH, tile), f32),
            pltpu.VMEM((2, CH, LANES), bf16),
        ],
        compiler_params=pltpu.CompilerParams(vmem_limit_bytes=48 * 1024 * 1024),
        name="blocks_backward",
    )(*operands)


def gather_sides(axis, down, up):
    devices = lax.axis_size(axis)
    before = lax.ppermute(down, axis, [(i, i + 1) for i in range(devices - 1)])
    after = lax.ppermute(up, axis, [(i + 1, i) for i in range(devices - 1)])
    return before, after


def packed(wide, narrow, last):
    rows, narrow_rows = (wide.shape[0], narrow.shape[0])
    cut = slice(-WIDE_COLS, None) if last else slice(0, WIDE_COLS)
    wide = wide[:, :, cut]
    per = 128 // WIDE_COLS
    wide = jnp.concatenate(jnp.split(wide, per, axis=0), axis=2)
    cut = slice(-NARROW_COLS, None) if last else slice(0, NARROW_COLS)
    narrow = narrow[:, :, cut]
    per = 128 // NARROW_COLS
    fill = -narrow_rows % per
    narrow = jnp.concatenate([narrow, narrow[:fill]], axis=0)
    narrow = jnp.concatenate(jnp.split(narrow, per, axis=0), axis=2)
    return jnp.concatenate([wide, narrow], axis=0)


def unpacked(message, wide_rows, narrow_rows):
    per = 128 // WIDE_COLS
    count = wide_rows // per
    wide = jnp.concatenate(jnp.split(message[:count], per, axis=2), axis=0)
    per = 128 // NARROW_COLS
    narrow = jnp.concatenate(jnp.split(message[count:], per, axis=2), axis=0)
    return wide, narrow[:narrow_rows]


def with_surroundings(band, cotangent):
    devices = lax.axis_size("off")
    mine = jnp.concatenate([band, cotangent], axis=1)
    other = lax.ppermute(mine[:, :, ::-1], "off", [(i, devices - 1 - i) for i in range(devices)])
    wide = jnp.concatenate([band, other[:, :CH]], axis=1)
    narrow = jnp.concatenate([cotangent, other[:, CH:]], axis=1)
    before, after = gather_sides(
        "pos",
        jnp.concatenate([wide[-WIDE_ROWS:], narrow[-NARROW_ROWS:]], axis=0),
        jnp.concatenate([wide[:WIDE_ROWS], narrow[:NARROW_ROWS]], axis=0),
    )
    wide = jnp.concatenate([before[:WIDE_ROWS], wide, after[:WIDE_ROWS]], axis=0)
    narrow = jnp.concatenate([before[WIDE_ROWS:], narrow, after[WIDE_ROWS:]], axis=0)
    before, after = gather_sides(
        "off", packed(wide, narrow, True), packed(wide, narrow, False)
    )
    before = unpacked(before, wide.shape[0], narrow.shape[0])
    after = unpacked(after, wide.shape[0], narrow.shape[0])
    full = []
    for tile, low, high in zip((wide, narrow), before, after):
        gap = LANES - tile.shape[2] - low.shape[2] - high.shape[2]
        zero = jnp.zeros(tile.shape[:2] + (gap,), tile.dtype)
        full.append(jnp.concatenate([tile, high, zero, low], axis=2))
    return full


def summed_over_mesh(parts):
    rows, columns = (lax.axis_size("pos"), lax.axis_size("off"))
    whole = parts.shape
    parts = parts.reshape(rows, -1)
    part = jnp.sum(lax.all_to_all(parts, "pos", 0, 0, tiled=True), axis=0)
    copies = jnp.broadcast_to(part[None], (columns,) + part.shape)
    part = jnp.sum(lax.all_to_all(copies, "off", 0, 0, tiled=True), axis=0)
    copies = jnp.broadcast_to(part[None], (rows,) + part.shape)
    return lax.all_to_all(copies, "pos", 0, 0, tiled=True).reshape(whole)


def local(band_in, conv_weight, mix_weight, norm_gain, norm_bias, cotangent):
    rows, tile = band_in.shape[1:]
    total_rows = rows * lax.axis_size("pos")
    total_cols = tile * lax.axis_size("off")
    grad_scale = 1.0 / math.sqrt(total_rows * total_cols)
    place = jnp.stack(
        [
            lax.axis_index("pos") * rows,
            lax.axis_index("off") * tile,
            jnp.int32(total_rows),
            jnp.int32(total_cols),
        ]
    )
    wide, narrow = with_surroundings(band_in.swapaxes(0, 1), cotangent.swapaxes(0, 1))
    gradient, grads = on_tile(
        wide, narrow, place, conv_weight, mix_weight, norm_gain, norm_bias, rows, tile
    )
    edge = TAPS * CH
    totals = summed_over_mesh(grads).reshape(2, CH, GRAD_COLS) * grad_scale
    conv_total = totals[:, :, :edge].reshape(2, CH, TAPS, CH).swapaxes(1, 2)
    return (
        gradient.swapaxes(0, 1),
        conv_total,
        totals[:, :, edge : edge + CH],
        totals[:, :, edge + CH],
        totals[:, :, edge + CH + 1],
    )


def solution(mesh):
    placed = (P(None, "pos", "off"), P(), P(), P(), P(), P(None, "pos", "off"))
    return jax.shard_map(
        local,
        mesh=mesh,
        in_specs=placed,
        out_specs=(P(None, "pos", "off"), P(), P(), P(), P()),
        check_vma=False,
    )
```

time: 150 us -> 130 us (0.87)
  Pallas kernels: 43.6 us -> 23.4 us
    pallas_call x1, Pallas kernels: 43.6 us -> 23.4 us  [on_tile(): pl.pallas_call(body, out_shape=(jax.ShapeDtypeStruct((rows, CH, tile), bf...]
  transfers between devices with their start and end apart: 6 -> 6, of which waited for: 5 -> 5; matrix products, arithmetic and copies ran while one was open for 2% -> 3% of each run, Pallas kernels for 0% -> 0%
where the time goes in v3:
time: 130 us; the launch traced here: 129 us
  blocking collectives  42.1 us (32%)
  starting transfers between devices  29 us (22%)
  Pallas kernels  23.4 us (18%)
  waiting for transfers between devices  21.6 us (17%)
  local copies, waits for them, and re-layouts  9.23 us (7%)
  other arithmetic  2.84 us (2%)
    all_to_all x1, blocking collectives, summed_over_mesh(): part = jnp.sum(lax.all_to_all(parts, 'pos', 0, 0, tiled=True), axis=0)  32.7 us
    pallas_call x1, Pallas kernels, on_tile(): pl.pallas_call(body, out_shape=(jax.ShapeDtypeStruct((rows, CH, tile), bf...  23.4 us
    all_to_all x1, waiting for transfers between devices, summed_over_mesh(): return lax.all_to_all(copies, 'pos', 0, 0, tiled=True).reshape(whole)  12 us
    ppermute x2, starting transfers between devices, gather_sides(): after = lax.ppermute(up, axis, [(i + 1, i) for i in range(devices - 1)])  10.4 us
    all_to_all x1, blocking collectives, summed_over_mesh(): part = jnp.sum(lax.all_to_all(copies, 'off', 0, 0, tiled=True), axis=0)  9.41 us
    ppermute x2, waiting for transfers between devices, gather_sides(): after = lax.ppermute(up, axis, [(i + 1, i) for i in range(devices - 1)])  7.33 us
    ppermute x2, starting transfers between devices, gather_sides(): before = lax.ppermute(down, axis, [(i, i + 1) for i in range(devices - 1)])  6.51 us
    ppermute x1, starting transfers between devices, with_surroundings(): lax.ppermute(mine[:, :, ::-1], 'off', [(i, devices - 1 - i) for i in rang...  6.22 us
  transfers between devices with their start and end apart: 6, of which 5 were waited for; matrix products, arithmetic and copies ran while one was open for 3% of the time, Pallas kernels for 0%

profile of v3, /device:TPU:1, one launch (start us, length us, event | category | flops | bytes accessed | tf_op | source)
XLA Modules:
  0.0 129.4 jit_solution(8844295227679198994)
XLA Ops:
  0.6 1.1 copy_bitcast_fusion
  1.9 6.2 %collective-permute-start = (bf16[16,64,128]{2,1,0:T(8,128)(2,1)S(1)}, bf16[16,64,128]{2,1,0:T(8,128)(2,1)S(1)}, u32[]{:S(2)}, u32[]{:S(2)}) collective-permute-start(bf16[16,64,128]{2,1,0:T(8,128)(2,1)S(1)} %rev.3), channel_id=1, source_target_pairs={{0,7},{1,6},{2,5},{3,4},{4,3},{5,2},{6,1},{7,0},{8,15},{9,14},{10,... | collective-permute-start | bytes 786440 | tf_op jit(solution)/shard_map/ppermute | solution.py:345
  10.0 1.9 %collective-permute-done = bf16[16,64,128]{2,1,0:T(8,128)(2,1)S(1)} collective-permute-done((bf16[16,64,128]{2,1,0:T(8,128)(2,1)S(1)}, bf16[16,64,128]{2,1,0:T(8,128)(2,1)S(1)}, u32[]{:S(2)}, u32[]{:S(2)}) %collective-permute-start) | collective-permute-done | bytes 262176 | tf_op jit(solution)/shard_map/ppermute | solution.py:345
  12.0 9.2 %collective-permute-start.2 = (bf16[18,64,128]{2,1,0:T(8,128)(2,1)S(1)}, bf16[18,64,128]{2,1,0:T(8,128)(2,1)S(1)}, u32[]{:S(2)}, u32[]{:S(2)}) collective-permute-start(bf16[18,64,128]{2,1,0:T(8,128)(2,1)S(1)} %fusion.19), channel_id=1, source_target_pairs={{8,0},{16,8},{24,16},{32,24},{40,32},{48,40},{56,48},{64,56},{72,6... | collective-permute-start | bytes 884744 | tf_op jit(solution)/shard_map/ppermute | solution.py:314
  21.2 1.9 %collective-permute-start.1 = (bf16[18,64,128]{2,1,0:T(8,128)(2,1)S(1)}, bf16[18,64,128]{2,1,0:T(8,128)(2,1)S(1)}, u32[]{:S(2)}, u32[]{:S(2)}) collective-permute-start(bf16[18,64,128]{2,1,0:T(8,128)(2,1)S(1)} %pad_maximum_fusion.2), channel_id=1, source_target_pairs={{0,8},{8,16},{16,24},{24,32},{32,40},{40,48},{48,56},{56,64},{64,7... | collective-permute-start | bytes 884744 | tf_op jit(solution)/shard_map/ppermute | solution.py:313
  23.1 4.1 %collective-permute-done.2 = bf16[18,64,128]{2,1,0:T(8,128)(2,1)S(1)} collective-permute-done((bf16[18,64,128]{2,1,0:T(8,128)(2,1)S(1)}, bf16[18,64,128]{2,1,0:T(8,128)(2,1)S(1)}, u32[]{:S(2)}, u32[]{:S(2)}) %collective-permute-start.2) | collective-permute-done | bytes 294944 | tf_op jit(solution)/shard_map/ppermute | solution.py:314
  27.4 0.3 collective-permute-done.1
  28.0 0.2 concatenate.133
  28.7 0.4 fusion.31
  29.1 1.3 collective-permute-start.3
  30.6 4.6 %collective-permute-start.4 = (bf16[14,64,128]{2,1,0:T(8,128)(2,1)S(1)}, bf16[14,64,128]{2,1,0:T(8,128)(2,1)S(1)}, u32[]{:S(2)}, u32[]{:S(2)}) collective-permute-start(bf16[14,64,128]{2,1,0:T(8,128)(2,1)S(1)} %get-tuple-element.42), channel_id=1, source_target_pairs={{0,1},{1,2},{2,3},{3,4},{4,5},{5,6},{6,7},{8,9},{9,10},{10,11},{11... | collective-permute-start | bytes 688136 | tf_op jit(solution)/shard_map/ppermute | solution.py:313
  35.2 3.2 %collective-permute-done.3 = bf16[14,64,128]{2,1,0:T(8,128)(2,1)S(1)} collective-permute-done((bf16[14,64,128]{2,1,0:T(8,128)(2,1)S(1)}, bf16[14,64,128]{2,1,0:T(8,128)(2,1)S(1)}, u32[]{:S(2)}, u32[]{:S(2)}) %collective-permute-start.3) | collective-permute-done | bytes 229408 | tf_op jit(solution)/shard_map/ppermute | solution.py:314
  39.7 0.3 pad_maximum_fusion.narrow
  40.5 1.2 maximum_maximum_fusion.wide
  41.8 23.4 %blocks_backward.1 = (bf16[16,32,128]{2,1,0:T(8,128)(2,1)S(1)}, f32[64,384]{1,0:T(8,128)S(1)}) custom-call(s32[4]{0:T(128)S(1)} %pad_add_fusion.place, bf16[40,64,256]{2,1,0:T(8,128)(2,1)S(1)} %maximum_maximum_fusion.wide, bf16[28,64,256]{2,1,0:T(8,128)(2,1)S(1)} %pad_maximum_fusion.narrow, bf16[2,64,576]{2,1,0:T(8,128)(2,1)S(1)} %pad_maximum_fusion.3.conv, ...), custom_call_target="tpu_custom_call" | custom-call | tf_op jit(solution)/shard_map/blocks_backward/pallas_call | solution.py:282
  65.4 32.7 %all_to_all.21 = f32[64,1,384]{2,1,0:T(1,128)S(1)} all-to-all(f32[64,1,384]{2,1,0:T(1,128)S(1)} %copy.115), channel_id=1, replica_groups=mesh['pos'=64,'off'=8] {'pos'}, dimensions={0} | all-to-all | bytes 196608 | tf_op jit(solution)/shard_map/all_to_all | solution.py:372
  98.2 9.4 %all_to_all.22 = f32[8,1,384]{2,1,0:T(1,128)S(1)} all-to-all(f32[8,1,384]{2,1,0:T(1,128)S(1)} %broadcast_in_dim.32), channel_id=1, replica_groups=mesh['pos'=64,'off'=8] {'off'}, dimensions={0} | all-to-all | bytes 24576 | tf_op jit(solution)/shard_map/all_to_all | solution.py:374
  107.6 0.7 broadcast_in_dim.33
  108.3 5.9 %all-to-all-start.2 = ((f32[64,1,384]{2,1,0:T(1,128)}), f32[64,1,384]{2,1,0:T(1,128)S(1)}, u32[]{:S(2)}, u32[]{:S(2)}) async-start(f32[64,1,384]{2,1,0:T(1,128)} %broadcast_in_dim.33), calls=%async_computation.2 | async-start | bytes 196608 | tf_op jit(solution)/shard_map/all_to_all | solution.py:376
  114.2 0.7 copy.119
  114.9 12.0 %all-to-all-done.2 = f32[64,1,384]{2,1,0:T(1,128)S(1)} async-done(((f32[64,1,384]{2,1,0:T(1,128)}), f32[64,1,384]{2,1,0:T(1,128)S(1)}, u32[]{:S(2)}, u32[]{:S(2)}) %all-to-all-start.2) | async-done | bytes 98336 | tf_op jit(solution)/shard_map/all_to_all | solution.py:376
  127.0 0.7 slice.171
  127.7 0.7 slice_reduce_fusion
  128.6 0.9 copy.120
  (79 shorter events, 5.1 us)
Async XLA Ops:
  0.6 7.5 %copy-start = (bf16[2,9,32,32]{3,2,1,0:T(8,128)(2,1)S(1)}, bf16[2,9,32,32]{3,2,1,0:T(8,128)(2,1)}, u32[]{:S(2)}) copy-start(bf16[2,9,32,32]{3,2,1,0:T(8,128)(2,1)} %param.7) | copy-start | bytes 110596
  1.9 10.0 %collective-permute-start = (bf16[16,64,128]{2,1,0:T(8,128)(2,1)S(1)}, bf16[16,64,128]{2,1,0:T(8,128)(2,1)S(1)}, u32[]{:S(2)}, u32[]{:S(2)}) collective-permute-start(bf16[16,64,128]{2,1,0:T(8,128)(2,1)S(1)} %rev.3), channel_id=1, source_target_pairs={{0,7},{1,6},{2,5},{3,4},{4,3},{5,2},{6,1},{7,0},{8,15},{9,14},{10,... | collective-permute-start | bytes 786440 | tf_op jit(solution)/shard_map/ppermute | solution.py:345
  8.3 1.3 copy-start.1
  8.3 1.4 %copy-start.2 = (f32[2,32]{1,0:T(2,128)S(1)}, f32[2,32]{1,0:T(2,128)}, u32[]{:S(2)}) copy-start(f32[2,32]{1,0:T(2,128)} %param.9) | copy-start | bytes 772
  8.3 1.5 %copy-start.3 = (f32[2,32]{1,0:T(2,128)S(1)}, f32[2,32]{1,0:T(2,128)}, u32[]{:S(2)}) copy-start(f32[2,32]{1,0:T(2,128)} %param.10) | copy-start | bytes 772
  12.0 15.2 %collective-permute-start.2 = (bf16[18,64,128]{2,1,0:T(8,128)(2,1)S(1)}, bf16[18,64,128]{2,1,0:T(8,128)(2,1)S(1)}, u32[]{:S(2)}, u32[]{:S(2)}) collective-permute-start(bf16[18,64,128]{2,1,0:T(8,128)(2,1)S(1)} %fusion.19), channel_id=1, source_target_pairs={{8,0},{16,8},{24,16},{32,24},{40,32},{48,40},{56,48},{64,56},{72,6... | collective-permute-start | bytes 884744 | tf_op jit(solution)/shard_map/ppermute | solution.py:314
  21.2 6.5 %collective-permute-start.1 = (bf16[18,64,128]{2,1,0:T(8,128)(2,1)S(1)}, bf16[18,64,128]{2,1,0:T(8,128)(2,1)S(1)}, u32[]{:S(2)}, u32[]{:S(2)}) collective-permute-start(bf16[18,64,128]{2,1,0:T(8,128)(2,1)S(1)} %pad_maximum_fusion.2), channel_id=1, source_target_pairs={{0,8},{8,16},{16,24},{24,32},{32,40},{40,48},{48,56},{56,64},{64,7... | collective-permute-start | bytes 884744 | tf_op jit(solution)/shard_map/ppermute | solution.py:313
  29.1 9.2 %collective-permute-start.3 = (bf16[14,64,128]{2,1,0:T(8,128)(2,1)S(1)}, bf16[14,64,128]{2,1,0:T(8,128)(2,1)S(1)}, u32[]{:S(2)}, u32[]{:S(2)}) collective-permute-start(bf16[14,64,128]{2,1,0:T(8,128)(2,1)S(1)} %get-tuple-element.41), channel_id=1, source_target_pairs={{1,0},{2,1},{3,2},{4,3},{5,4},{6,5},{7,6},{9,8},{10,9},{11,10},{12... | collective-permute-start | bytes 688136 | tf_op jit(solution)/shard_map/ppermute | solution.py:314
  30.6 8.5 %collective-permute-start.4 = (bf16[14,64,128]{2,1,0:T(8,128)(2,1)S(1)}, bf16[14,64,128]{2,1,0:T(8,128)(2,1)S(1)}, u32[]{:S(2)}, u32[]{:S(2)}) collective-permute-start(bf16[14,64,128]{2,1,0:T(8,128)(2,1)S(1)} %get-tuple-element.42), channel_id=1, source_target_pairs={{0,1},{1,2},{2,3},{3,4},{4,5},{5,6},{6,7},{8,9},{9,10},{10,11},{11... | collective-permute-start | bytes 688136 | tf_op jit(solution)/shard_map/ppermute | solution.py:313
  108.3 18.6 %all-to-all-start.2 = ((f32[64,1,384]{2,1,0:T(1,128)}), f32[64,1,384]{2,1,0:T(1,128)S(1)}, u32[]{:S(2)}, u32[]{:S(2)}) async-start(f32[64,1,384]{2,1,0:T(1,128)} %broadcast_in_dim.33), calls=%async_computation.2 | async-start | bytes 196608 | tf_op jit(solution)/shard_map/all_to_all | solution.py:376

commit v4 on v3

--- a/solution.py
+++ b/solution.py
@@ -17,6 +17,10 @@
 NARROW_COLS = 16
 LANES = 256
 GRAD_COLS = 384
+ACT_ROWS = 8
+FIRST_ROWS = 12
+SECOND_ROWS = 14
+BETWEEN_ROWS = 10
 
 SLOPE = 1.702
 
@@ -40,8 +44,10 @@
 
 def body(
     place,
-    wide,
-    narrow,
+    wide_tile,
+    narrow_tile,
+    before,
+    after,
     conv,
     conv_back,
     conv_back_own,
@@ -65,6 +71,9 @@
     pre1,
     slope1,
     masks,
+    sides,
+    wide,
+    narrow,
 ):
     rows = out.shape[0]
     tile = out.shape[2]
@@ -75,6 +84,15 @@
     masks[0] = jnp.where((column >= 0) & (column < total_cols), 1.0, 0.0).astype(bf16)
     masks[1] = jnp.where((column > 0) & (column <= total_cols), 1.0, 0.0).astype(bf16)
 
+    side_lane = lax.broadcasted_iota(jnp.int32, (2 * CH, 128), 1)
+    wide_slots = 128 // WIDE_COLS
+    for base, cols in ((0, WIDE_COLS), (wide_slots, NARROW_COLS)):
+        for slot in range(128 // cols):
+            here = (side_lane >= slot * cols) & (side_lane < (slot + 1) * cols)
+            sides[0, base + slot] = jnp.where(here, 1.0, 0.0).astype(bf16)
+            sides[1, base + slot] = jnp.where(here, 0.0, 1.0).astype(bf16)
+    own = slice(0, CH)
+
     def half_in_rows(local_row):
         row = first_row + local_row
         factor = jnp.where((row >= 0) & (row < total_rows), 0.5, 0.0)
@@ -89,10 +107,19 @@
             stores.append((target, (step + 2, index), moved))
         return stores
 
-    def over_rows(count, at_once, stores_of):
+    hand_pre, hand_mix = ({}, {})
+
+    def over_rows(count, at_once, *stages):
         def step(m, carry):
-            stores = [stores_of(at_once * m + k) for k in range(at_once)]
-            for target, index, values in sum(stores, []):
+            stores = []
+            for stage in stages:
+                for k in range(at_once):
+                    for target, index, values in stage(at_once * m + k, k):
+                        if isinstance(target, dict):
+                            target[index] = values
+                        else:
+                            stores.append((target, index, values))
+            for target, index, values in stores:
                 target[index] = values
             return carry
 
@@ -118,68 +145,118 @@
     def both_halves(values):
         return jnp.concatenate([values, values], axis=0)
 
-    def first_act(q):
-        return spread(act0, q, gated(wide[q].astype(f32)).astype(bf16), FIRST_DILATION)
-
-    over_rows(rows + 2 * WIDE_ROWS, 4, first_act)
-
-    def first_block(n):
+    def with_sides(tile_row, message, slot, cols):
+        pick = slot if cols == WIDE_COLS else wide_slots + slot
+        both = after[message] * sides[0, pick] + before[message] * sides[1, pick]
+        if slot:
+            both = pltpu.roll(both, 128 - slot * cols, 1)
+        return jnp.concatenate([tile_row, both], axis=1)
+
+    wide_messages = (rows + 2 * WIDE_ROWS) // wide_slots
+    narrow_messages = before.shape[0] - wide_messages
+
+    def fill_wide(m, carry):
+        stores = []
+        for k in range(ACT_ROWS):
+            message = m * (ACT_ROWS // wide_slots) + k // wide_slots
+            slot = k % wide_slots
+            q = message + slot * wide_messages
+            row = with_sides(wide_tile[q], message, slot, WIDE_COLS)
+            stores.append((wide, q, row))
+            stores += spread(act0, q, gated(row.astype(f32)).astype(bf16), FIRST_DILATION)
+        for target, index, values in stores:
+            target[index] = values
+        return carry
+
+    lax.fori_loop(0, (rows + 2 * WIDE_ROWS) // ACT_ROWS, fill_wide, 0)
+
+    def fill_narrow(message, carry):
+        for slot in range((rows + 2 * NARROW_ROWS) // narrow_messages):
+            n = message + slot * narrow_messages
+            narrow[n] = with_sides(
+                narrow_tile[n], wide_messages + message, slot, NARROW_COLS
+            )
+        return carry
+
+    lax.fori_loop(0, narrow_messages, fill_narrow, 0)
+
+    def first_conv(n, k):
+        pre = dot(conv[0], stacked(act0, n + FIRST_DILATION, FIRST_DILATION, 1))
+        return [(hand_pre, k, pre)]
+
+    def first_mix(n, k):
+        pre = hand_pre[k]
+        hidden = gated(across(gain[0]) * pre + across(bias[0])).astype(bf16)
+        return [
+            (hand_mix, k, dot(mix[0], hidden)),
+            (pre0, n, pre[:CH]),
+            (hid0, n, hidden[:CH, :tile]),
+        ]
+
+    def first_mirror(n, k):
         q = n + FIRST_DILATION
-        pre = dot(conv[0], stacked(act0, q, FIRST_DILATION, 1))
-        hidden = gated(across(gain[0]) * pre + across(bias[0])).astype(bf16)
-        summed = (wide[q].astype(f32) + dot(mix[0], hidden)).astype(bf16)
+        summed = (wide[q].astype(f32) + hand_mix[k]).astype(bf16)
         other = pltpu.roll(summed[CH:], 1, 1)
         both = (summed[:CH] * masks[0] + other * masks[1]) * half_in_rows(q - WIDE_ROWS)
         act = gated(both.astype(f32)).astype(bf16)
         acts = jnp.concatenate([act * masks[0], act * masks[1]], axis=0)
-        return spread(act1, n, acts, SECOND_DILATION) + [
-            (mid, n, both),
-            (pre0, n, pre[:CH]),
-            (hid0, n, hidden[:CH, :tile]),
-        ]
-
-    over_rows(rows + 2 * (WIDE_ROWS - FIRST_DILATION), 4, first_block)
-
-    def second_block(n):
+        return spread(act1, n, acts, SECOND_DILATION) + [(mid, n, both)]
+
+    over_rows(
+        rows + 2 * (WIDE_ROWS - FIRST_DILATION), FIRST_ROWS, first_conv, first_mix, first_mirror
+    )
+
+    def second_conv(n, k):
         pre = dot(conv[1], stacked(act1, n + SECOND_DILATION, SECOND_DILATION, 1))
-        halved = (0.5 * SLOPE) * (across(gain[1]) * pre + across(bias[1]))
-        bent = jnp.tanh(halved)
         cot = narrow[n]
         total = (cot[:CH] + pltpu.roll(cot[CH:], 1, 1)) * jnp.asarray(0.5, bf16)
         sides = jnp.concatenate([total * masks[0], total * masks[1]], axis=0)
-        grad_pre = dot(mix_back[1], sides) * twice_slope(halved, bent)
+        return [
+            (hand_pre, k, pre),
+            (hand_mix, k, dot(mix_back[1], sides)),
+            (gsum1, n, total),
+        ]
+
+    def second_slope(n, k):
+        pre = hand_pre[k]
+        halved = (0.5 * SLOPE) * (across(gain[1]) * pre + across(bias[1]))
+        bent = jnp.tanh(halved)
+        grad_pre = hand_mix[k] * twice_slope(halved, bent)
         hidden = (halved[:CH, :tile] * (1.0 / SLOPE)) * (1.0 + bent[:CH, :tile])
         grad_conv = (grad_pre * across(gain[1])).astype(bf16)
         return spread(back1, n, grad_conv, SECOND_DILATION) + [
-            (gsum1, n, total),
             (pre1, n, pre[:CH, :tile]),
             (slope1, n, grad_pre[:CH, :tile]),
             (hid1, n, hidden.astype(bf16)),
         ]
 
-    over_rows(rows + 2 * NARROW_ROWS, 4, second_block)
-
-    def between(n):
-        back = dot(conv_back[...], stacked(back1, n + SECOND_DILATION, SECOND_DILATION, -1))
+    over_rows(rows + 2 * NARROW_ROWS, SECOND_ROWS, second_conv, second_slope)
+
+    def between_conv(n, k):
+        rows_at = n + SECOND_DILATION
+        return [(hand_pre, k, dot(conv_back[...], stacked(back1, rows_at, SECOND_DILATION, -1)))]
+
+    def between_mirror(n, k):
         halved = (0.5 * SLOPE) * mid[n + NARROW_ROWS + FIRST_DILATION].astype(f32)
         slope = twice_slope(halved, jnp.tanh(halved))
         total = gsum1[n + SECOND_DILATION].astype(f32)
-        grad_in = (both_halves(total) + both_halves(slope) * back).astype(bf16)
+        grad_in = (both_halves(total) + both_halves(slope) * hand_pre[k]).astype(bf16)
         both = grad_in[:CH] * masks[0] + grad_in[CH:] * masks[1]
         both = (both * masks[0]) * half_in_rows(n - FIRST_DILATION)
+        return [(hand_mix, (k, own), dot(mix_back[0, :CH, :CH], both)), (gsum0, n, both)]
+
+    def between_slope(n, k):
         pre = pre0[n + WIDE_ROWS - 2 * FIRST_DILATION]
         halved = (0.5 * SLOPE) * (across(gain[0, :CH]) * pre + across(bias[0, :CH]))
-        grad_pre = dot(mix_back[0, :CH, :CH], both) * twice_slope(halved, jnp.tanh(halved))
+        grad_pre = hand_mix[k, own] * twice_slope(halved, jnp.tanh(halved))
         grad_conv = (grad_pre * across(gain[0, :CH])).astype(bf16)
-        return spread(back0, n, grad_conv, FIRST_DILATION) + [
-            (gsum0, n, both),
-            (slope0, n, grad_pre[:, :tile]),
-        ]
-
-    over_rows(rows + 2 * FIRST_DILATION, 4, between)
+        return spread(back0, n, grad_conv, FIRST_DILATION) + [(slope0, n, grad_pre[:, :tile])]
+
+    over_rows(
+        rows + 2 * FIRST_DILATION, BETWEEN_ROWS, between_conv, between_mirror, between_slope
+    )
 
     near = slice(0, tile)
-    own = slice(0, CH)
 
     def finish(m, carry):
         conv0, conv1, mix0, mix1, gain0, bias0, gain1, bias1 = carry
@@ -255,7 +332,7 @@
     return jnp.concatenate([top, jnp.concatenate([zero, weights], axis=2)], axis=1)
 
 
-def on_tile(wide, narrow, place, conv_weight, mix_weight, norm_gain, norm_bias, rows, tile):
+def on_tile(fields, place, conv_weight, mix_weight, norm_gain, norm_bias, rows, tile):
     bf16, f32 = (jnp.bfloat16, jnp.float32)
     back = 0.5 * conv_weight.swapaxes(2, 3)
 
@@ -264,8 +341,7 @@
 
     operands = (
         place,
-        wide,
-        narrow,
+        *fields,
         jnp.stack([two_sided(conv_weight[s]) for s in range(2)]),
         two_sided(back[1]),
         back[0].transpose(1, 0, 2).reshape(CH, TAPS * CH),
@@ -302,6 +378,9 @@
             pltpu.VMEM((narrow_rows, CH, tile), f32),
             pltpu.VMEM((narrow_rows, CH, tile), f32),
             pltpu.VMEM((2, CH, LANES), bf16),
+            pltpu.VMEM((2, 128 // WIDE_COLS + 128 // NARROW_COLS, 2 * CH, 128), bf16),
+            pltpu.VMEM((wide_rows, 2 * CH, LANES), bf16),
+            pltpu.VMEM((narrow_rows, 2 * CH, LANES), bf16),
         ],
         compiler_params=pltpu.CompilerParams(vmem_limit_bytes=48 * 1024 * 1024),
         name="blocks_backward",
@@ -316,27 +395,16 @@
 
 
 def packed(wide, narrow, last):
-    rows, narrow_rows = (wide.shape[0], narrow.shape[0])
-    cut = slice(-WIDE_COLS, None) if last else slice(0, WIDE_COLS)
-    wide = wide[:, :, cut]
-    per = 128 // WIDE_COLS
-    wide = jnp.concatenate(jnp.split(wide, per, axis=0), axis=2)
-    cut = slice(-NARROW_COLS, None) if last else slice(0, NARROW_COLS)
-    narrow = narrow[:, :, cut]
-    per = 128 // NARROW_COLS
-    fill = -narrow_rows % per
-    narrow = jnp.concatenate([narrow, narrow[:fill]], axis=0)
-    narrow = jnp.concatenate(jnp.split(narrow, per, axis=0), axis=2)
-    return jnp.concatenate([wide, narrow], axis=0)
-
-
-def unpacked(message, wide_rows, narrow_rows):
-    per = 128 // WIDE_COLS
-    count = wide_rows // per
-    wide = jnp.concatenate(jnp.split(message[:count], per, axis=2), axis=0)
-    per = 128 // NARROW_COLS
-    narrow = jnp.concatenate(jnp.split(message[count:], per, axis=2), axis=0)
-    return wide, narrow[:narrow_rows]
+    def in_slots(rows, cols):
+        slots = 128 // cols
+        edge = rows[:, :, -cols:] if last else rows[:, :, :cols]
+        edge = jnp.concatenate([edge, edge[: -rows.shape[0] % slots]], axis=0)
+        pieces = jnp.split(edge, slots, axis=0)
+        if last:
+            pieces = pieces[1:] + pieces[:1]
+        return jnp.concatenate(pieces, axis=2)
+
+    return jnp.concatenate([in_slots(wide, WIDE_COLS), in_slots(narrow, NARROW_COLS)], axis=0)
 
 
 def with_surroundings(band, cotangent):
@@ -355,25 +423,26 @@
     before, after = gather_sides(
         "off", packed(wide, narrow, True), packed(wide, narrow, False)
     )
-    before = unpacked(before, wide.shape[0], narrow.shape[0])
-    after = unpacked(after, wide.shape[0], narrow.shape[0])
-    full = []
-    for tile, low, high in zip((wide, narrow), before, after):
-        gap = LANES - tile.shape[2] - low.shape[2] - high.shape[2]
-        zero = jnp.zeros(tile.shape[:2] + (gap,), tile.dtype)
-        full.append(jnp.concatenate([tile, high, zero, low], axis=2))
-    return full
+    return wide, narrow, before, after
 
 
 def summed_over_mesh(parts):
     rows, columns = (lax.axis_size("pos"), lax.axis_size("off"))
-    whole = parts.shape
-    parts = parts.reshape(rows, -1)
-    part = jnp.sum(lax.all_to_all(parts, "pos", 0, 0, tiled=True), axis=0)
-    copies = jnp.broadcast_to(part[None], (columns,) + part.shape)
-    part = jnp.sum(lax.all_to_all(copies, "off", 0, 0, tiled=True), axis=0)
-    copies = jnp.broadcast_to(part[None], (rows,) + part.shape)
-    return lax.all_to_all(copies, "pos", 0, 0, tiled=True).reshape(whole)
+    size = 2 * columns
+    near = [[size * g + i for i in range(size)] for g in range(rows // 2)]
+    far = [[2 * g + i for g in range(rows // 2)] for i in range(2)]
+    axes = ("pos", "off")
+
+    def exchanged(blocks, axis, groups):
+        return lax.all_to_all(blocks, axis, 0, 0, tiled=True, axis_index_groups=groups)
+
+    def copies(part, count):
+        return jnp.broadcast_to(part[None], (count,) + part.shape)
+
+    blocks = parts.reshape(size, -1, parts.shape[1])
+    part = jnp.sum(exchanged(blocks, axes, near), axis=0)
+    part = jnp.sum(exchanged(copies(part, rows // 2), "pos", far), axis=0)
+    return exchanged(copies(part, size), axes, near).reshape(parts.shape)
 
 
 def local(band_in, conv_weight, mix_weight, norm_gain, norm_bias, cotangent):
@@ -389,9 +458,9 @@
             jnp.int32(total_cols),
         ]
     )
-    wide, narrow = with_surroundings(band_in.swapaxes(0, 1), cotangent.swapaxes(0, 1))
+    fields = with_surroundings(band_in.swapaxes(0, 1), cotangent.swapaxes(0, 1))
     gradient, grads = on_tile(
-        wide, narrow, place, conv_weight, mix_weight, norm_gain, norm_bias, rows, tile
+        fields, place, conv_weight, mix_weight, norm_gain, norm_bias, rows, tile
     )
     edge = TAPS * CH
     totals = summed_over_mesh(grads).reshape(2, CH, GRAD_COLS) * grad_scale

time: 130 us -> 112 us (0.86)
  Pallas kernels: 23.4 us -> 14.4 us
  waiting for transfers between devices: 21.6 us -> 16.7 us
  local copies, waits for them, and re-layouts: 9.23 us -> 7.37 us
  other arithmetic: 2.84 us -> 1.43 us
    pallas_call x1, Pallas kernels: 23.4 us -> 14.4 us  [on_tile(): pl.pallas_call(body, out_shape=(jax.ShapeDtypeStruct((rows, CH, tile), bf...]
    all_to_all x1, waiting for transfers between devices: 12 us -> 4.89 us  [exchanged(): lax.all_to_all(blocks, axis, 0, 0, tiled=True, axis_index_groups=groups)]
    ppermute x2, waiting for transfers between devices: 0.31 us -> 1.82 us  [gather_sides(): before = lax.ppermute(down, axis, [(i, i + 1) for i in range(devices - 1)])]
    unnamed x23 -> x11, local copies, waits for them, and re-layouts: 2.69 us -> 1.68 us
  transfers between devices with their start and end apart: 6 -> 6, of which waited for: 5 -> 6; matrix products, arithmetic and copies ran while one was open for 3% -> 2% of each run, Pallas kernels for 0% -> 0%
where the time goes in v4:
time: 112 us; the launch traced here: 111 us
  blocking collectives  41.9 us (37%)
  starting transfers between devices  28.4 us (25%)
  waiting for transfers between devices  16.7 us (15%)
  Pallas kernels  14.4 us (13%)
  local copies, waits for them, and re-layouts  7.37 us (7%)
  other arithmetic  1.43 us (1%)
    all_to_all x2, blocking collectives, exchanged(): lax.all_to_all(blocks, axis, 0, 0, tiled=True, axis_index_groups=groups)  41.9 us
    pallas_call x1, Pallas kernels, on_tile(): pl.pallas_call(body, out_shape=(jax.ShapeDtypeStruct((rows, CH, tile), bf...  14.4 us
    ppermute x2, starting transfers between devices, gather_sides(): after = lax.ppermute(up, axis, [(i + 1, i) for i in range(devices - 1)])  10.4 us
    ppermute x2, waiting for transfers between devices, gather_sides(): after = lax.ppermute(up, axis, [(i + 1, i) for i in range(devices - 1)])  6.79 us
    ppermute x1, starting transfers between devices, with_surroundings(): lax.ppermute(mine[:, :, ::-1], 'off', [(i, devices - 1 - i) for i in rang...  6.22 us
    ppermute x2, starting transfers between devices, gather_sides(): before = lax.ppermute(down, axis, [(i, i + 1) for i in range(devices - 1)])  5.88 us
    all_to_all x1, starting transfers between devices, exchanged(): lax.all_to_all(blocks, axis, 0, 0, tiled=True, axis_index_groups=groups)  5.88 us
    all_to_all x1, waiting for transfers between devices, exchanged(): lax.all_to_all(blocks, axis, 0, 0, tiled=True, axis_index_groups=groups)  4.89 us
  transfers between devices with their start and end apart: 6, of which 6 were waited for; matrix products, arithmetic and copies ran while one was open for 2% of the time, Pallas kernels for 0%

profile of v4, /device:TPU:1, one launch (start us, length us, event | category | flops | bytes accessed | tf_op | source)
XLA Modules:
  0.0 111.2 jit_solution(7742683290347003497)
XLA Ops:
  0.6 1.0 copy_bitcast_fusion
  1.9 6.2 %collective-permute-start = (bf16[16,64,128]{2,1,0:T(8,128)(2,1)S(1)}, bf16[16,64,128]{2,1,0:T(8,128)(2,1)S(1)}, u32[]{:S(2)}, u32[]{:S(2)}) collective-permute-start(bf16[16,64,128]{2,1,0:T(8,128)(2,1)S(1)} %rev.3), channel_id=1, source_target_pairs={{0,7},{1,6},{2,5},{3,4},{4,3},{5,2},{6,1},{7,0},{8,15},{9,14},{10,... | collective-permute-start | bytes 786440 | tf_op jit(solution)/shard_map/ppermute | solution.py:413
  8.7 3.2 %collective-permute-done = bf16[16,64,128]{2,1,0:T(8,128)(2,1)S(1)} collective-permute-done((bf16[16,64,128]{2,1,0:T(8,128)(2,1)S(1)}, bf16[16,64,128]{2,1,0:T(8,128)(2,1)S(1)}, u32[]{:S(2)}, u32[]{:S(2)}) %collective-permute-start) | collective-permute-done | bytes 262176 | tf_op jit(solution)/shard_map/ppermute | solution.py:413
  12.0 9.2 %collective-permute-start.2 = (bf16[18,64,128]{2,1,0:T(8,128)(2,1)S(1)}, bf16[18,64,128]{2,1,0:T(8,128)(2,1)S(1)}, u32[]{:S(2)}, u32[]{:S(2)}) collective-permute-start(bf16[18,64,128]{2,1,0:T(8,128)(2,1)S(1)} %fusion.21), channel_id=1, source_target_pairs={{8,0},{16,8},{24,16},{32,24},{40,32},{48,40},{56,48},{64,56},{72,6... | collective-permute-start | bytes 884744 | tf_op jit(solution)/shard_map/ppermute | solution.py:393
  21.2 1.9 %collective-permute-start.1 = (bf16[18,64,128]{2,1,0:T(8,128)(2,1)S(1)}, bf16[18,64,128]{2,1,0:T(8,128)(2,1)S(1)}, u32[]{:S(2)}, u32[]{:S(2)}) collective-permute-start(bf16[18,64,128]{2,1,0:T(8,128)(2,1)S(1)} %pad_maximum_fusion.3), channel_id=1, source_target_pairs={{0,8},{8,16},{16,24},{24,32},{32,40},{40,48},{48,56},{56,64},{64,7... | collective-permute-start | bytes 884744 | tf_op jit(solution)/shard_map/ppermute | solution.py:392
  24.3 2.9 %collective-permute-done.2 = bf16[18,64,128]{2,1,0:T(8,128)(2,1)S(1)} collective-permute-done((bf16[18,64,128]{2,1,0:T(8,128)(2,1)S(1)}, bf16[18,64,128]{2,1,0:T(8,128)(2,1)S(1)}, u32[]{:S(2)}, u32[]{:S(2)}) %collective-permute-start.2) | collective-permute-done | bytes 294944 | tf_op jit(solution)/shard_map/ppermute | solution.py:393
  27.4 0.3 collective-permute-done.1
  28.0 0.2 concatenate.112
  28.2 0.2 concatenate.115
  28.7 0.4 fusion.44
  29.2 4.0 %collective-permute-start.3 = (bf16[14,64,128]{2,1,0:T(8,128)(2,1)S(1)}, bf16[14,64,128]{2,1,0:T(8,128)(2,1)S(1)}, u32[]{:S(2)}, u32[]{:S(2)}) collective-permute-start(bf16[14,64,128]{2,1,0:T(8,128)(2,1)S(1)} %get-tuple-element.37), channel_id=1, source_target_pairs={{0,1},{1,2},{2,3},{3,4},{4,5},{5,6},{6,7},{8,9},{9,10},{10,11},{11... | collective-permute-start | bytes 688136 | tf_op jit(solution)/shard_map/ppermute | solution.py:392
  33.1 1.3 %collective-permute-start.4 = (bf16[14,64,128]{2,1,0:T(8,128)(2,1)S(1)}, bf16[14,64,128]{2,1,0:T(8,128)(2,1)S(1)}, u32[]{:S(2)}, u32[]{:S(2)}) collective-permute-start(bf16[14,64,128]{2,1,0:T(8,128)(2,1)S(1)} %get-tuple-element.36), channel_id=1, source_target_pairs={{1,0},{2,1},{3,2},{4,3},{5,4},{6,5},{7,6},{9,8},{10,9},{11,10},{12... | collective-permute-start | bytes 688136 | tf_op jit(solution)/shard_map/ppermute | solution.py:393
  34.6 1.5 %collective-permute-done.3.before = bf16[14,64,128]{2,1,0:T(8,128)(2,1)S(1)} collective-permute-done((bf16[14,64,128]{2,1,0:T(8,128)(2,1)S(1)}, bf16[14,64,128]{2,1,0:T(8,128)(2,1)S(1)}, u32[]{:S(2)}, u32[]{:S(2)}) %collective-permute-start.3) | collective-permute-done | bytes 229408 | tf_op jit(solution)/shard_map/ppermute | solution.py:392
  36.1 3.8 %collective-permute-done.4.after = bf16[14,64,128]{2,1,0:T(8,128)(2,1)S(1)} collective-permute-done((bf16[14,64,128]{2,1,0:T(8,128)(2,1)S(1)}, bf16[14,64,128]{2,1,0:T(8,128)(2,1)S(1)}, u32[]{:S(2)}, u32[]{:S(2)}) %collective-permute-start.4) | collective-permute-done | bytes 229408 | tf_op jit(solution)/shard_map/ppermute | solution.py:393
  40.1 14.4 %blocks_backward.1 = (bf16[16,32,128]{2,1,0:T(8,128)(2,1)S(1)}, f32[64,384]{1,0:T(8,128)S(1)}) custom-call(s32[4]{0:T(128)S(1)} %pad_add_fusion.place, bf16[40,64,128]{2,1,0:T(8,128)(2,1)S(1)} %pad_maximum_fusion.wide_tile, bf16[28,64,128]{2,1,0:T(8,128)(2,1)S(1)} %pad_maximum_fusion.1.narrow_tile, bf16[14,64,128]{2,1,0:T(8,128)(2,1)S(1)} %collective-permute-done.3.before, ...), custom_call_target="tpu_custom_call" | custom-call | tf_op jit(solution)/shard_map/blocks_backward/pallas_call | solution.py:358
  54.5 11.2 %all_to_all.15 = f32[16,4,384]{2,1,0:T(4,128)S(1)} all-to-all(f32[16,4,384]{2,1,0:T(4,128)S(1)} %reshape.52), channel_id=1, replica_groups={{0,1,2,3,4,5,6,7,8,9,10,11,12,13,14,15},{16,17,18,19,20,21,22,23,24,25,..., dimensions={0} | all-to-all | bytes 196608 | tf_op jit(solution)/shard_map/all_to_all | solution.py:437
  65.8 30.7 %all_to_all.16 = f32[32,4,384]{2,1,0:T(4,128)S(1)} all-to-all(f32[32,4,384]{2,1,0:T(4,128)S(1)} %broadcast_in_dim.10), channel_id=1, replica_groups={{0,16,32,48,64,80,96,112,128,144,160,176,192,208,224,240,256,272,288,30..., dimensions={0} | all-to-all | bytes 393216 | tf_op jit(solution)/shard_map/all_to_all | solution.py:437
  96.5 0.7 broadcast_in_dim.11
  97.2 5.9 %all-to-all-start.2 = ((f32[16,4,384]{2,1,0:T(4,128)}), f32[16,4,384]{2,1,0:T(4,128)S(1)}, u32[]{:S(2)}, u32[]{:S(2)}) async-start(f32[16,4,384]{2,1,0:T(4,128)} %broadcast_in_dim.11), calls=%async_computation.2 | async-start | bytes 196608 | tf_op jit(solution)/shard_map/all_to_all | solution.py:437
  103.1 0.7 copy.82
  103.8 4.9 %all-to-all-done.2 = f32[16,4,384]{2,1,0:T(4,128)S(1)} async-done(((f32[16,4,384]{2,1,0:T(4,128)}), f32[16,4,384]{2,1,0:T(4,128)S(1)}, u32[]{:S(2)}, u32[]{:S(2)}) %all-to-all-start.2) | async-done | bytes 98336 | tf_op jit(solution)/shard_map/all_to_all | solution.py:437
  108.7 0.7 slice.149
  109.4 0.7 slice_reduce_fusion
  110.3 0.9 copy.83
  (60 shorter events, 3.2 us)
Async XLA Ops:
  1.7 6.5 %copy-start = (bf16[2,9,32,32]{3,2,1,0:T(8,128)(2,1)S(1)}, bf16[2,9,32,32]{3,2,1,0:T(8,128)(2,1)}, u32[]{:S(2)}) copy-start(bf16[2,9,32,32]{3,2,1,0:T(8,128)(2,1)} %param.7) | copy-start | bytes 110596
  1.9 6.4 %copy-start.1 = (bf16[2,32,32]{2,1,0:T(8,128)(2,1)S(1)}, bf16[2,32,32]{2,1,0:T(8,128)(2,1)}, u32[]{:S(2)}) copy-start(bf16[2,32,32]{2,1,0:T(8,128)(2,1)} %param.8) | copy-start | bytes 12292
  1.9 10.0 %collective-permute-start = (bf16[16,64,128]{2,1,0:T(8,128)(2,1)S(1)}, bf16[16,64,128]{2,1,0:T(8,128)(2,1)S(1)}, u32[]{:S(2)}, u32[]{:S(2)}) collective-permute-start(bf16[16,64,128]{2,1,0:T(8,128)(2,1)S(1)} %rev.3), channel_id=1, source_target_pairs={{0,7},{1,6},{2,5},{3,4},{4,3},{5,2},{6,1},{7,0},{8,15},{9,14},{10,... | collective-permute-start | bytes 786440 | tf_op jit(solution)/shard_map/ppermute | solution.py:413
  12.0 15.2 %collective-permute-start.2 = (bf16[18,64,128]{2,1,0:T(8,128)(2,1)S(1)}, bf16[18,64,128]{2,1,0:T(8,128)(2,1)S(1)}, u32[]{:S(2)}, u32[]{:S(2)}) collective-permute-start(bf16[18,64,128]{2,1,0:T(8,128)(2,1)S(1)} %fusion.21), channel_id=1, source_target_pairs={{8,0},{16,8},{24,16},{32,24},{40,32},{48,40},{56,48},{64,56},{72,6... | collective-permute-start | bytes 884744 | tf_op jit(solution)/shard_map/ppermute | solution.py:393
  21.2 6.5 %collective-permute-start.1 = (bf16[18,64,128]{2,1,0:T(8,128)(2,1)S(1)}, bf16[18,64,128]{2,1,0:T(8,128)(2,1)S(1)}, u32[]{:S(2)}, u32[]{:S(2)}) collective-permute-start(bf16[18,64,128]{2,1,0:T(8,128)(2,1)S(1)} %pad_maximum_fusion.3), channel_id=1, source_target_pairs={{0,8},{8,16},{16,24},{24,32},{32,40},{40,48},{48,56},{56,64},{64,7... | collective-permute-start | bytes 884744 | tf_op jit(solution)/shard_map/ppermute | solution.py:392
  23.2 0.8 copy-start.2
  23.2 0.9 copy-start.3
  29.2 6.9 %collective-permute-start.3 = (bf16[14,64,128]{2,1,0:T(8,128)(2,1)S(1)}, bf16[14,64,128]{2,1,0:T(8,128)(2,1)S(1)}, u32[]{:S(2)}, u32[]{:S(2)}) collective-permute-start(bf16[14,64,128]{2,1,0:T(8,128)(2,1)S(1)} %get-tuple-element.37), channel_id=1, source_target_pairs={{0,1},{1,2},{2,3},{3,4},{4,5},{5,6},{6,7},{8,9},{9,10},{10,11},{11... | collective-permute-start | bytes 688136 | tf_op jit(solution)/shard_map/ppermute | solution.py:392
  33.1 6.8 %collective-permute-start.4 = (bf16[14,64,128]{2,1,0:T(8,128)(2,1)S(1)}, bf16[14,64,128]{2,1,0:T(8,128)(2,1)S(1)}, u32[]{:S(2)}, u32[]{:S(2)}) collective-permute-start(bf16[14,64,128]{2,1,0:T(8,128)(2,1)S(1)} %get-tuple-element.36), channel_id=1, source_target_pairs={{1,0},{2,1},{3,2},{4,3},{5,4},{6,5},{7,6},{9,8},{10,9},{11,10},{12... | collective-permute-start | bytes 688136 | tf_op jit(solution)/shard_map/ppermute | solution.py:393
  97.2 11.5 %all-to-all-start.2 = ((f32[16,4,384]{2,1,0:T(4,128)}), f32[16,4,384]{2,1,0:T(4,128)S(1)}, u32[]{:S(2)}, u32[]{:S(2)}) async-start(f32[16,4,384]{2,1,0:T(4,128)} %broadcast_in_dim.11), calls=%async_computation.2 | async-start | bytes 196608 | tf_op jit(solution)/shard_map/all_to_all | solution.py:437

commit v5 on v4

--- a/solution.py
+++ b/solution.py
@@ -1,3 +1,4 @@
+import functools
 import math
 
 import jax
@@ -389,9 +390,14 @@
 
 def gather_sides(axis, down, up):
     devices = lax.axis_size(axis)
-    before = lax.ppermute(down, axis, [(i, i + 1) for i in range(devices - 1)])
-    after = lax.ppermute(up, axis, [(i + 1, i) for i in range(devices - 1)])
-    return before, after
+    odd = lax.axis_index(axis) % 2 == 1
+    routes = []
+    for start in (0, 1):
+        pairs = [(i, i + 1) for i in range(start, devices - 1, 2)]
+        routes.append(pairs + [(j, i) for i, j in pairs])
+    within = lax.ppermute(jnp.where(odd, up, down), axis, routes[0])
+    across = lax.ppermute(jnp.where(odd, down, up), axis, routes[1])
+    return jnp.where(odd, within, across), jnp.where(odd, across, within)
 
 
 def packed(wide, narrow, last):
@@ -426,6 +432,40 @@
     return wide, narrow, before, after
 
 
+def unpack(scale, blocks, conv, mix, gain, bias, grads):
+    edge = TAPS * CH
+    count, height = blocks.shape[:2]
+    for k in range(count):
+        grads[k * height : (k + 1) * height] = blocks[k]
+    for s in range(2):
+        part = slice(s * CH, (s + 1) * CH)
+        for tap in range(TAPS):
+            conv[s, tap] = grads[part, tap * CH : (tap + 1) * CH] * scale
+        mix[s] = grads[part, edge : edge + CH] * scale
+        rest = (grads[part, 2 * 128 : 3 * 128] * scale).T
+        start = edge + CH - 2 * 128
+        gain[s : s + 1] = rest[start : start + 1]
+        bias[s : s + 1] = rest[start + 1 : start + 2]
+
+
+def unpacked(blocks, scale):
+    f32 = jnp.float32
+    vmem = pl.BlockSpec(memory_space=pltpu.VMEM)
+    return pl.pallas_call(
+        functools.partial(unpack, scale),
+        out_shape=(
+            jax.ShapeDtypeStruct((2, TAPS, CH, CH), f32),
+            jax.ShapeDtypeStruct((2, CH, CH), f32),
+            jax.ShapeDtypeStruct((2, CH), f32),
+            jax.ShapeDtypeStruct((2, CH), f32),
+        ),
+        in_specs=[vmem],
+        out_specs=(vmem,) * 4,
+        scratch_shapes=[pltpu.VMEM((2 * CH, GRAD_COLS), f32)],
+        name="unpack_gradients",
+    )(blocks)
+
+
 def summed_over_mesh(parts):
     rows, columns = (lax.axis_size("pos"), lax.axis_size("off"))
     size = 2 * columns
@@ -441,8 +481,9 @@
 
     blocks = parts.reshape(size, -1, parts.shape[1])
     part = jnp.sum(exchanged(blocks, axes, near), axis=0)
-    part = jnp.sum(exchanged(copies(part, rows // 2), "pos", far), axis=0)
-    return exchanged(copies(part, size), axes, near).reshape(parts.shape)
+    part = exchanged(copies(part.astype(jnp.bfloat16), rows // 2), "pos", far)
+    part = jnp.sum(part.astype(jnp.float32), axis=0)
+    return exchanged(copies(part, size), axes, near)
 
 
 def local(band_in, conv_weight, mix_weight, norm_gain, norm_bias, cotangent):
@@ -462,16 +503,7 @@
     gradient, grads = on_tile(
         fields, place, conv_weight, mix_weight, norm_gain, norm_bias, rows, tile
     )
-    edge = TAPS * CH
-    totals = summed_over_mesh(grads).reshape(2, CH, GRAD_COLS) * grad_scale
-    conv_total = totals[:, :, :edge].reshape(2, CH, TAPS, CH).swapaxes(1, 2)
-    return (
-        gradient.swapaxes(0, 1),
-        conv_total,
-        totals[:, :, edge : edge + CH],
-        totals[:, :, edge + CH],
-        totals[:, :, edge + CH + 1],
-    )
+    return (gradient.swapaxes(0, 1), *unpacked(summed_over_mesh(grads), grad_scale))
 
 
 def solution(mesh):

time: 112 us -> 113 us (level)
  starting transfers between devices: 28.4 us -> 25.5 us
  blocking collectives: 41.9 us -> 44.2 us
  waiting for transfers between devices: 16.7 us -> 18.8 us
  local copies, waits for them, and re-layouts: 7.37 us -> 5.54 us
  Pallas kernels: 14.4 us -> 16.2 us
    ppermute x4, waiting for transfers between devices: 8.61 us -> 11.8 us  [the longest x2 7.73 us: gather_sides(): across = lax.ppermute(jnp.where(odd, down, up), axis, routes[1])]
    ppermute x4, starting transfers between devices: 16.3 us -> 13.7 us  [the longest x2 11.1 us: gather_sides(): within = lax.ppermute(jnp.where(odd, up, down), axis, routes[0])]
    all_to_all x2, blocking collectives: 41.9 us -> 44.2 us  [exchanged(): lax.all_to_all(blocks, axis, 0, 0, tiled=True, axis_index_groups=groups)]
    pallas_call x0 -> x1, Pallas kernels: none -> 1.78 us  [unpacked(): pl.pallas_call(functools.partial(unpack, scale), out_shape=(jax.ShapeDtyp...]
    slice x4 -> x1, local copies, waits for them, and re-layouts: 1.58 us -> 0.02 us  [with_surroundings(): wide = jnp.concatenate([band, other[:, :CH]], axis=1)]
  transfers between devices with their start and end apart: 6 -> 6, of which waited for: 6 -> 4; matrix products, arithmetic and copies ran while one was open for 2% -> 2% of each run, Pallas kernels for 0% -> 0%
where the time goes in v5:
time: 113 us
  blocking collectives  44.2 us (39%)
  starting transfers between devices  25.5 us (23%)
  waiting for transfers between devices  18.8 us (17%)
  Pallas kernels  16.2 us (14%)
  local copies, waits for them, and re-layouts  5.54 us (5%)
  other arithmetic  1.6 us (1%)
    all_to_all x2, blocking collectives, exchanged(): lax.all_to_all(blocks, axis, 0, 0, tiled=True, axis_index_groups=groups)  44.2 us
    pallas_call x1, Pallas kernels, on_tile(): pl.pallas_call(body, out_shape=(jax.ShapeDtypeStruct((rows, CH, tile), bf...  14.4 us
    ppermute x2, starting transfers between devices, gather_sides(): within = lax.ppermute(jnp.where(odd, up, down), axis, routes[0])  11.1 us
    ppermute x2, waiting for transfers between devices, gather_sides(): across = lax.ppermute(jnp.where(odd, down, up), axis, routes[1])  7.73 us
    ppermute x1, starting transfers between devices, with_surroundings(): lax.ppermute(mine[:, :, ::-1], 'off', [(i, devices - 1 - i) for i in rang...  6.22 us
    all_to_all x1, starting transfers between devices, exchanged(): lax.all_to_all(blocks, axis, 0, 0, tiled=True, axis_index_groups=groups)  5.64 us
    all_to_all x1, waiting for transfers between devices, exchanged(): lax.all_to_all(blocks, axis, 0, 0, tiled=True, axis_index_groups=groups)  4.89 us
    ppermute x2, waiting for transfers between devices, gather_sides(): within = lax.ppermute(jnp.where(odd, up, down), axis, routes[0])  4.03 us
  transfers between devices with their start and end apart: 6, of which 4 were waited for; matrix products, arithmetic and copies ran while one was open for 2% of the time, Pallas kernels for 0%

profile of v5, /device:TPU:1, one launch (start us, length us, event | category | flops | bytes accessed | tf_op | source)
XLA Modules:
  0.0 112.9 jit_solution(17096946945706214293)
XLA Ops:
  0.6 1.0 copy_bitcast_fusion
  1.7 0.2 rev.3
  1.9 6.2 %collective-permute-start = (bf16[16,64,128]{2,1,0:T(8,128)(2,1)S(1)}, bf16[16,64,128]{2,1,0:T(8,128)(2,1)S(1)}, u32[]{:S(2)}, u32[]{:S(2)}) collective-permute-start(bf16[16,64,128]{2,1,0:T(8,128)(2,1)S(1)} %rev.3), channel_id=1, source_target_pairs={{0,7},{1,6},{2,5},{3,4},{4,3},{5,2},{6,1},{7,0},{8,15},{9,14},{10,... | collective-permute-start | bytes 786440 | tf_op jit(solution)/shard_map/ppermute | solution.py:419
  8.9 0.2 copy.67
  9.7 2.2 %collective-permute-done = bf16[16,64,128]{2,1,0:T(8,128)(2,1)S(1)} collective-permute-done((bf16[16,64,128]{2,1,0:T(8,128)(2,1)S(1)}, bf16[16,64,128]{2,1,0:T(8,128)(2,1)S(1)}, u32[]{:S(2)}, u32[]{:S(2)}) %collective-permute-start) | collective-permute-done | bytes 262176 | tf_op jit(solution)/shard_map/ppermute | solution.py:419
  11.9 0.2 broadcast_select_fusion.3
  12.1 9.2 %collective-permute-start.1 = (bf16[18,64,128]{2,1,0:T(8,128)(2,1)S(1)}, bf16[18,64,128]{2,1,0:T(8,128)(2,1)S(1)}, u32[]{:S(2)}, u32[]{:S(2)}) collective-permute-start(bf16[18,64,128]{2,1,0:T(8,128)(2,1)S(1)} %get-tuple-element.45), channel_id=1, source_target_pairs={{0,8},{16,24},{32,40},{48,56},{64,72},{80,88},{96,104},{112,120},{... | collective-permute-start | bytes 884744 | tf_op jit(solution)/shard_map/ppermute | solution.py:398
  21.3 1.9 %collective-permute-start.2 = (bf16[18,64,128]{2,1,0:T(8,128)(2,1)S(1)}, bf16[18,64,128]{2,1,0:T(8,128)(2,1)S(1)}, u32[]{:S(2)}, u32[]{:S(2)}) collective-permute-start(bf16[18,64,128]{2,1,0:T(8,128)(2,1)S(1)} %get-tuple-element.46), channel_id=1, source_target_pairs={{8,16},{24,32},{40,48},{56,64},{72,80},{88,96},{104,112},{120,128}... | collective-permute-start | bytes 884744 | tf_op jit(solution)/shard_map/ppermute | solution.py:399
  23.4 7.7 %collective-permute-done.2 = bf16[18,64,128]{2,1,0:T(8,128)(2,1)S(1)} collective-permute-done((bf16[18,64,128]{2,1,0:T(8,128)(2,1)S(1)}, bf16[18,64,128]{2,1,0:T(8,128)(2,1)S(1)}, u32[]{:S(2)}, u32[]{:S(2)}) %collective-permute-start.2) | collective-permute-done | bytes 294944 | tf_op jit(solution)/shard_map/ppermute | solution.py:399
  31.9 0.2 concatenate.112
  32.1 0.2 concatenate.115
  32.4 0.5 broadcast_select_fusion.6
  32.9 1.9 %collective-permute-start.3 = (bf16[14,64,128]{2,1,0:T(8,128)(2,1)S(1)}, bf16[14,64,128]{2,1,0:T(8,128)(2,1)S(1)}, u32[]{:S(2)}, u32[]{:S(2)}) collective-permute-start(bf16[14,64,128]{2,1,0:T(8,128)(2,1)S(1)} %broadcast_select_fusion.7), channel_id=1, source_target_pairs={{0,1},{2,3},{4,5},{6,7},{1,0},{3,2},{5,4},{7,6},{8,9},{10,11},{12,... | collective-permute-start | bytes 688136 | tf_op jit(solution)/shard_map/ppermute | solution.py:398
  34.8 0.7 collective-permute-start.4
  35.6 4.0 %collective-permute-done.3 = bf16[14,64,128]{2,1,0:T(8,128)(2,1)S(1)} collective-permute-done((bf16[14,64,128]{2,1,0:T(8,128)(2,1)S(1)}, bf16[14,64,128]{2,1,0:T(8,128)(2,1)S(1)}, u32[]{:S(2)}, u32[]{:S(2)}) %collective-permute-start.3) | collective-permute-done | bytes 229408 | tf_op jit(solution)/shard_map/ppermute | solution.py:398
  39.9 14.4 %blocks_backward.1 = (bf16[16,32,128]{2,1,0:T(8,128)(2,1)S(1)}, f32[64,384]{1,0:T(8,128)S(1)}) custom-call(s32[4]{0:T(128)S(1)} %pad_add_fusion.place, bf16[40,64,128]{2,1,0:T(8,128)(2,1)S(1)} %pad_maximum_fusion.wide_tile, bf16[28,64,128]{2,1,0:T(8,128)(2,1)S(1)} %pad_maximum_fusion.1.narrow_tile, bf16[14,64,128]{2,1,0:T(8,128)(2,1)S(1)} %get-tuple-element.50.before, ...), custom_call_target="tpu_custom_call" | custom-call | tf_op jit(solution)/shard_map/blocks_backward/pallas_call | solution.py:359
  54.3 11.4 %all_to_all.15 = f32[16,4,384]{2,1,0:T(4,128)S(1)} all-to-all(f32[16,4,384]{2,1,0:T(4,128)S(1)} %reshape.49), channel_id=1, replica_groups={{0,1,2,3,4,5,6,7,8,9,10,11,12,13,14,15},{16,17,18,19,20,21,22,23,24,25,..., dimensions={0} | all-to-all | bytes 196608 | tf_op jit(solution)/shard_map/all_to_all | solution.py:477
  65.7 32.8 %all_to_all.16 = bf16[32,4,384]{2,1,0:T(4,128)(2,1)S(1)} all-to-all(bf16[32,4,384]{2,1,0:T(4,128)(2,1)S(1)} %broadcast_in_dim.10), channel_id=1, replica_groups={{0,16,32,48,64,80,96,112,128,144,160,176,192,208,224,240,256,272,288,30..., dimensions={0} | all-to-all | bytes 196608 | tf_op jit(solution)/shard_map/all_to_all | solution.py:477
  98.6 0.7 broadcast_in_dim.11
  99.2 5.6 %all-to-all-start.2 = ((f32[16,4,384]{2,1,0:T(4,128)}), f32[16,4,384]{2,1,0:T(4,128)S(1)}, u32[]{:S(2)}, u32[]{:S(2)}) async-start(f32[16,4,384]{2,1,0:T(4,128)} %broadcast_in_dim.11), calls=%async_computation.2 | async-start | bytes 196608 | tf_op jit(solution)/shard_map/all_to_all | solution.py:477
  104.9 0.7 copy.75
  105.6 4.9 %all-to-all-done.2.blocks = f32[16,4,384]{2,1,0:T(4,128)S(1)} async-done(((f32[16,4,384]{2,1,0:T(4,128)}), f32[16,4,384]{2,1,0:T(4,128)S(1)}, u32[]{:S(2)}, u32[]{:S(2)}) %all-to-all-start.2) | async-done | bytes 98336 | tf_op jit(solution)/shard_map/all_to_all | solution.py:477
  110.5 0.6 copy-done.1
  111.1 1.8 %unpack_gradients.1 = (f32[2,9,32,32]{3,2,1,0:T(8,128)}, f32[2,32,32]{2,1,0:T(8,128)}, f32[2,32]{1,0:T(2,128)}, f32[2,32]{1,0:T(2,128)}) custom-call(f32[16,4,384]{2,1,0:T(4,128)} %copy-done.1), custom_call_target="tpu_custom_call" | custom-call | tf_op jit(solution)/shard_map/unpack_gradients/pallas_call | solution.py:454
  (59 shorter events, 2.7 us)
Async XLA Ops:
  1.7 6.4 %copy-start = (bf16[2,9,32,32]{3,2,1,0:T(8,128)(2,1)S(1)}, bf16[2,9,32,32]{3,2,1,0:T(8,128)(2,1)}, u32[]{:S(2)}) copy-start(bf16[2,9,32,32]{3,2,1,0:T(8,128)(2,1)} %param.7) | copy-start | bytes 110596
  1.9 10.0 %collective-permute-start = (bf16[16,64,128]{2,1,0:T(8,128)(2,1)S(1)}, bf16[16,64,128]{2,1,0:T(8,128)(2,1)S(1)}, u32[]{:S(2)}, u32[]{:S(2)}) collective-permute-start(bf16[16,64,128]{2,1,0:T(8,128)(2,1)S(1)} %rev.3), channel_id=1, source_target_pairs={{0,7},{1,6},{2,5},{3,4},{4,3},{5,2},{6,1},{7,0},{8,15},{9,14},{10,... | collective-permute-start | bytes 786440 | tf_op jit(solution)/shard_map/ppermute | solution.py:419
  8.5 0.9 copy-start.2
  8.5 1.0 copy-start.3
  8.5 1.0 copy-start.4
  12.1 11.3 %collective-permute-start.1 = (bf16[18,64,128]{2,1,0:T(8,128)(2,1)S(1)}, bf16[18,64,128]{2,1,0:T(8,128)(2,1)S(1)}, u32[]{:S(2)}, u32[]{:S(2)}) collective-permute-start(bf16[18,64,128]{2,1,0:T(8,128)(2,1)S(1)} %get-tuple-element.45), channel_id=1, source_target_pairs={{0,8},{16,24},{32,40},{48,56},{64,72},{80,88},{96,104},{112,120},{... | collective-permute-start | bytes 884744 | tf_op jit(solution)/shard_map/ppermute | solution.py:398
  21.3 9.9 %collective-permute-start.2 = (bf16[18,64,128]{2,1,0:T(8,128)(2,1)S(1)}, bf16[18,64,128]{2,1,0:T(8,128)(2,1)S(1)}, u32[]{:S(2)}, u32[]{:S(2)}) collective-permute-start(bf16[18,64,128]{2,1,0:T(8,128)(2,1)S(1)} %get-tuple-element.46), channel_id=1, source_target_pairs={{8,16},{24,32},{40,48},{56,64},{72,80},{88,96},{104,112},{120,128}... | collective-permute-start | bytes 884744 | tf_op jit(solution)/shard_map/ppermute | solution.py:399
  32.9 6.8 %collective-permute-start.3 = (bf16[14,64,128]{2,1,0:T(8,128)(2,1)S(1)}, bf16[14,64,128]{2,1,0:T(8,128)(2,1)S(1)}, u32[]{:S(2)}, u32[]{:S(2)}) collective-permute-start(bf16[14,64,128]{2,1,0:T(8,128)(2,1)S(1)} %broadcast_select_fusion.7), channel_id=1, source_target_pairs={{0,1},{2,3},{4,5},{6,7},{1,0},{3,2},{5,4},{7,6},{8,9},{10,11},{12,... | collective-permute-start | bytes 688136 | tf_op jit(solution)/shard_map/ppermute | solution.py:398
  34.8 4.8 %collective-permute-start.4 = (bf16[14,64,128]{2,1,0:T(8,128)(2,1)S(1)}, bf16[14,64,128]{2,1,0:T(8,128)(2,1)S(1)}, u32[]{:S(2)}, u32[]{:S(2)}) collective-permute-start(bf16[14,64,128]{2,1,0:T(8,128)(2,1)S(1)} %get-tuple-element.42), channel_id=1, source_target_pairs={{1,2},{3,4},{5,6},{2,1},{4,3},{6,5},{9,10},{11,12},{13,14},{10,9},... | collective-permute-start | bytes 688136 | tf_op jit(solution)/shard_map/ppermute | solution.py:399
  99.2 11.2 %all-to-all-start.2 = ((f32[16,4,384]{2,1,0:T(4,128)}), f32[16,4,384]{2,1,0:T(4,128)S(1)}, u32[]{:S(2)}, u32[]{:S(2)}) async-start(f32[16,4,384]{2,1,0:T(4,128)} %broadcast_in_dim.11), calls=%async_computation.2 | async-start | bytes 196608 | tf_op jit(solution)/shard_map/all_to_all | solution.py:477
  110.5 0.6 copy-start.1

commit v6 on v5

--- a/solution.py
+++ b/solution.py
@@ -14,12 +14,12 @@
 TAPS = 9
 WIDE_ROWS = 2 * (FIRST_DILATION + SECOND_DILATION)
 NARROW_ROWS = FIRST_DILATION + SECOND_DILATION
-WIDE_COLS = 32
+WIDE_COLS = 25
 NARROW_COLS = 16
 LANES = 256
 GRAD_COLS = 384
-ACT_ROWS = 8
-FIRST_ROWS = 12
+ACT_ROWS = 10
+FIRST_ROWS = 18
 SECOND_ROWS = 14
 BETWEEN_ROWS = 10
 
@@ -303,7 +303,7 @@
     tile_zero = jnp.zeros((CH, tile), f32)
     start = (taps_zero,) * 2 + (small_zero,) * 2 + (tile_zero,) * 4
     conv0, conv1, mix0, mix1, gain0, bias0, gain1, bias1 = lax.fori_loop(
-        0, rows // 2, finish, start, unroll=2
+        0, rows // 2, finish, start, unroll=4
     )
     edge = TAPS * CH
     for s, parts in enumerate(((conv0, mix0, gain0, bias0), (conv1, mix1, gain1, bias1))):
@@ -395,8 +395,8 @@
     for start in (0, 1):
         pairs = [(i, i + 1) for i in range(start, devices - 1, 2)]
         routes.append(pairs + [(j, i) for i, j in pairs])
+    across = lax.ppermute(jnp.where(odd, down, up), axis, routes[1])
     within = lax.ppermute(jnp.where(odd, up, down), axis, routes[0])
-    across = lax.ppermute(jnp.where(odd, down, up), axis, routes[1])
     return jnp.where(odd, within, across), jnp.where(odd, across, within)
 
 
@@ -406,9 +406,10 @@
         edge = rows[:, :, -cols:] if last else rows[:, :, :cols]
         edge = jnp.concatenate([edge, edge[: -rows.shape[0] % slots]], axis=0)
         pieces = jnp.split(edge, slots, axis=0)
+        gap = jnp.zeros(pieces[0].shape[:2] + (128 - slots * cols,), edge.dtype)
         if last:
-            pieces = pieces[1:] + pieces[:1]
-        return jnp.concatenate(pieces, axis=2)
+            return jnp.concatenate(pieces[1:] + [gap] + pieces[:1], axis=2)
+        return jnp.concatenate(pieces + [gap], axis=2)
 
     return jnp.concatenate([in_slots(wide, WIDE_COLS), in_slots(narrow, NARROW_COLS)], axis=0)
 

time: 113 us -> 114 us (level)
  local copies, waits for them, and re-layouts: 5.54 us -> 7.99 us
  blocking collectives: 44.2 us -> 42.8 us
    all_to_all x2, blocking collectives: 44.2 us -> 42.8 us  [exchanged(): lax.all_to_all(blocks, axis, 0, 0, tiled=True, axis_index_groups=groups)]
    split x2 -> x3, other arithmetic: 0.23 us -> 1.59 us  [in_slots(): pieces = jnp.split(edge, slots, axis=0)]
  transfers between devices with their start and end apart: 6 -> 6, of which waited for: 4 -> 4; matrix products, arithmetic and copies ran while one was open for 2% -> 3% of each run, Pallas kernels for 0% -> 0%
where the time goes in v6:
time: 114 us; the launch traced here: 113 us
  blocking collectives  42.8 us (38%)
  starting transfers between devices  25.5 us (22%)
  waiting for transfers between devices  17.8 us (16%)
  Pallas kernels  15.8 us (14%)
  local copies, waits for them, and re-layouts  7.99 us (7%)
  other arithmetic  2.45 us (2%)
    all_to_all x2, blocking collectives, exchanged(): lax.all_to_all(blocks, axis, 0, 0, tiled=True, axis_index_groups=groups)  42.8 us
    pallas_call x1, Pallas kernels, on_tile(): pl.pallas_call(body, out_shape=(jax.ShapeDtypeStruct((rows, CH, tile), bf...  14.1 us
    ppermute x2, starting transfers between devices, gather_sides(): within = lax.ppermute(jnp.where(odd, up, down), axis, routes[0])  11.1 us
    ppermute x2, waiting for transfers between devices, gather_sides(): across = lax.ppermute(jnp.where(odd, down, up), axis, routes[1])  7.63 us
    ppermute x1, starting transfers between devices, with_surroundings(): lax.ppermute(mine[:, :, ::-1], 'off', [(i, devices - 1 - i) for i in rang...  6.22 us
    all_to_all x1, starting transfers between devices, exchanged(): lax.all_to_all(blocks, axis, 0, 0, tiled=True, axis_index_groups=groups)  5.64 us
    all_to_all x1, waiting for transfers between devices, exchanged(): lax.all_to_all(blocks, axis, 0, 0, tiled=True, axis_index_groups=groups)  4.89 us
    ppermute x2, waiting for transfers between devices, gather_sides(): within = lax.ppermute(jnp.where(odd, up, down), axis, routes[0])  3.68 us
  transfers between devices with their start and end apart: 6, of which 4 were waited for; matrix products, arithmetic and copies ran while one was open for 3% of the time, Pallas kernels for 0%

profile of v6, /device:TPU:1, one launch (start us, length us, event | category | flops | bytes accessed | tf_op | source)
XLA Modules:
  0.0 113.5 jit_solution(15344155783221124272)
XLA Ops:
  0.6 1.0 copy_bitcast_fusion
  1.9 6.2 %collective-permute-start = (bf16[16,64,128]{2,1,0:T(8,128)(2,1)S(1)}, bf16[16,64,128]{2,1,0:T(8,128)(2,1)S(1)}, u32[]{:S(2)}, u32[]{:S(2)}) collective-permute-start(bf16[16,64,128]{2,1,0:T(8,128)(2,1)S(1)} %rev.3), channel_id=1, source_target_pairs={{0,7},{1,6},{2,5},{3,4},{4,3},{5,2},{6,1},{7,0},{8,15},{9,14},{10,... | collective-permute-start | bytes 786440 | tf_op jit(solution)/shard_map/ppermute | solution.py:420
  9.6 0.6 tile.19
  10.2 1.6 %collective-permute-done = bf16[16,64,128]{2,1,0:T(8,128)(2,1)S(1)} collective-permute-done((bf16[16,64,128]{2,1,0:T(8,128)(2,1)S(1)}, bf16[16,64,128]{2,1,0:T(8,128)(2,1)S(1)}, u32[]{:S(2)}, u32[]{:S(2)}) %collective-permute-start) | collective-permute-done | bytes 262176 | tf_op jit(solution)/shard_map/ppermute | solution.py:420
  12.0 9.2 %collective-permute-start.1 = (bf16[18,64,128]{2,1,0:T(8,128)(2,1)S(1)}, bf16[18,64,128]{2,1,0:T(8,128)(2,1)S(1)}, u32[]{:S(2)}, u32[]{:S(2)}) collective-permute-start(bf16[18,64,128]{2,1,0:T(8,128)(2,1)S(1)} %get-tuple-element.44), channel_id=1, source_target_pairs={{0,8},{16,24},{32,40},{48,56},{64,72},{80,88},{96,104},{112,120},{... | collective-permute-start | bytes 884744 | tf_op jit(solution)/shard_map/ppermute | solution.py:399
  21.2 1.9 %collective-permute-start.2 = (bf16[18,64,128]{2,1,0:T(8,128)(2,1)S(1)}, bf16[18,64,128]{2,1,0:T(8,128)(2,1)S(1)}, u32[]{:S(2)}, u32[]{:S(2)}) collective-permute-start(bf16[18,64,128]{2,1,0:T(8,128)(2,1)S(1)} %get-tuple-element.45), channel_id=1, source_target_pairs={{8,16},{24,32},{40,48},{56,64},{72,80},{88,96},{104,112},{120,128}... | collective-permute-start | bytes 884744 | tf_op jit(solution)/shard_map/ppermute | solution.py:398
  23.4 7.6 %collective-permute-done.2 = bf16[18,64,128]{2,1,0:T(8,128)(2,1)S(1)} collective-permute-done((bf16[18,64,128]{2,1,0:T(8,128)(2,1)S(1)}, bf16[18,64,128]{2,1,0:T(8,128)(2,1)S(1)}, u32[]{:S(2)}, u32[]{:S(2)}) %collective-permute-start.2) | collective-permute-done | bytes 294944 | tf_op jit(solution)/shard_map/ppermute | solution.py:398
  31.3 0.7 fusion.29
  32.1 0.7 pad_maximum_fusion.20
  32.9 0.7 pad_maximum_fusion.21
  33.8 0.3 concatenate.109
  34.5 0.5 copy-done.2
  35.6 1.9 %collective-permute-start.3 = (bf16[12,64,128]{2,1,0:T(8,128)(2,1)S(1)}, bf16[12,64,128]{2,1,0:T(8,128)(2,1)S(1)}, u32[]{:S(2)}, u32[]{:S(2)}) collective-permute-start(bf16[12,64,128]{2,1,0:T(8,128)(2,1)S(1)} %get-tuple-element.53), channel_id=1, source_target_pairs={{0,1},{2,3},{4,5},{6,7},{1,0},{3,2},{5,4},{7,6},{8,9},{10,11},{12,... | collective-permute-start | bytes 589832 | tf_op jit(solution)/shard_map/ppermute | solution.py:399
  37.5 0.7 collective-permute-start.4
  38.3 3.7 %collective-permute-done.3 = bf16[12,64,128]{2,1,0:T(8,128)(2,1)S(1)} collective-permute-done((bf16[12,64,128]{2,1,0:T(8,128)(2,1)S(1)}, bf16[12,64,128]{2,1,0:T(8,128)(2,1)S(1)}, u32[]{:S(2)}, u32[]{:S(2)}) %collective-permute-start.3) | collective-permute-done | bytes 196640 | tf_op jit(solution)/shard_map/ppermute | solution.py:399
  42.2 14.1 %blocks_backward.1 = (bf16[16,32,128]{2,1,0:T(8,128)(2,1)S(1)}, f32[64,384]{1,0:T(8,128)S(1)}) custom-call(s32[4]{0:T(128)S(1)} %pad_add_fusion.place, bf16[40,64,128]{2,1,0:T(8,128)(2,1)S(1)} %pad_maximum_fusion.wide_tile, bf16[28,64,128]{2,1,0:T(8,128)(2,1)S(1)} %pad_maximum_fusion.1.narrow_tile, bf16[12,64,128]{2,1,0:T(8,128)(2,1)S(1)} %get-tuple-element.51.before, ...), custom_call_target="tpu_custom_call" | custom-call | tf_op jit(solution)/shard_map/blocks_backward/pallas_call | solution.py:359
  56.3 11.4 %all_to_all.15 = f32[16,4,384]{2,1,0:T(4,128)S(1)} all-to-all(f32[16,4,384]{2,1,0:T(4,128)S(1)} %reshape.49), channel_id=1, replica_groups={{0,1,2,3,4,5,6,7,8,9,10,11,12,13,14,15},{16,17,18,19,20,21,22,23,24,25,..., dimensions={0} | all-to-all | bytes 196608 | tf_op jit(solution)/shard_map/all_to_all | solution.py:478
  67.7 31.4 %all_to_all.16 = bf16[32,4,384]{2,1,0:T(4,128)(2,1)S(1)} all-to-all(bf16[32,4,384]{2,1,0:T(4,128)(2,1)S(1)} %broadcast_in_dim.10), channel_id=1, replica_groups={{0,16,32,48,64,80,96,112,128,144,160,176,192,208,224,240,256,272,288,30..., dimensions={0} | all-to-all | bytes 196608 | tf_op jit(solution)/shard_map/all_to_all | solution.py:478
  99.2 0.7 broadcast_in_dim.11
  99.8 5.6 %all-to-all-start.2 = ((f32[16,4,384]{2,1,0:T(4,128)}), f32[16,4,384]{2,1,0:T(4,128)S(1)}, u32[]{:S(2)}, u32[]{:S(2)}) async-start(f32[16,4,384]{2,1,0:T(4,128)} %broadcast_in_dim.11), calls=%async_computation.2 | async-start | bytes 196608 | tf_op jit(solution)/shard_map/all_to_all | solution.py:478
  105.5 0.7 copy.75
  106.2 4.9 %all-to-all-done.2.blocks = f32[16,4,384]{2,1,0:T(4,128)S(1)} async-done(((f32[16,4,384]{2,1,0:T(4,128)}), f32[16,4,384]{2,1,0:T(4,128)S(1)}, u32[]{:S(2)}, u32[]{:S(2)}) %all-to-all-start.2) | async-done | bytes 98336 | tf_op jit(solution)/shard_map/all_to_all | solution.py:478
  111.1 0.6 copy-done.1
  111.7 1.8 %unpack_gradients.1 = (f32[2,9,32,32]{3,2,1,0:T(8,128)}, f32[2,32,32]{2,1,0:T(8,128)}, f32[2,32]{1,0:T(2,128)}, f32[2,32]{1,0:T(2,128)}) custom-call(f32[16,4,384]{2,1,0:T(4,128)} %copy-done.1), custom_call_target="tpu_custom_call" | custom-call | tf_op jit(solution)/shard_map/unpack_gradients/pallas_call | solution.py:455
  (76 shorter events, 3.9 us)
Async XLA Ops:
  1.7 6.4 %copy-start = (bf16[2,9,32,32]{3,2,1,0:T(8,128)(2,1)S(1)}, bf16[2,9,32,32]{3,2,1,0:T(8,128)(2,1)}, u32[]{:S(2)}) copy-start(bf16[2,9,32,32]{3,2,1,0:T(8,128)(2,1)} %param.7) | copy-start | bytes 110596
  1.9 10.0 %collective-permute-start = (bf16[16,64,128]{2,1,0:T(8,128)(2,1)S(1)}, bf16[16,64,128]{2,1,0:T(8,128)(2,1)S(1)}, u32[]{:S(2)}, u32[]{:S(2)}) collective-permute-start(bf16[16,64,128]{2,1,0:T(8,128)(2,1)S(1)} %rev.3), channel_id=1, source_target_pairs={{0,7},{1,6},{2,5},{3,4},{4,3},{5,2},{6,1},{7,0},{8,15},{9,14},{10,... | collective-permute-start | bytes 786440 | tf_op jit(solution)/shard_map/ppermute | solution.py:420
  8.5 0.9 copy-start.8
  8.5 1.0 copy-start.10
  8.5 1.0 copy-start.11
  12.0 11.3 %collective-permute-start.1 = (bf16[18,64,128]{2,1,0:T(8,128)(2,1)S(1)}, bf16[18,64,128]{2,1,0:T(8,128)(2,1)S(1)}, u32[]{:S(2)}, u32[]{:S(2)}) collective-permute-start(bf16[18,64,128]{2,1,0:T(8,128)(2,1)S(1)} %get-tuple-element.44), channel_id=1, source_target_pairs={{0,8},{16,24},{32,40},{48,56},{64,72},{80,88},{96,104},{112,120},{... | collective-permute-start | bytes 884744 | tf_op jit(solution)/shard_map/ppermute | solution.py:399
  21.2 9.8 %collective-permute-start.2 = (bf16[18,64,128]{2,1,0:T(8,128)(2,1)S(1)}, bf16[18,64,128]{2,1,0:T(8,128)(2,1)S(1)}, u32[]{:S(2)}, u32[]{:S(2)}) collective-permute-start(bf16[18,64,128]{2,1,0:T(8,128)(2,1)S(1)} %get-tuple-element.45), channel_id=1, source_target_pairs={{8,16},{24,32},{40,48},{56,64},{72,80},{88,96},{104,112},{120,128}... | collective-permute-start | bytes 884744 | tf_op jit(solution)/shard_map/ppermute | solution.py:398
  34.1 0.8 copy-start.2
  34.1 0.9 copy-start.3
  34.1 0.9 copy-start.4
  34.1 0.9 copy-start.5
  34.1 0.9 copy-start.7
  34.1 1.2 %copy-start.6 = (bf16[4,64,16]{2,1,0:T(8,128)(2,1)S(1)}, bf16[4,64,16]{2,1,0:T(8,128)(2,1)}, u32[]{:S(2)}) copy-start(bf16[4,64,16]{2,1,0:T(8,128)(2,1)} %get-tuple-element.63) | copy-start | bytes 24580
  35.6 6.4 %collective-permute-start.3 = (bf16[12,64,128]{2,1,0:T(8,128)(2,1)S(1)}, bf16[12,64,128]{2,1,0:T(8,128)(2,1)S(1)}, u32[]{:S(2)}, u32[]{:S(2)}) collective-permute-start(bf16[12,64,128]{2,1,0:T(8,128)(2,1)S(1)} %get-tuple-element.53), channel_id=1, source_target_pairs={{0,1},{2,3},{4,5},{6,7},{1,0},{3,2},{5,4},{7,6},{8,9},{10,11},{12,... | collective-permute-start | bytes 589832 | tf_op jit(solution)/shard_map/ppermute | solution.py:399
  37.5 4.5 %collective-permute-start.4 = (bf16[12,64,128]{2,1,0:T(8,128)(2,1)S(1)}, bf16[12,64,128]{2,1,0:T(8,128)(2,1)S(1)}, u32[]{:S(2)}, u32[]{:S(2)}) collective-permute-start(bf16[12,64,128]{2,1,0:T(8,128)(2,1)S(1)} %get-tuple-element.52), channel_id=1, source_target_pairs={{1,2},{3,4},{5,6},{2,1},{4,3},{6,5},{9,10},{11,12},{13,14},{10,9},... | collective-permute-start | bytes 589832 | tf_op jit(solution)/shard_map/ppermute | solution.py:398
  38.3 3.8 %copy-start.9 = (f32[2,64]{1,0:T(2,128)S(1)}, f32[2,64]{1,0:T(2,128)}, u32[]{:S(2)}) copy-start(f32[2,64]{1,0:T(2,128)} %tile.19) | copy-start | bytes 1540
  99.8 11.2 %all-to-all-start.2 = ((f32[16,4,384]{2,1,0:T(4,128)}), f32[16,4,384]{2,1,0:T(4,128)S(1)}, u32[]{:S(2)}, u32[]{:S(2)}) async-start(f32[16,4,384]{2,1,0:T(4,128)} %broadcast_in_dim.11), calls=%async_computation.2 | async-start | bytes 196608 | tf_op jit(solution)/shard_map/all_to_all | solution.py:478
  111.1 0.6 copy-start.1
